TPU v7x, 32 devices: a whole 2x2x4 slice. The times are simulated.
32 devices in a mesh: gx: 4 (over z), gy: 2 (over y), gz: 4 (over x, core).
Axes of the slice: x: 2, y: 2, z: 4, core: 2. Of those that a mesh axis runs over, the one named last changes fastest.
Arguments:
- cell_state: float32 [3, 32, 32, 512], P(None, 'gx', 'gy', 'gz'), may hold values from 0 to 1, as said below
- old_mass: float32 [3, 32, 32, 512], P(None, 'gx', 'gy', 'gz'), may hold values from 0 to 1.5
- pore_volume: float32 [32, 32, 512], P('gx', 'gy', 'gz'), may hold values from 0.5 to 2
- transmissibility: float32 [13, 32, 32, 512], P(None, 'gx', 'gy', 'gz'), may hold values from 0.02 to 1
- active_mask: int32 [32, 32, 512], P('gx', 'gy', 'gz'), may hold values 0 or 1
- pvt_region: int32 [32, 32, 512], P('gx', 'gy', 'gz'), may hold values from 0 to 7
- formation_factor: float32 [3, 8], replicated, may hold values from 0.6 to 1.5
- compressibility: float32 [3, 8], replicated, may hold values from 0.05 to 0.2
- inverse_viscosity: float32 [3, 8], replicated, may hold values from 0.3 to 3
Outputs:
- residual: float32 [3, 32, 32, 512], P(None, 'gx', 'gy', 'gz')
- pressure_update: float32 [32, 32, 512], P('gx', 'gy', 'gz')
Inputs may be any that keep to these rules, and one draw needn't show every extreme that they name: `cell_state`: channel 0 is the pressure; channels 1 and 2 are positive saturations whose sum stays below 1.
All inputs are finite; a program needn't handle non-finite values. No bound on the sum of `active_mask` on one device may be relied on, other than what follows from the above.
Results may differ from a plain program's by a relative error of at most 0.0003.
Values sent between devices are 32-bit elements; how exact they have to be, the bound alone decides.
No kernel may reach another device: no remote copies, remote signals or barrier semaphores. Data moves between devices by JAX's collectives and lax.ppermute only.
A program may use at most 64 MiB of HBM per device.

v0:
```python
import jax
import jax.numpy as jnp
from jax import lax
from jax.sharding import PartitionSpec as P

SWEEPS = 4


neighbour_offsets = [
    (along_x, along_y, along_z)
    for along_x in (-1, 0, 1)
    for along_y in (-1, 0, 1)
    for along_z in (-1, 0, 1)
    if (along_x, along_y, along_z) != (0, 0, 0)
]
upper_offsets = [offset for offset in neighbour_offsets if offset > (0, 0, 0)]
relax_weight = 0.7


def extended(cells, sides, width):
    for axis, dim in sides:
        count = lax.axis_size(axis)
        ends = count - 1
        head = lax.slice_in_dim(cells, 0, width, axis=dim)
        tail = lax.slice_in_dim(cells, cells.shape[dim] - width, cells.shape[dim], axis=dim)
        cells = jnp.concatenate(
            [
                lax.ppermute(tail, axis, [(i, (i + 1) % count) for i in range(ends)]),
                cells,
                lax.ppermute(head, axis, [((i + 1) % count, i) for i in range(ends)]),
            ],
            axis=dim,
        )
    return cells


def window(values_in, offset):
    extent = values_in.shape[-3:]
    return values_in[
        ...,
        1 + offset[0] : extent[0] - 1 + offset[0],
        1 + offset[1] : extent[1] - 1 + offset[1],
        1 + offset[2] : extent[2] - 1 + offset[2],
    ]


def lookup(table_in, region_float):
    looked_up = jnp.zeros((table_in.shape[0],) + region_float.shape, region_float.dtype)
    for level in range(table_in.shape[1]):
        chosen = (region_float == level).astype(region_float.dtype)
        looked_up = looked_up + table_in[:, level][:, None, None, None] * chosen[None]
    return looked_up


def assemble(padded, old_mass, pore_volume, tables):
    formation, compress_table, viscous_inverse = tables
    pressure = padded[0]
    active = padded[3]
    saturation = jnp.stack([padded[1], 1.0 - padded[1] - padded[2], padded[2]])
    compress_rate = lookup(compress_table, padded[4])
    expansion = lookup(formation, padded[4]) * jnp.exp(compress_rate * (pressure[None] - 0.5))
    mobility = lookup(viscous_inverse, padded[4]) * expansion * saturation * saturation
    slope_all = compress_rate * mobility
    centre = (0, 0, 0)
    press_here = window(pressure, centre)
    active_here = window(active, centre)
    mobility_here = window(mobility, centre)
    slope_here = window(slope_all, centre)
    saturation_here = window(saturation, centre)
    expansion_here = window(expansion, centre)
    storage = pore_volume * jnp.sum(window(compress_rate, centre) * saturation_here, axis=0)
    scaling = 1.0 / jnp.where(active_here > 0, storage, 1.0)
    weights = scaling[None] / expansion_here
    flux_total = jnp.zeros_like(saturation_here)
    diagonal = jnp.ones_like(press_here)
    couplings = []
    for offset in neighbour_offsets:
        if offset in upper_offsets:
            link_trans = window(padded[5 + upper_offsets.index(offset)], centre)
        else:
            mirror = (-offset[0], -offset[1], -offset[2])
            link_trans = window(padded[5 + upper_offsets.index(mirror)], offset)
        link_trans = link_trans * active_here * window(active, offset)
        press_drop = press_here - window(pressure, offset)
        mobility_mean = 0.5 * (mobility_here + window(mobility, offset))
        flux_total = flux_total + link_trans * mobility_mean * press_drop
        diagonal = diagonal + link_trans * jnp.sum(
            weights * (0.5 * slope_here * press_drop + mobility_mean), axis=0
        )
        couplings.append(
            link_trans
            * jnp.sum(
                weights * (0.5 * window(slope_all, offset) * press_drop - mobility_mean), axis=0
            )
        )
    residual = active_here * (
        pore_volume * expansion_here * saturation_here - old_mass + flux_total
    )
    pressure_rhs = -jnp.sum(weights * residual, axis=0)
    return (residual, diagonal, jnp.stack(couplings), pressure_rhs)


def relax(padded_update, diagonal, couplings, pressure_rhs):
    centre_update = window(padded_update, (0, 0, 0))
    product = diagonal * centre_update
    for position, offset in enumerate(neighbour_offsets):
        product = product + couplings[position] * window(padded_update, offset)
    return centre_update + relax_weight * (pressure_rhs - product) / diagonal


def body(
    cell_state,
    old_mass,
    pore_volume,
    transmissibility,
    active_mask,
    pvt_region,
    formation_factor,
    compressibility,
    inverse_viscosity,
):
    tables = (formation_factor, compressibility, inverse_viscosity)
    flag_rows = jnp.stack([active_mask.astype(jnp.float32), pvt_region.astype(jnp.float32)])
    stacked = jnp.concatenate([cell_state, flag_rows, transmissibility], axis=0)
    padded = extended(stacked, (("gx", 1), ("gy", 2), ("gz", 3)), 1)
    residual, diagonal, couplings, pressure_rhs = assemble(padded, old_mass, pore_volume, tables)
    update = relax_weight * pressure_rhs / diagonal
    for sweep_index in range(SWEEPS - 1):
        rimmed = extended(update, (("gx", 0), ("gy", 1), ("gz", 2)), 1)
        update = relax(rimmed, diagonal, couplings, pressure_rhs)
    return (residual, update)


def solution(mesh):
    return jax.shard_map(
        body,
        mesh=mesh,
        in_specs=(
            P(None, "gx", "gy", "gz"),
            P(None, "gx", "gy", "gz"),
            P("gx", "gy", "gz"),
            P(None, "gx", "gy", "gz"),
            P("gx", "gy", "gz"),
            P("gx", "gy", "gz"),
            P(),
            P(),
            P(),
        ),
        out_specs=(P(None, "gx", "gy", "gz"), P("gx", "gy", "gz")),
        check_vma=False,
    )
```

profile of v0, /device:TPU:1, one launch (start us, length us, event | category | flops | bytes accessed | tf_op | source)
XLA Modules:
  0.0 141.2 jit_solution(13541402414916819100)
XLA Ops:
  1.6 1.0 pad_maximum_fusion.9
  2.6 4.0 %collective-permute-start = (f32[18,1,16,128]{3,2,1,0:T(8,128)S(1)}, f32[18,1,16,128]{3,2,1,0:T(8,128)S(1)}, u32[]{:S(2)}, u32[]{:S(2)}) collective-permute-start(f32[18,1,16,128]{3,2,1,0:T(8,128)S(1)} %get-tuple-element.296), channel_id=1, source_target_pairs={{0,8},{8,16},{16,24},{1,9},{9,17},{17,25},{2,10},{10,18},{18,26},{... | collective-permute-start | bytes 442376 | tf_op jit(solution)/shard_map/ppermute | solution.py:28
  6.7 1.3 collective-permute-start.1
  8.0 1.2 collective-permute-done
  9.2 3.8 %collective-permute-done.1 = f32[18,1,16,128]{3,2,1,0:T(8,128)S(1)} collective-permute-done((f32[18,1,16,128]{3,2,1,0:T(8,128)S(1)}, f32[18,1,16,128]{3,2,1,0:T(8,128)S(1)}, u32[]{:S(2)}, u32[]{:S(2)}) %collective-permute-start.1) | collective-permute-done | bytes 147488 | tf_op jit(solution)/shard_map/ppermute | solution.py:30
  13.0 1.1 pad_maximum_fusion.21
  14.1 3.1 %collective-permute-start.2 = (f32[18,10,1,128]{3,2,1,0:T(1,128)S(1)}, f32[18,10,1,128]{3,2,1,0:T(1,128)S(1)}, u32[]{:S(2)}, u32[]{:S(2)}) collective-permute-start(f32[18,10,1,128]{3,2,1,0:T(1,128)S(1)} %get-tuple-element.294), channel_id=1, source_target_pairs={{0,4},{1,5},{2,6},{3,7},{8,12},{9,13},{10,14},{11,15},{16,20},{17,... | collective-permute-start | bytes 276488 | tf_op jit(solution)/shard_map/ppermute | solution.py:28
  17.3 1.3 collective-permute-start.3
  18.6 1.0 slice_reduce_fusion.7
  19.7 2.9 %collective-permute-done.3 = f32[18,10,1,128]{3,2,1,0:T(1,128)S(1)} collective-permute-done((f32[18,10,1,128]{3,2,1,0:T(1,128)S(1)}, f32[18,10,1,128]{3,2,1,0:T(1,128)S(1)}, u32[]{:S(2)}, u32[]{:S(2)}) %collective-permute-start.3) | collective-permute-done | bytes 92192 | tf_op jit(solution)/shard_map/ppermute | solution.py:30
  23.6 2.1 %fusion.176 = (f32[18,10,18,1]{3,2,1,0:T(8,128)}, f32[18,10,18,1]{3,2,1,0:T(8,128)S(1)}) fusion(f32[18,10,18,128]{3,2,1,0:T(8,128)S(1)} %pad_maximum_fusion.1), kind=kLoop, calls=%fused_computation.560 | loop fusion | bytes 51840 | tf_op jit(solution)/shard_map/slice | solution.py:25
  25.7 3.4 %copy.24 = f32[18,10,18,1]{2,3,1,0:T(1,128)} copy(f32[18,10,18,1]{3,2,1,0:T(8,128)} %get-tuple-element.272) | data formatting | bytes 25920
  29.1 1.8 %copy.25 = f32[18,10,18,1]{2,3,1,0:T(1,128)} copy(f32[18,10,18,1]{3,2,1,0:T(8,128)S(1)} %get-tuple-element.273) | data formatting | bytes 25920
  30.9 5.1 %collective-permute-start.5 = (f32[18,10,18,1]{2,3,1,0:T(1,128)}, f32[18,10,18,1]{2,3,1,0:T(1,128)}, u32[]{:S(2)}, u32[]{:S(2)}) collective-permute-start(f32[18,10,18,1]{2,3,1,0:T(1,128)} %copy.25), channel_id=1, source_target_pairs={{1,0},{2,1},{3,2},{5,4},{6,5},{7,6},{9,8},{10,9},{11,10},{13,12},{... | collective-permute-start | bytes 38888 | tf_op jit(solution)/shard_map/ppermute | solution.py:30
  36.0 3.0 %collective-permute-start.4 = (f32[18,10,18,1]{2,3,1,0:T(1,128)}, f32[18,10,18,1]{2,3,1,0:T(1,128)}, u32[]{:S(2)}, u32[]{:S(2)}) collective-permute-start(f32[18,10,18,1]{2,3,1,0:T(1,128)} %copy.24), channel_id=1, source_target_pairs={{0,1},{1,2},{2,3},{4,5},{5,6},{6,7},{8,9},{9,10},{10,11},{12,13},{... | collective-permute-start | bytes 38888 | tf_op jit(solution)/shard_map/ppermute | solution.py:28
  39.9 1.0 collective-permute-done.4
  40.9 2.1 %copy.22 = f32[18,10,18,1]{3,2,1,0:T(8,128)S(1)} copy(f32[18,10,18,1]{2,3,1,0:T(1,128)} %collective-permute-done.4) | data formatting | bytes 25920 | tf_op jit(solution)/shard_map/ppermute | solution.py:28
  43.0 3.5 %copy.23 = f32[18,10,18,1]{3,2,1,0:T(8,128)} copy(f32[18,10,18,1]{2,3,1,0:T(1,128)} %collective-permute-done.5) | data formatting | bytes 25920 | tf_op jit(solution)/shard_map/ppermute | solution.py:30
  46.5 7.7 %pad_maximum_fusion = f32[18,10,18,130]{3,2,1,0:T(8,128)S(1)} fusion(f32[18,10,18,1]{3,2,1,0:T(8,128)} %copy.23, f32[18,10,1,128]{3,2,1,0:T(1,128)} %copy-done.4, f32[18,1,16,128]{3,2,1,0:T(8,128)} %copy-done.2, f32[13,8,16,128]{3,2,1,0:T(8,128)S(1)} %copy-done, f32[1,8,16,128]{3,2,1,0:T(8,128)S(1)} %get-tuple-element.438, ...), kind=kLoop, calls=%fused_computation | loop fusion | flops 3790800 | bytes 3369600 | tf_op jit(solution)/shard_map/concatenate | solution.py:26
  56.0 1.5 %fusion.175 = (f32[3,10,18,130]{3,2,1,0:T(8,128)S(1)}, f32[3,10,18,130]{3,2,1,0:T(8,128)S(1)}, f32[3,10,18,130]{3,2,1,0:T(8,128)S(1)}, f32[3,10,18,130]{3,2,1,0:T(8,128)S(1)}) fusion(f32[1,10,18,130]{3,2,1,0:T(8,128)S(1)} %get-tuple-element.261, f32[1,10,18,130]{3,2,1,0:T(8,128)S(1)} %get-tuple-element.247, f32[1,10,18,130]{3,2,1,0:T(8,128)S(1)} %get-tuple-element.262, ...), kind=kLoop, calls=%fused_computation.559 | loop fusion | flops 3720600 | bytes 2246688 | tf_op jit(solution)/shard_map/mul | solution.py:63
  62.4 2.3 %fusion.77 = (f32[8,16,128]{2,1,0:T(8,128)S(1)}, f32[8,16,128]{2,1,0:T(8,128)S(1)}, f32[8,16,128]{2,1,0:T(8,128)S(1)}, f32[8,16,128]{2,1,0:T(8,128)S(1)}, f32[8,...) fusion(f32[3,8,16,128]{3,2,1,0:T(8,128)S(1)} %get-tuple-element.136, f32[3,10,18,130]{3,2,1,0:T(8,128)S(1)} %get-tuple-element.190, ...), kind=kLoop, calls=%fused_computation.140 | loop fusion | flops 6209536 | bytes 10878976 | tf_op jit(solution)/shard_map/reduce_sum | solution.py:92
  64.9 3.2 %collective-permute-start.6 = (f32[1,16,128]{2,1,0:T(8,128)S(1)}, f32[1,16,128]{2,1,0:T(8,128)S(1)}, u32[]{:S(2)}, u32[]{:S(2)}) collective-permute-start(f32[1,16,128]{2,1,0:T(8,128)S(1)} %get-tuple-element.436), channel_id=1, source_target_pairs={{0,8},{8,16},{16,24},{1,9},{9,17},{17,25},{2,10},{10,18},{18,26},{... | collective-permute-start | bytes 24584 | tf_op jit(solution)/shard_map/ppermute | solution.py:28
  68.1 1.3 collective-permute-start.7
  69.5 3.1 %collective-permute-done.7 = f32[1,16,128]{2,1,0:T(8,128)S(1)} collective-permute-done((f32[1,16,128]{2,1,0:T(8,128)S(1)}, f32[1,16,128]{2,1,0:T(8,128)S(1)}, u32[]{:S(2)}, u32[]{:S(2)}) %collective-permute-start.7) | collective-permute-done | bytes 8224 | tf_op jit(solution)/shard_map/ppermute | solution.py:30
  72.6 1.3 collective-permute-start.8
  73.9 1.3 collective-permute-start.9
  75.2 3.1 %collective-permute-done.9 = f32[10,1,128]{2,1,0:T(1,128)S(1)} collective-permute-done((f32[10,1,128]{2,1,0:T(1,128)S(1)}, f32[10,1,128]{2,1,0:T(1,128)S(1)}, u32[]{:S(2)}, u32[]{:S(2)}) %collective-permute-start.9) | collective-permute-done | bytes 5152 | tf_op jit(solution)/shard_map/ppermute | solution.py:30
  78.4 7.1 %collective-permute-start.10 = (f32[10,18,1]{2,1,0:T(8,128)S(1)}, f32[10,18,1]{2,1,0:T(8,128)S(1)}, u32[]{:S(2)}, u32[]{:S(2)}) collective-permute-start(f32[10,18,1]{2,1,0:T(8,128)S(1)} %get-tuple-element.412), channel_id=1, source_target_pairs={{0,1},{1,2},{2,3},{4,5},{5,6},{6,7},{8,9},{9,10},{10,11},{12,13},{... | collective-permute-start | bytes 2168 | tf_op jit(solution)/shard_map/ppermute | solution.py:28
  85.5 2.1 %collective-permute-start.11 = (f32[10,18,1]{2,1,0:T(8,128)S(1)}, f32[10,18,1]{2,1,0:T(8,128)S(1)}, u32[]{:S(2)}, u32[]{:S(2)}) collective-permute-start(f32[10,18,1]{2,1,0:T(8,128)S(1)} %get-tuple-element.413), channel_id=1, source_target_pairs={{1,0},{2,1},{3,2},{5,4},{6,5},{7,6},{9,8},{10,9},{11,10},{13,12},{... | collective-permute-start | bytes 2168 | tf_op jit(solution)/shard_map/ppermute | solution.py:30
  87.7 4.0 %collective-permute-done.11 = f32[10,18,1]{2,1,0:T(8,128)S(1)} collective-permute-done((f32[10,18,1]{2,1,0:T(8,128)S(1)}, f32[10,18,1]{2,1,0:T(8,128)S(1)}, u32[]{:S(2)}, u32[]{:S(2)}) %collective-permute-start.11) | collective-permute-done | bytes 752 | tf_op jit(solution)/shard_map/ppermute | solution.py:30
  92.4 3.2 %collective-permute-start.12 = (f32[1,16,128]{2,1,0:T(8,128)S(1)}, f32[1,16,128]{2,1,0:T(8,128)S(1)}, u32[]{:S(2)}, u32[]{:S(2)}) collective-permute-start(f32[1,16,128]{2,1,0:T(8,128)S(1)} %get-tuple-element.434), channel_id=1, source_target_pairs={{0,8},{8,16},{16,24},{1,9},{9,17},{17,25},{2,10},{10,18},{18,26},{... | collective-permute-start | bytes 24584 | tf_op jit(solution)/shard_map/ppermute | solution.py:28
  95.6 1.3 collective-permute-start.13
  97.0 3.1 %collective-permute-done.13 = f32[1,16,128]{2,1,0:T(8,128)S(1)} collective-permute-done((f32[1,16,128]{2,1,0:T(8,128)S(1)}, f32[1,16,128]{2,1,0:T(8,128)S(1)}, u32[]{:S(2)}, u32[]{:S(2)}) %collective-permute-start.13) | collective-permute-done | bytes 8224 | tf_op jit(solution)/shard_map/ppermute | solution.py:30
  100.1 1.4 collective-permute-start.14
  101.4 1.3 collective-permute-start.15
  102.7 3.1 %collective-permute-done.15 = f32[10,1,128]{2,1,0:T(1,128)S(1)} collective-permute-done((f32[10,1,128]{2,1,0:T(1,128)S(1)}, f32[10,1,128]{2,1,0:T(1,128)S(1)}, u32[]{:S(2)}, u32[]{:S(2)}) %collective-permute-start.15) | collective-permute-done | bytes 5152 | tf_op jit(solution)/shard_map/ppermute | solution.py:30
  105.9 4.7 %collective-permute-start.16 = (f32[10,18,1]{2,1,0:T(8,128)S(1)}, f32[10,18,1]{2,1,0:T(8,128)S(1)}, u32[]{:S(2)}, u32[]{:S(2)}) collective-permute-start(f32[10,18,1]{2,1,0:T(8,128)S(1)} %get-tuple-element.410), channel_id=1, source_target_pairs={{0,1},{1,2},{2,3},{4,5},{5,6},{6,7},{8,9},{9,10},{10,11},{12,13},{... | collective-permute-start | bytes 2168 | tf_op jit(solution)/shard_map/ppermute | solution.py:28
  110.6 1.9 %collective-permute-start.17 = (f32[10,18,1]{2,1,0:T(8,128)S(1)}, f32[10,18,1]{2,1,0:T(8,128)S(1)}, u32[]{:S(2)}, u32[]{:S(2)}) collective-permute-start(f32[10,18,1]{2,1,0:T(8,128)S(1)} %get-tuple-element.411), channel_id=1, source_target_pairs={{1,0},{2,1},{3,2},{5,4},{6,5},{7,6},{9,8},{10,9},{11,10},{13,12},{... | collective-permute-start | bytes 2168 | tf_op jit(solution)/shard_map/ppermute | solution.py:30
  112.5 4.2 %collective-permute-done.17 = f32[10,18,1]{2,1,0:T(8,128)S(1)} collective-permute-done((f32[10,18,1]{2,1,0:T(8,128)S(1)}, f32[10,18,1]{2,1,0:T(8,128)S(1)}, u32[]{:S(2)}, u32[]{:S(2)}) %collective-permute-start.17) | collective-permute-done | bytes 752 | tf_op jit(solution)/shard_map/ppermute | solution.py:30
  117.3 1.6 %collective-permute-start.18 = (f32[1,16,128]{2,1,0:T(8,128)S(1)}, f32[1,16,128]{2,1,0:T(8,128)S(1)}, u32[]{:S(2)}, u32[]{:S(2)}) collective-permute-start(f32[1,16,128]{2,1,0:T(8,128)S(1)} %get-tuple-element.432), channel_id=1, source_target_pairs={{0,8},{8,16},{16,24},{1,9},{9,17},{17,25},{2,10},{10,18},{18,26},{... | collective-permute-start | bytes 24584 | tf_op jit(solution)/shard_map/ppermute | solution.py:28
  118.9 1.3 collective-permute-start.19
  120.2 3.1 %collective-permute-done.19 = f32[1,16,128]{2,1,0:T(8,128)S(1)} collective-permute-done((f32[1,16,128]{2,1,0:T(8,128)S(1)}, f32[1,16,128]{2,1,0:T(8,128)S(1)}, u32[]{:S(2)}, u32[]{:S(2)}) %collective-permute-start.19) | collective-permute-done | bytes 8224 | tf_op jit(solution)/shard_map/ppermute | solution.py:30
  123.3 1.4 collective-permute-start.20
  124.7 1.3 collective-permute-start.21
  126.0 3.1 %collective-permute-done.21 = f32[10,1,128]{2,1,0:T(1,128)S(1)} collective-permute-done((f32[10,1,128]{2,1,0:T(1,128)S(1)}, f32[10,1,128]{2,1,0:T(1,128)S(1)}, u32[]{:S(2)}, u32[]{:S(2)}) %collective-permute-start.21) | collective-permute-done | bytes 5152 | tf_op jit(solution)/shard_map/ppermute | solution.py:30
  129.2 4.7 %collective-permute-start.22 = (f32[10,18,1]{2,1,0:T(8,128)S(1)}, f32[10,18,1]{2,1,0:T(8,128)S(1)}, u32[]{:S(2)}, u32[]{:S(2)}) collective-permute-start(f32[10,18,1]{2,1,0:T(8,128)S(1)} %get-tuple-element.408), channel_id=1, source_target_pairs={{0,1},{1,2},{2,3},{4,5},{5,6},{6,7},{8,9},{9,10},{10,11},{12,13},{... | collective-permute-start | bytes 2168 | tf_op jit(solution)/shard_map/ppermute | solution.py:28
  133.9 1.9 %collective-permute-start.23 = (f32[10,18,1]{2,1,0:T(8,128)S(1)}, f32[10,18,1]{2,1,0:T(8,128)S(1)}, u32[]{:S(2)}, u32[]{:S(2)}) collective-permute-start(f32[10,18,1]{2,1,0:T(8,128)S(1)} %get-tuple-element.409), channel_id=1, source_target_pairs={{1,0},{2,1},{3,2},{5,4},{6,5},{7,6},{9,8},{10,9},{11,10},{13,12},{... | collective-permute-start | bytes 2168 | tf_op jit(solution)/shard_map/ppermute | solution.py:30
  135.8 4.2 %collective-permute-done.23 = f32[10,18,1]{2,1,0:T(8,128)S(1)} collective-permute-done((f32[10,18,1]{2,1,0:T(8,128)S(1)}, f32[10,18,1]{2,1,0:T(8,128)S(1)}, u32[]{:S(2)}, u32[]{:S(2)}) %collective-permute-start.23) | collective-permute-done | bytes 752 | tf_op jit(solution)/shard_map/ppermute | solution.py:30
  (118 shorter events, 12.2 us)
Async XLA Ops:
  0.6 12.4 %copy-start = (f32[13,8,16,128]{3,2,1,0:T(8,128)S(1)}, f32[13,8,16,128]{3,2,1,0:T(8,128)}, u32[]{:S(2)}) copy-start(f32[13,8,16,128]{3,2,1,0:T(8,128)} %param.12) | copy-start | bytes 2555908
  0.6 22.6 %copy-start.1 = (f32[3,8,16,128]{3,2,1,0:T(8,128)S(1)}, f32[3,8,16,128]{3,2,1,0:T(8,128)}, u32[]{:S(2)}) copy-start(f32[3,8,16,128]{3,2,1,0:T(8,128)} %param.9) | copy-start | bytes 589828
  0.7 17.9 %copy-start.8 = (f32[3,8]{1,0:T(4,128)S(1)}, f32[3,8]{1,0:T(4,128)}, u32[]{:S(2)}) copy-start(f32[3,8]{1,0:T(4,128)} %param.17) | copy-start | bytes 292
  0.7 17.9 %copy-start.9 = (f32[3,8]{1,0:T(4,128)S(1)}, f32[3,8]{1,0:T(4,128)}, u32[]{:S(2)}) copy-start(f32[3,8]{1,0:T(4,128)} %param.16) | copy-start | bytes 292
  2.6 6.5 %collective-permute-start = (f32[18,1,16,128]{3,2,1,0:T(8,128)S(1)}, f32[18,1,16,128]{3,2,1,0:T(8,128)S(1)}, u32[]{:S(2)}, u32[]{:S(2)}) collective-permute-start(f32[18,1,16,128]{3,2,1,0:T(8,128)S(1)} %get-tuple-element.296), channel_id=1, source_target_pairs={{0,8},{8,16},{16,24},{1,9},{9,17},{17,25},{2,10},{10,18},{18,26},{... | collective-permute-start | bytes 442376 | tf_op jit(solution)/shard_map/ppermute | solution.py:28
  6.7 6.3 %collective-permute-start.1 = (f32[18,1,16,128]{3,2,1,0:T(8,128)S(1)}, f32[18,1,16,128]{3,2,1,0:T(8,128)S(1)}, u32[]{:S(2)}, u32[]{:S(2)}) collective-permute-start(f32[18,1,16,128]{3,2,1,0:T(8,128)S(1)} %get-tuple-element.297), channel_id=1, source_target_pairs={{8,0},{16,8},{24,16},{9,1},{17,9},{25,17},{10,2},{18,10},{26,18},{... | collective-permute-start | bytes 442376 | tf_op jit(solution)/shard_map/ppermute | solution.py:30
  13.0 9.6 %copy-start.2 = (f32[18,1,16,128]{3,2,1,0:T(8,128)}, f32[18,1,16,128]{3,2,1,0:T(8,128)S(1)}, u32[]{:S(2)}) copy-start(f32[18,1,16,128]{3,2,1,0:T(8,128)S(1)} %collective-permute-done.1) | copy-start | bytes 442372
  14.1 5.5 %collective-permute-start.2 = (f32[18,10,1,128]{3,2,1,0:T(1,128)S(1)}, f32[18,10,1,128]{3,2,1,0:T(1,128)S(1)}, u32[]{:S(2)}, u32[]{:S(2)}) collective-permute-start(f32[18,10,1,128]{3,2,1,0:T(1,128)S(1)} %get-tuple-element.294), channel_id=1, source_target_pairs={{0,4},{1,5},{2,6},{3,7},{8,12},{9,13},{10,14},{11,15},{16,20},{17,... | collective-permute-start | bytes 276488 | tf_op jit(solution)/shard_map/ppermute | solution.py:28
  17.3 5.3 %collective-permute-start.3 = (f32[18,10,1,128]{3,2,1,0:T(1,128)S(1)}, f32[18,10,1,128]{3,2,1,0:T(1,128)S(1)}, u32[]{:S(2)}, u32[]{:S(2)}) collective-permute-start(f32[18,10,1,128]{3,2,1,0:T(1,128)S(1)} %get-tuple-element.295), channel_id=1, source_target_pairs={{4,0},{5,1},{6,2},{7,3},{12,8},{13,9},{14,10},{15,11},{20,16},{21,... | collective-permute-start | bytes 276488 | tf_op jit(solution)/shard_map/ppermute | solution.py:30
  19.7 2.9 %copy-start.3 = (f32[18,10,1,128]{3,2,1,0:T(1,128)}, f32[18,10,1,128]{3,2,1,0:T(1,128)S(1)}, u32[]{:S(2)}) copy-start(f32[18,10,1,128]{3,2,1,0:T(1,128)S(1)} %collective-permute-done.2) | copy-start | bytes 276484
  25.7 13.4 %copy-start.7 = (f32[3,8]{1,0:T(4,128)S(1)}, f32[3,8]{1,0:T(4,128)}, u32[]{:S(2)}) copy-start(f32[3,8]{1,0:T(4,128)} %param.15) | copy-start | bytes 292
  30.9 12.1 %collective-permute-start.5 = (f32[18,10,18,1]{2,3,1,0:T(1,128)}, f32[18,10,18,1]{2,3,1,0:T(1,128)}, u32[]{:S(2)}, u32[]{:S(2)}) collective-permute-start(f32[18,10,18,1]{2,3,1,0:T(1,128)} %copy.25), channel_id=1, source_target_pairs={{1,0},{2,1},{3,2},{5,4},{6,5},{7,6},{9,8},{10,9},{11,10},{13,12},{... | collective-permute-start | bytes 38888 | tf_op jit(solution)/shard_map/ppermute | solution.py:30
  36.0 4.9 %collective-permute-start.4 = (f32[18,10,18,1]{2,3,1,0:T(1,128)}, f32[18,10,18,1]{2,3,1,0:T(1,128)}, u32[]{:S(2)}, u32[]{:S(2)}) collective-permute-start(f32[18,10,18,1]{2,3,1,0:T(1,128)} %copy.24), channel_id=1, source_target_pairs={{0,1},{1,2},{2,3},{4,5},{5,6},{6,7},{8,9},{9,10},{10,11},{12,13},{... | collective-permute-start | bytes 38888 | tf_op jit(solution)/shard_map/ppermute | solution.py:28
  55.1 0.7 copy-start.10
  55.1 0.7 copy-start.11
  55.1 0.7 copy-start.12
  55.1 0.7 copy-start.13
  55.1 0.7 copy-start.14
  55.2 0.7 copy-start.15
  55.2 0.7 copy-start.16
  55.2 0.7 copy-start.17
  55.2 0.7 copy-start.18
  55.2 0.7 copy-start.19
  55.2 0.7 copy-start.20
  55.2 0.7 copy-start.21
  55.2 0.7 copy-start.22
  55.2 0.7 copy-start.23
  55.2 0.7 copy-start.24
  57.9 0.8 copy-start.5
  61.5 0.9 copy-start.6
  64.9 4.5 %collective-permute-start.6 = (f32[1,16,128]{2,1,0:T(8,128)S(1)}, f32[1,16,128]{2,1,0:T(8,128)S(1)}, u32[]{:S(2)}, u32[]{:S(2)}) collective-permute-start(f32[1,16,128]{2,1,0:T(8,128)S(1)} %get-tuple-element.436), channel_id=1, source_target_pairs={{0,8},{8,16},{16,24},{1,9},{9,17},{17,25},{2,10},{10,18},{18,26},{... | collective-permute-start | bytes 24584 | tf_op jit(solution)/shard_map/ppermute | solution.py:28
  68.1 4.5 %collective-permute-start.7 = (f32[1,16,128]{2,1,0:T(8,128)S(1)}, f32[1,16,128]{2,1,0:T(8,128)S(1)}, u32[]{:S(2)}, u32[]{:S(2)}) collective-permute-start(f32[1,16,128]{2,1,0:T(8,128)S(1)} %get-tuple-element.437), channel_id=1, source_target_pairs={{8,0},{16,8},{24,16},{9,1},{17,9},{25,17},{10,2},{18,10},{26,18},{... | collective-permute-start | bytes 24584 | tf_op jit(solution)/shard_map/ppermute | solution.py:30
  72.6 2.6 %collective-permute-start.8 = (f32[10,1,128]{2,1,0:T(1,128)S(1)}, f32[10,1,128]{2,1,0:T(1,128)S(1)}, u32[]{:S(2)}, u32[]{:S(2)}) collective-permute-start(f32[10,1,128]{2,1,0:T(1,128)S(1)} %get-tuple-element.430), channel_id=1, source_target_pairs={{0,4},{1,5},{2,6},{3,7},{8,12},{9,13},{10,14},{11,15},{16,20},{17,... | collective-permute-start | bytes 15368 | tf_op jit(solution)/shard_map/ppermute | solution.py:28
  73.9 4.4 %collective-permute-start.9 = (f32[10,1,128]{2,1,0:T(1,128)S(1)}, f32[10,1,128]{2,1,0:T(1,128)S(1)}, u32[]{:S(2)}, u32[]{:S(2)}) collective-permute-start(f32[10,1,128]{2,1,0:T(1,128)S(1)} %get-tuple-element.431), channel_id=1, source_target_pairs={{4,0},{5,1},{6,2},{7,3},{12,8},{13,9},{14,10},{15,11},{20,16},{21,... | collective-permute-start | bytes 15368 | tf_op jit(solution)/shard_map/ppermute | solution.py:30
  78.4 9.3 %collective-permute-start.10 = (f32[10,18,1]{2,1,0:T(8,128)S(1)}, f32[10,18,1]{2,1,0:T(8,128)S(1)}, u32[]{:S(2)}, u32[]{:S(2)}) collective-permute-start(f32[10,18,1]{2,1,0:T(8,128)S(1)} %get-tuple-element.412), channel_id=1, source_target_pairs={{0,1},{1,2},{2,3},{4,5},{5,6},{6,7},{8,9},{9,10},{10,11},{12,13},{... | collective-permute-start | bytes 2168 | tf_op jit(solution)/shard_map/ppermute | solution.py:28
  85.5 6.2 %collective-permute-start.11 = (f32[10,18,1]{2,1,0:T(8,128)S(1)}, f32[10,18,1]{2,1,0:T(8,128)S(1)}, u32[]{:S(2)}, u32[]{:S(2)}) collective-permute-start(f32[10,18,1]{2,1,0:T(8,128)S(1)} %get-tuple-element.413), channel_id=1, source_target_pairs={{1,0},{2,1},{3,2},{5,4},{6,5},{7,6},{9,8},{10,9},{11,10},{13,12},{... | collective-permute-start | bytes 2168 | tf_op jit(solution)/shard_map/ppermute | solution.py:30
  92.4 4.5 %collective-permute-start.12 = (f32[1,16,128]{2,1,0:T(8,128)S(1)}, f32[1,16,128]{2,1,0:T(8,128)S(1)}, u32[]{:S(2)}, u32[]{:S(2)}) collective-permute-start(f32[1,16,128]{2,1,0:T(8,128)S(1)} %get-tuple-element.434), channel_id=1, source_target_pairs={{0,8},{8,16},{16,24},{1,9},{9,17},{17,25},{2,10},{10,18},{18,26},{... | collective-permute-start | bytes 24584 | tf_op jit(solution)/shard_map/ppermute | solution.py:28
  95.6 4.4 %collective-permute-start.13 = (f32[1,16,128]{2,1,0:T(8,128)S(1)}, f32[1,16,128]{2,1,0:T(8,128)S(1)}, u32[]{:S(2)}, u32[]{:S(2)}) collective-permute-start(f32[1,16,128]{2,1,0:T(8,128)S(1)} %get-tuple-element.435), channel_id=1, source_target_pairs={{8,0},{16,8},{24,16},{9,1},{17,9},{25,17},{10,2},{18,10},{26,18},{... | collective-permute-start | bytes 24584 | tf_op jit(solution)/shard_map/ppermute | solution.py:30
  100.1 2.7 %collective-permute-start.14 = (f32[10,1,128]{2,1,0:T(1,128)S(1)}, f32[10,1,128]{2,1,0:T(1,128)S(1)}, u32[]{:S(2)}, u32[]{:S(2)}) collective-permute-start(f32[10,1,128]{2,1,0:T(1,128)S(1)} %get-tuple-element.426), channel_id=1, source_target_pairs={{0,4},{1,5},{2,6},{3,7},{8,12},{9,13},{10,14},{11,15},{16,20},{17,... | collective-permute-start | bytes 15368 | tf_op jit(solution)/shard_map/ppermute | solution.py:28
  101.4 4.4 %collective-permute-start.15 = (f32[10,1,128]{2,1,0:T(1,128)S(1)}, f32[10,1,128]{2,1,0:T(1,128)S(1)}, u32[]{:S(2)}, u32[]{:S(2)}) collective-permute-start(f32[10,1,128]{2,1,0:T(1,128)S(1)} %get-tuple-element.427), channel_id=1, source_target_pairs={{4,0},{5,1},{6,2},{7,3},{12,8},{13,9},{14,10},{15,11},{20,16},{21,... | collective-permute-start | bytes 15368 | tf_op jit(solution)/shard_map/ppermute | solution.py:30
  105.9 6.6 %collective-permute-start.16 = (f32[10,18,1]{2,1,0:T(8,128)S(1)}, f32[10,18,1]{2,1,0:T(8,128)S(1)}, u32[]{:S(2)}, u32[]{:S(2)}) collective-permute-start(f32[10,18,1]{2,1,0:T(8,128)S(1)} %get-tuple-element.410), channel_id=1, source_target_pairs={{0,1},{1,2},{2,3},{4,5},{5,6},{6,7},{8,9},{9,10},{10,11},{12,13},{... | collective-permute-start | bytes 2168 | tf_op jit(solution)/shard_map/ppermute | solution.py:28
  110.6 6.2 %collective-permute-start.17 = (f32[10,18,1]{2,1,0:T(8,128)S(1)}, f32[10,18,1]{2,1,0:T(8,128)S(1)}, u32[]{:S(2)}, u32[]{:S(2)}) collective-permute-start(f32[10,18,1]{2,1,0:T(8,128)S(1)} %get-tuple-element.411), channel_id=1, source_target_pairs={{1,0},{2,1},{3,2},{5,4},{6,5},{7,6},{9,8},{10,9},{11,10},{13,12},{... | collective-permute-start | bytes 2168 | tf_op jit(solution)/shard_map/ppermute | solution.py:30
  117.3 3.0 %collective-permute-start.18 = (f32[1,16,128]{2,1,0:T(8,128)S(1)}, f32[1,16,128]{2,1,0:T(8,128)S(1)}, u32[]{:S(2)}, u32[]{:S(2)}) collective-permute-start(f32[1,16,128]{2,1,0:T(8,128)S(1)} %get-tuple-element.432), channel_id=1, source_target_pairs={{0,8},{8,16},{16,24},{1,9},{9,17},{17,25},{2,10},{10,18},{18,26},{... | collective-permute-start | bytes 24584 | tf_op jit(solution)/shard_map/ppermute | solution.py:28
  118.9 4.4 %collective-permute-start.19 = (f32[1,16,128]{2,1,0:T(8,128)S(1)}, f32[1,16,128]{2,1,0:T(8,128)S(1)}, u32[]{:S(2)}, u32[]{:S(2)}) collective-permute-start(f32[1,16,128]{2,1,0:T(8,128)S(1)} %get-tuple-element.433), channel_id=1, source_target_pairs={{8,0},{16,8},{24,16},{9,1},{17,9},{25,17},{10,2},{18,10},{26,18},{... | collective-permute-start | bytes 24584 | tf_op jit(solution)/shard_map/ppermute | solution.py:30
  123.3 2.7 %collective-permute-start.20 = (f32[10,1,128]{2,1,0:T(1,128)S(1)}, f32[10,1,128]{2,1,0:T(1,128)S(1)}, u32[]{:S(2)}, u32[]{:S(2)}) collective-permute-start(f32[10,1,128]{2,1,0:T(1,128)S(1)} %get-tuple-element.422), channel_id=1, source_target_pairs={{0,4},{1,5},{2,6},{3,7},{8,12},{9,13},{10,14},{11,15},{16,20},{17,... | collective-permute-start | bytes 15368 | tf_op jit(solution)/shard_map/ppermute | solution.py:28
  124.7 4.4 %collective-permute-start.21 = (f32[10,1,128]{2,1,0:T(1,128)S(1)}, f32[10,1,128]{2,1,0:T(1,128)S(1)}, u32[]{:S(2)}, u32[]{:S(2)}) collective-permute-start(f32[10,1,128]{2,1,0:T(1,128)S(1)} %get-tuple-element.423), channel_id=1, source_target_pairs={{4,0},{5,1},{6,2},{7,3},{12,8},{13,9},{14,10},{15,11},{20,16},{21,... | collective-permute-start | bytes 15368 | tf_op jit(solution)/shard_map/ppermute | solution.py:30
  129.2 6.6 %collective-permute-start.22 = (f32[10,18,1]{2,1,0:T(8,128)S(1)}, f32[10,18,1]{2,1,0:T(8,128)S(1)}, u32[]{:S(2)}, u32[]{:S(2)}) collective-permute-start(f32[10,18,1]{2,1,0:T(8,128)S(1)} %get-tuple-element.408), channel_id=1, source_target_pairs={{0,1},{1,2},{2,3},{4,5},{5,6},{6,7},{8,9},{9,10},{10,11},{12,13},{... | collective-permute-start | bytes 2168 | tf_op jit(solution)/shard_map/ppermute | solution.py:28
  133.9 6.2 %collective-permute-start.23 = (f32[10,18,1]{2,1,0:T(8,128)S(1)}, f32[10,18,1]{2,1,0:T(8,128)S(1)}, u32[]{:S(2)}, u32[]{:S(2)}) collective-permute-start(f32[10,18,1]{2,1,0:T(8,128)S(1)} %get-tuple-element.409), channel_id=1, source_target_pairs={{1,0},{2,1},{3,2},{5,4},{6,5},{7,6},{9,8},{10,9},{11,10},{13,12},{... | collective-permute-start | bytes 2168 | tf_op jit(solution)/shard_map/ppermute | solution.py:30
  (7 other events, 4.8 us)
where the time goes:
time: 142 us; the launch traced here: 141 us
  starting transfers between devices  60.1 us (42%)
  waiting for transfers between devices  39.9 us (28%)
  other arithmetic  23.3 us (16%)
  local copies, waits for them, and re-layouts  16.3 us (11%)
  between operations  1.61 us (1%)
    ppermute x12, starting transfers between devices, extended(): lax.ppermute(tail, axis, [(i, (i + 1) % count) for i in range(ends)])  38.6 us
    ppermute x12, waiting for transfers between devices, extended(): lax.ppermute(head, axis, [((i + 1) % count, i) for i in range(ends)])  37.7 us
    ppermute x12, starting transfers between devices, extended(): lax.ppermute(head, axis, [((i + 1) % count, i) for i in range(ends)])  21.5 us
    concatenate x11, other arithmetic, extended(): jnp.concatenate([lax.ppermute(tail, axis, [(i, (i + 1) % count) for i in...  8.74 us
    unnamed x64, local copies, waits for them, and re-layouts  6.45 us
    reduce_sum x8, other arithmetic, assemble(): jnp.sum(weights * (0.5 * window(slope_all, offset) * press_drop - mobilit...  5.3 us
    ppermute x1, local copies, waits for them, and re-layouts, extended(): lax.ppermute(head, axis, [((i + 1) % count, i) for i in range(ends)])  3.45 us
  transfers between devices with their start and end apart: 24, of which 13 were waited for; matrix products, arithmetic and copies ran while one was open for 3% of the time, Pallas kernels for 0%

commit v1 on v0

v1 whole, which is shorter than its diff:
```python
import functools

import jax
import jax.numpy as jnp
from jax import lax
from jax.experimental import pallas as pl
from jax.experimental.pallas import tpu as pltpu
from jax.sharding import PartitionSpec as P

SWEEPS = 4
W = SWEEPS
relax_weight = 0.7

neighbour_offsets = [
    (along_x, along_y, along_z)
    for along_x in (-1, 0, 1)
    for along_y in (-1, 0, 1)
    for along_z in (-1, 0, 1)
    if (along_x, along_y, along_z) != (0, 0, 0)
]
upper_offsets = [offset for offset in neighbour_offsets if offset > (0, 0, 0)]
UP = len(upper_offsets)
FLAT = sum(1 for offset in upper_offsets if offset[0] == 0)
STEP = UP - FLAT

FAR = 5 + STEP
CHANNELS = FAR + FLAT + 4
NEAR = W - 1
XMAIN = CHANNELS * NEAR + FAR
XMSG = XMAIN + 2 * W
VMEM = pl.BlockSpec(memory_space=pltpu.VMEM)
ANY = pl.BlockSpec(memory_space=pl.ANY)
f32 = jnp.float32


def t_channel(k):
    return FAR + k if k < FLAT else 5 + k - FLAT


def channel_of(local, c, planes):
    state, mass, pore, trans, active, region = local
    if c < 3:
        return state[c, planes]
    if c == 3:
        return active[planes].astype(f32)
    if c == 4:
        return region[planes].astype(f32)
    if c < FAR:
        return trans[FLAT + c - 5, planes]
    if c < FAR + FLAT:
        return trans[c - FAR, planes]
    if c < CHANNELS - 1:
        return mass[c - FAR - FLAT, planes]
    return pore[planes]


def pick(parity, even, odd):
    shape = (even if odd is None else odd).shape
    if even is None:
        even = jnp.zeros(shape, f32)
    if odd is None:
        odd = jnp.zeros(shape, f32)
    return jnp.where(jnp.full(shape, parity, jnp.int32) == 0, even, odd)


def parity_of(axis):
    return lax.rem(lax.axis_index(axis), 2)


def swaps(axis, first, second):
    count = lax.axis_size(axis)
    got = []
    for start, message in ((0, first), (1, second)):
        pairs = [(i, i + 1) for i in range(start, count - 1, 2)]
        if not pairs:
            got.append(None)
            continue
        got.append(lax.ppermute(message, axis, pairs + [(b, a) for a, b in pairs]))
    return got


def lanes_of(shape):
    return lax.broadcasted_iota(jnp.int32, shape, len(shape) - 1)


def pack_z(axis, *refs):
    local, (first, second) = refs[:6], refs[6:]
    planes, rows, depth = local[2].shape
    even = parity_of(axis)
    lane = lanes_of((rows, depth))

    @pl.loop(0, planes)
    def _(x):
        high = jnp.zeros((rows, depth), f32)
        low = jnp.zeros((rows, depth), f32)
        for c in range(CHANNELS):
            values = channel_of(local, c, x)
            here = (lane >= W * c) & (lane < W * c + W)
            high = jnp.where(here, pltpu.roll(values, (W * c + W) % depth, 1), high)
            low = jnp.where(here, pltpu.roll(values, (W * c) % depth, 1), low)
        first[x] = pick(even, high, low)
        second[x] = pick(even, low, high)


def pack_x(axis, *refs):
    local, outs = refs[:6], refs[6:]
    planes = local[2].shape[0]
    even = parity_of(axis)
    for out, up in zip(outs, (even == 0, even != 0)):
        near = jnp.where(up, planes - NEAR, 0)
        far = jnp.where(up, planes - W, W - 1)
        for c in range(CHANNELS):
            for q in range(NEAR):
                out[c * NEAR + q] = channel_of(local, c, near + q)
            if c < FAR:
                out[CHANNELS * NEAR + c] = channel_of(local, c, far)


def join_x(axis, z_axis, planes, za, zb, a_in, b_in, a_out, b_out, low, high, sems):
    even_z = parity_of(z_axis)
    even = parity_of(axis)
    low[...] = pick(even_z, zb[...], za[...])
    high[...] = pick(even_z, za[...], zb[...])
    copies = []
    for n, (out, up) in enumerate(((a_out, even == 0), (b_out, even != 0))):
        start = jnp.where(up, planes - W, 0)
        for m, source in enumerate((low, high)):
            copies.append(
                pltpu.make_async_copy(
                    source.at[pl.ds(start, W)],
                    out.at[pl.ds(XMAIN + m * W, W)],
                    sems.at[n, m],
                )
            )
    for copy in copies:
        copy.start()
    for copy in copies:
        copy.wait()


def pack_y(axis, z_axis, *refs):
    local, (za, zb), outs = refs[:6], refs[6:8], refs[8:]
    planes, rows = local[2].shape[:2]
    even = parity_of(axis)
    even_z = parity_of(z_axis)
    for n in range(CHANNELS):
        for x in range(planes):
            values = channel_of(local, n, x)
            head, tail = values[:W], values[rows - W :]
            for out, up, down in zip(outs, (tail, head), (head, tail)):
                out[n * planes + x] = pick(even, up, down)
    for x in range(planes):
        for m, values in enumerate((pick(even_z, zb[x], za[x]), pick(even_z, za[x], zb[x]))):
            head, tail = values[:W], values[rows - W :]
            for out, up, down in zip(outs, (tail, head), (head, tail)):
                out[(CHANNELS + m) * planes + x] = pick(even, up, down)


def join_y(axis, x_axis, count, planes, *refs):
    xa, xb = refs[:2]
    outs = refs[2 + count : 2 + 2 * count]
    stage, sems = refs[2 + 2 * count :]
    rows = xa.shape[1]
    even = parity_of(axis)
    even_x = parity_of(x_axis)

    @pl.loop(0, XMSG)
    def _(n):
        a, b = xa[n], xb[n]
        for m, values in enumerate((pick(even_x, b, a), pick(even_x, a, b))):
            head, tail = values[:W], values[rows - W :]
            for i, (up, down) in enumerate(((tail, head), (head, tail))[:count]):
                stage[i, m * XMSG + n] = pick(even, up, down)

    base = (CHANNELS + 2) * planes
    copies = [
        pltpu.make_async_copy(stage.at[i], out.at[pl.ds(base, 2 * XMSG)], sems.at[i])
        for i, out in enumerate(outs)
    ]
    for copy in copies:
        copy.start()
    for copy in copies:
        copy.wait()


PRESS, MOB, SLOPE, ACT = 0, 1, 4, 7
SHIFTED = 8
TOP = 8


def shift_z(first, second, step):
    depth = first.shape[-1]
    lane = lanes_of(first.shape)
    edge = lane == (depth - 1 if step > 0 else 0)
    amount = depth - 1 if step > 0 else 1
    a, b = pltpu.roll(first, amount, 1), pltpu.roll(second, amount, 1)
    return jnp.where(edge, b, a), jnp.where(edge, a, b)


def solve(axes, count_y, *refs):
    local = refs[:6]
    tables = refs[6:9]
    za, zb, xa, xb = refs[9:13]
    ys = refs[13 : 13 + count_y]
    residual, update = refs[13 + count_y : 15 + count_y]
    (zl, zh, raw, fields, lower, weight, coupling, scale, start, store, sol) = refs[15 + count_y :]
    planes, rows, depth = local[2].shape
    even_x, even_y, even_z = (parity_of(axis) for axis in axes)
    ya = ys[0] if count_y > 0 else None
    yb = ys[1] if count_y > 1 else None
    total = planes + 2 * W

    def both(a, b, even):
        return pick(even, b, a), pick(even, a, b)

    def put_halo_rows(target, n):
        low, high = None, None
        a = None if ya is None else ya[n]
        b = None if yb is None else yb[n]
        if a is None:
            low = high = jnp.zeros((W, depth), f32)
        else:
            low, high = pick(even_y, b, a), pick(even_y, a, b)
        target[TOP - W : TOP, :] = low
        target[TOP + rows : TOP + rows + W, :] = high

    body_rows = slice(TOP, TOP + rows)
    x_base = (CHANNELS + 2) * planes

    @pl.loop(0, planes)
    def _(x):
        low, high = both(za[x], zb[x], even_z)
        for m, (target, values) in enumerate(((zl, low), (zh, high))):
            put_halo_rows(target.at[W + x], (CHANNELS + m) * planes + x)
            target[W + x, body_rows, :] = values
        for c in range(CHANNELS):
            put_halo_rows(raw.at[c, W + x, 0], c * planes + x)
            raw[c, W + x, 0, body_rows, :] = channel_of(local, c, x)

    def from_x(target_low, target_high, n):
        low, high = both(xa[n], xb[n], even_x)
        put_halo_rows(target_low, x_base + n)
        target_low[body_rows, :] = low
        put_halo_rows(target_high, x_base + XMSG + n)
        target_high[body_rows, :] = high

    @pl.loop(0, CHANNELS)
    def _(c):
        for q in range(NEAR):
            from_x(raw.at[c, 1 + q, 0], raw.at[c, W + planes + q, 0], c * NEAR + q)

    @pl.loop(0, FAR)
    def _(c):
        from_x(raw.at[c, 0, 0], raw.at[c, total - 1, 0], CHANNELS * NEAR + c)

    for m, target in enumerate((zl, zh)):
        for q in range(W):
            from_x(target.at[q], target.at[W + planes + q], XMAIN + m * W + q)

    tiles = (rows + 2 * W) // 8
    lane = lanes_of((8, depth))

    @pl.loop(0, total)
    def _(x):
        for tile in range(tiles):
            span = slice(TOP - W + 8 * tile, TOP - W + 8 * tile + 8)
            low, high = zl[x, span, :], zh[x, span, :]
            for c in range(CHANNELS):
                above = pltpu.roll(high, (depth - W * c) % depth, 1)
                below = pltpu.roll(low, (2 * depth - W - W * c) % depth, 1)
                raw[c, x, 1, span, :] = jnp.where(lane < W, above, below)

    @pl.loop(0, total)
    def _(x):
        for tile in range(tiles):
            span = slice(TOP - W + 8 * tile, TOP - W + 8 * tile + 8)
            pair = []
            for side in range(2):
                get = lambda c: raw[c, x, side, span, :]
                press, water, gas, active, region = (get(c) for c in range(5))
                looked = [[jnp.full((8, depth), table[c, 0], f32) for c in range(3)] for table in tables]
                for level in range(1, tables[0].shape[1]):
                    chosen = region == level
                    for one, table in zip(looked, tables):
                        for c in range(3):
                            one[c] = jnp.where(chosen, table[c, level], one[c])
                formation, compress, viscous = looked
                sat = (water, 1.0 - water - gas, gas)
                expand = [formation[c] * jnp.exp(compress[c] * (press - 0.5)) for c in range(3)]
                mob = [viscous[c] * expand[c] * sat[c] * sat[c] for c in range(3)]
                pore = get(CHANNELS - 1)
                stored = pore * (compress[0] * sat[0] + compress[1] * sat[1] + compress[2] * sat[2])
                stored = jnp.where(active > 0, stored, 1.0)
                for c in range(3):
                    weight[c, x, side, span, :] = active / (expand[c] * stored)
                    raw[FAR + FLAT + c, x, side, span, :] = (
                        pore * expand[c] * sat[c] - get(FAR + FLAT + c)
                    )
                one = [press] + mob + [compress[c] * mob[c] for c in range(3)] + [active]
                trans = []
                for k in range(UP):
                    half = 0.5 * get(t_channel(k))
                    raw[t_channel(k), x, side, span, :] = half
                    trans.append(half * active)
                pair.append((one, trans))
            for f in range(SHIFTED):
                a, b = pair[0][0][f], pair[1][0][f]
                for step in (-1, 0, 1):
                    u, v = (a, b) if step == 0 else shift_z(a, b, step)
                    fields[f, step + 1, x, 0, span, :] = u
                    fields[f, step + 1, x, 1, span, :] = v
            for k, offset in enumerate(upper_offsets):
                u, v = pair[0][1][k], pair[1][1][k]
                if offset[2] != 0:
                    u, v = shift_z(u, v, -offset[2])
                lower[k, x, 0, span, :] = u
                lower[k, x, 1, span, :] = v

    base = TOP - W + 1

    def put_solution(slot, x, first, a, b):
        for step in (-1, 0, 1):
            u, v = (a, b) if step == 0 else shift_z(a, b, step)
            sol[slot, step + 1, x, 0, pl.ds(first, 8), :] = u
            sol[slot, step + 1, x, 1, pl.ds(first, 8), :] = v

    @pl.loop(1, total - 1)
    def _(x):
        for tile in range(tiles):
            first = base + 8 * tile
            out = slice(8 * tile, 8 * tile + 8)
            pair = []
            for side in range(2):
                def at(f, offset):
                    return fields[
                        f, offset[2] + 1, x + offset[0], side, pl.ds(first + offset[1], 8), :
                    ]

                here = (0, 0, 0)
                press = at(PRESS, here)
                w = [weight[c, x, side, pl.ds(first, 8), :] for c in range(3)]
                mob = [at(MOB + c, here) for c in range(3)]
                own_mob = w[0] * mob[0] + w[1] * mob[1] + w[2] * mob[2]
                own_slope = w[0] * at(SLOPE, here) + w[1] * at(SLOPE + 1, here) + w[2] * at(SLOPE + 2, here)
                flux = [jnp.zeros((8, depth), f32) for _ in range(3)]
                drops = jnp.zeros((8, depth), f32)
                means = jnp.ones((8, depth), f32)
                for n, offset in enumerate(neighbour_offsets):
                    if offset > here:
                        k = upper_offsets.index(offset)
                        link = raw[t_channel(k), x, side, pl.ds(first, 8), :] * at(ACT, offset)
                    else:
                        k = upper_offsets.index(tuple(-o for o in offset))
                        link = lower[k, x + offset[0], side, pl.ds(first + offset[1], 8), :]
                    drop = link * (press - at(PRESS, offset))
                    other = [at(MOB + c, offset) for c in range(3)]
                    for c in range(3):
                        flux[c] = flux[c] + drop * other[c]
                    drops = drops + drop
                    mean = own_mob + (w[0] * other[0] + w[1] * other[1] + w[2] * other[2])
                    slope = (
                        w[0] * at(SLOPE, offset)
                        + w[1] * at(SLOPE + 1, offset)
                        + w[2] * at(SLOPE + 2, offset)
                    )
                    mean = link * mean
                    means = means + mean
                    coupling[n, x, side, out, :] = drop * slope - mean
                active = at(ACT, here)
                res = [
                    active
                    * (raw[FAR + FLAT + c, x, side, pl.ds(first, 8), :] + (flux[c] + mob[c] * drops))
                    for c in range(3)
                ]
                if side == 0:
                    for c in range(3):
                        store[c, x, out, :] = res[c]
                diagonal = means + own_slope * drops
                rate = relax_weight / diagonal
                right = -(w[0] * res[0] + w[1] * res[1] + w[2] * res[2])
                guess = rate * right
                scale[x, side, out, :] = rate
                start[x, side, out, :] = guess
                pair.append(guess)
            put_solution(0, x, first, *pair)

    def relaxed(slot, x, side, first):
        get = lambda offset: sol[
            slot, offset[2] + 1, x + offset[0], side, pl.ds(first + offset[1], 8), :
        ]
        out = pl.ds(first - base, 8)
        parts = [jnp.zeros((8, depth), f32) for _ in range(2)]
        for n, offset in enumerate(neighbour_offsets):
            parts[n % 2] = parts[n % 2] + coupling[n, x, side, out, :] * get(offset)
        return (
            (1.0 - relax_weight) * get((0, 0, 0))
            + start[x, side, out, :]
            - scale[x, side, out, :] * (parts[0] + parts[1])
        )

    for sweep in range(2, SWEEPS):
        slot = sweep % 2

        @pl.loop(sweep, total - sweep)
        def _(x):
            for tile in range(tiles):
                first = base + 8 * tile
                put_solution(1 - slot, x, first, relaxed(slot, x, 0, first), relaxed(slot, x, 1, first))

    @pl.loop(0, planes)
    def _(x):
        for tile in range(rows // 8):
            first = TOP + 8 * tile
            span = slice(8 * tile, 8 * tile + 8)
            update[x, span, :] = relaxed(SWEEPS % 2, W + x, 0, first)
            for c in range(3):
                residual[c, x, span, :] = store[c, W + x, pl.ds(first - base, 8), :]


def params(mib):
    return pltpu.CompilerParams(vmem_limit_bytes=mib << 20)


def body(
    cell_state,
    old_mass,
    pore_volume,
    transmissibility,
    active_mask,
    pvt_region,
    formation_factor,
    compressibility,
    inverse_viscosity,
):
    ax, ay, az = "gx", "gy", "gz"
    planes, rows, depth = pore_volume.shape
    local = (cell_state, old_mass, pore_volume, transmissibility, active_mask, pvt_region)
    like = lambda *shape: jax.ShapeDtypeStruct(shape, f32)
    face = like(planes, rows, depth)
    z_send = pl.pallas_call(
        functools.partial(pack_z, az), out_shape=(face, face), compiler_params=params(16), name="pack_z"
    )(*local)
    za, zb = (
        jnp.zeros(face.shape, f32) if got is None else got for got in swaps(az, *z_send)
    )

    x_shape = like(XMSG, rows, depth)
    x_send = pl.pallas_call(
        functools.partial(pack_x, ax), out_shape=(x_shape, x_shape), compiler_params=params(16), name="pack_x"
    )(*local)
    x_send = pl.pallas_call(
        functools.partial(join_x, ax, az, planes),
        out_shape=(x_shape, x_shape),
        in_specs=[VMEM, VMEM, ANY, ANY],
        out_specs=(ANY, ANY),
        scratch_shapes=[
            pltpu.VMEM(face.shape, f32),
            pltpu.VMEM(face.shape, f32),
            pltpu.SemaphoreType.DMA((2, 2)),
        ],
        input_output_aliases={2: 0, 3: 1},
        compiler_params=params(8),
        name="join_x",
    )(za, zb, *x_send)
    xa, xb = (
        jnp.zeros(x_shape.shape, f32) if got is None else got for got in swaps(ax, *x_send)
    )

    count_y = min(lax.axis_size(ay) - 1, 2)
    ys = []
    if count_y:
        y_shape = like((CHANNELS + 2) * planes + 2 * XMSG, W, depth)
        y_send = pl.pallas_call(
            functools.partial(pack_y, ay, az),
            out_shape=(y_shape,) * count_y,
            compiler_params=params(16),
            name="pack_y",
        )(*local, za, zb)
        y_send = pl.pallas_call(
            functools.partial(join_y, ay, ax, count_y, planes),
            out_shape=(y_shape,) * count_y,
            in_specs=[VMEM, VMEM] + [ANY] * count_y,
            out_specs=(ANY,) * count_y,
            scratch_shapes=[
                pltpu.VMEM((count_y, 2 * XMSG, W, depth), f32),
                pltpu.SemaphoreType.DMA((count_y,)),
            ],
            input_output_aliases={2 + i: i for i in range(count_y)},
            compiler_params=params(16),
            name="join_y",
        )(xa, xb, *y_send)
        ys = swaps(ay, y_send[0], y_send[-1])[:count_y]

    total = planes + 2 * W
    tall = rows + 2 * TOP
    inner = rows + 2 * W
    smem = pl.BlockSpec(memory_space=pltpu.SMEM)
    return pl.pallas_call(
        functools.partial(solve, (ax, ay, az), count_y),
        out_shape=(like(3, planes, rows, depth), face),
        in_specs=[VMEM] * 6 + [smem] * 3 + [VMEM] * (4 + count_y),
        out_specs=(VMEM, VMEM),
        scratch_shapes=[
            pltpu.VMEM((total, tall, depth), f32),
            pltpu.VMEM((total, tall, depth), f32),
            pltpu.VMEM((CHANNELS, total, 2, tall, depth), f32),
            pltpu.VMEM((SHIFTED, 3, total, 2, tall, depth), f32),
            pltpu.VMEM((UP, total, 2, tall, depth), f32),
            pltpu.VMEM((3, total, 2, tall, depth), f32),
            pltpu.VMEM((2 * UP, total, 2, inner, depth), f32),
            pltpu.VMEM((total, 2, inner, depth), f32),
            pltpu.VMEM((total, 2, inner, depth), f32),
            pltpu.VMEM((3, total, inner, depth), f32),
            pltpu.VMEM((2, 3, total, 2, tall, depth), f32),
        ],
        compiler_params=params(60),
        name="solve",
    )(
        *local,
        formation_factor,
        compressibility,
        inverse_viscosity,
        za,
        zb,
        xa,
        xb,
        *ys,
    )


def solution(mesh):
    return jax.shard_map(
        body,
        mesh=mesh,
        in_specs=(
            P(None, "gx", "gy", "gz"),
            P(None, "gx", "gy", "gz"),
            P("gx", "gy", "gz"),
            P(None, "gx", "gy", "gz"),
            P("gx", "gy", "gz"),
            P("gx", "gy", "gz"),
            P(),
            P(),
            P(),
        ),
        out_specs=(P(None, "gx", "gy", "gz"), P("gx", "gy", "gz")),
        check_vma=False,
    )
```

time: 142 us -> 77.3 us (0.54)
  the two profiles are of different devices: /device:TPU:1 before, /device:TPU:17 now
where the time goes in v1:
time: 77.3 us; the launch traced here: 77 us
  waiting for transfers between devices  31.2 us (40%)
  Pallas kernels  30.3 us (39%)
  starting transfers between devices  8.27 us (11%)
  local copies, waits for them, and re-layouts  6.52 us (8%)
    ppermute x5, waiting for transfers between devices, swaps(): got.append(lax.ppermute(message, axis, pairs + [(b, a) for a, b in pairs]))  31.2 us
    pallas_call x1, Pallas kernels, body(): pl.pallas_call(functools.partial(solve, (ax, ay, az), count_y), out_shape...  27.8 us
    ppermute x5, starting transfers between devices, swaps(): got.append(lax.ppermute(message, axis, pairs + [(b, a) for a, b in pairs]))  8.27 us
    unnamed x22, local copies, waits for them, and re-layouts  6.52 us
  transfers between devices with their start and end apart: 5, of which 4 were waited for; matrix products, arithmetic and copies ran while one was open for 0% of the time, Pallas kernels for 0%

profile of v1, /device:TPU:17, one launch (start us, length us, event | category | flops | bytes accessed | tf_op | source)
XLA Modules:
  0.0 77.0 jit_solution(4224037577143191964)
XLA Ops:
  0.6 0.0 copy-start
  0.6 1.1 %copy-done = f32[13,8,16,128]{3,2,1,0:T(8,128)S(1)} copy-done((f32[13,8,16,128]{3,2,1,0:T(8,128)S(1)}, f32[13,8,16,128]{3,2,1,0:T(8,128)}, u32[]{:S(2)}) %copy-start) | copy-done | bytes 851992
  1.8 0.0 copy-start.1
  1.8 0.9 %copy-done.1 = f32[3,8,16,128]{3,2,1,0:T(8,128)S(1)} copy-done((f32[3,8,16,128]{3,2,1,0:T(8,128)S(1)}, f32[3,8,16,128]{3,2,1,0:T(8,128)}, u32[]{:S(2)}) %copy-start.1) | copy-done | bytes 196632
  2.7 0.0 copy-start.2
  2.7 0.9 %copy-done.2 = f32[3,8,16,128]{3,2,1,0:T(8,128)S(1)} copy-done((f32[3,8,16,128]{3,2,1,0:T(8,128)S(1)}, f32[3,8,16,128]{3,2,1,0:T(8,128)}, u32[]{:S(2)}) %copy-start.2) | copy-done | bytes 196632
  3.6 0.0 copy-start.5
  3.6 0.8 %copy-done.5 = f32[8,16,128]{2,1,0:T(8,128)S(1)} copy-done((f32[8,16,128]{2,1,0:T(8,128)S(1)}, f32[8,16,128]{2,1,0:T(8,128)}, u32[]{:S(2)}) %copy-start.5) | copy-done | bytes 65560
  4.5 0.0 copy-start.6
  4.5 0.8 %copy-done.6 = s32[8,16,128]{2,1,0:T(8,128)S(1)} copy-done((s32[8,16,128]{2,1,0:T(8,128)S(1)}, s32[8,16,128]{2,1,0:T(8,128)}, u32[]{:S(2)}) %copy-start.6) | copy-done | bytes 65560
  5.3 0.0 copy-start.7
  5.3 0.8 %copy-done.7 = s32[8,16,128]{2,1,0:T(8,128)S(1)} copy-done((s32[8,16,128]{2,1,0:T(8,128)S(1)}, s32[8,16,128]{2,1,0:T(8,128)}, u32[]{:S(2)}) %copy-start.7) | copy-done | bytes 65560
  6.2 1.3 %pack_z.1 = (f32[8,16,128]{2,1,0:T(8,128)S(1)}, f32[8,16,128]{2,1,0:T(8,128)S(1)}) custom-call(f32[3,8,16,128]{3,2,1,0:T(8,128)S(1)} %copy-done.1, f32[3,8,16,128]{3,2,1,0:T(8,128)S(1)} %copy-done.2, f32[8,16,128]{2,1,0:T(8,128)S(1)} %copy-done.5, f32[13,8,16,128]{3,2,1,0:T(8,128)S(1)} %copy-done, s32[8,16,128]{2,1,0:T(8,128)S(1)} %copy-done.6, ...), custom_call_target="tpu_custom_call" | custom-call | tf_op jit(solution)/shard_map/pack_z/pallas_call | solution.py:440
  7.4 0.7 collective-permute-start
  8.2 3.0 %collective-permute-start.1 = (f32[8,16,128]{2,1,0:T(8,128)S(1)}, f32[8,16,128]{2,1,0:T(8,128)S(1)}, u32[]{:S(2)}, u32[]{:S(2)}) collective-permute-start(f32[8,16,128]{2,1,0:T(8,128)S(1)} %get-tuple-element.9), channel_id=1, source_target_pairs={{1,2},{2,1},{5,6},{6,5},{9,10},{10,9},{13,14},{14,13},{17,18},{18,... | collective-permute-start | bytes 196616 | tf_op jit(solution)/shard_map/ppermute | solution.py:78
  11.2 0.1 pack_x.1
  11.3 0.0 collective-permute-done.za.refs_6_.refs_9_
  11.3 0.0 copy-start.8
  11.3 2.7 %collective-permute-done.1.zb.refs_7_.refs_10_ = f32[8,16,128]{2,1,0:T(8,128)S(1)} collective-permute-done((f32[8,16,128]{2,1,0:T(8,128)S(1)}, f32[8,16,128]{2,1,0:T(8,128)S(1)}, u32[]{:S(2)}, u32[]{:S(2)}) %collective-permute-start.1) | collective-permute-done | bytes 65568 | tf_op jit(solution)/shard_map/ppermute | solution.py:78
  14.1 0.0 copy-start.9
  14.1 0.2 join_x.1
  14.3 1.4 %collective-permute-start.2 = (f32[88,16,128]{2,1,0:T(8,128)S(1)}, f32[88,16,128]{2,1,0:T(8,128)S(1)}, u32[]{:S(2)}, u32[]{:S(2)}) collective-permute-start(f32[88,16,128]{2,1,0:T(8,128)S(1)} %get-tuple-element.12), channel_id=1, source_target_pairs={{0,8},{16,24},{8,0},{24,16},{1,9},{17,25},{9,1},{25,17},{2,10},{18... | collective-permute-start | bytes 2162696 | tf_op jit(solution)/shard_map/ppermute | solution.py:78
  15.7 1.9 %collective-permute-start.3 = (f32[88,16,128]{2,1,0:T(8,128)S(1)}, f32[88,16,128]{2,1,0:T(8,128)S(1)}, u32[]{:S(2)}, u32[]{:S(2)}) collective-permute-start(f32[88,16,128]{2,1,0:T(8,128)S(1)} %get-tuple-element.13), channel_id=1, source_target_pairs={{8,16},{16,8},{9,17},{17,9},{10,18},{18,10},{11,19},{19,11},{12,20... | collective-permute-start | bytes 2162696 | tf_op jit(solution)/shard_map/ppermute | solution.py:78
  17.6 0.0 copy-done.8
  17.6 0.0 copy-done.9
  17.6 0.1 pack_y.1.refs_2_
  17.7 10.4 %collective-permute-done.2.refs_0_.refs_11_ = f32[88,16,128]{2,1,0:T(8,128)S(1)} collective-permute-done((f32[88,16,128]{2,1,0:T(8,128)S(1)}, f32[88,16,128]{2,1,0:T(8,128)S(1)}, u32[]{:S(2)}, u32[]{:S(2)}) %collective-permute-start.2) | collective-permute-done | bytes 720928 | tf_op jit(solution)/shard_map/ppermute | solution.py:78
  28.1 0.0 copy-start.3
  28.1 3.5 %collective-permute-done.3.refs_1_.refs_12_ = f32[88,16,128]{2,1,0:T(8,128)S(1)} collective-permute-done((f32[88,16,128]{2,1,0:T(8,128)S(1)}, f32[88,16,128]{2,1,0:T(8,128)S(1)}, u32[]{:S(2)}, u32[]{:S(2)}) %collective-permute-start.3) | collective-permute-done | bytes 720928 | tf_op jit(solution)/shard_map/ppermute | solution.py:78
  31.5 0.0 copy-start.4
  31.5 0.8 join_y.1
  32.3 0.0 copy-done.3
  32.3 0.1 copy-done.4
  32.4 1.2 %collective-permute-start.4 = (f32[368,4,128]{2,1,0:T(4,128)S(1)}, f32[368,4,128]{2,1,0:T(4,128)S(1)}, u32[]{:S(2)}, u32[]{:S(2)}) collective-permute-start(f32[368,4,128]{2,1,0:T(4,128)S(1)} %join_y.1), channel_id=1, source_target_pairs={{0,4},{4,0},{1,5},{5,1},{2,6},{6,2},{3,7},{7,3},{8,12},{12,8},{9,1... | collective-permute-start | bytes 2261000 | tf_op jit(solution)/shard_map/ppermute | solution.py:78
  33.6 14.6 %collective-permute-done.4.refs_13_ = f32[368,4,128]{2,1,0:T(4,128)S(1)} collective-permute-done((f32[368,4,128]{2,1,0:T(4,128)S(1)}, f32[368,4,128]{2,1,0:T(4,128)S(1)}, u32[]{:S(2)}, u32[]{:S(2)}) %collective-permute-start.4) | collective-permute-done | bytes 753696 | tf_op jit(solution)/shard_map/ppermute | solution.py:78
  48.2 0.0 copy-start.10
  48.2 0.9 %copy-done.10 = f32[368,4,128]{2,1,0:T(4,128)} copy-done((f32[368,4,128]{2,1,0:T(4,128)}, f32[368,4,128]{2,1,0:T(4,128)S(1)}, u32[]{:S(2)}) %copy-start.10) | copy-done | bytes 753688
  49.1 27.8 %solve.1 = (f32[3,8,16,128]{3,2,1,0:T(8,128)}, f32[8,16,128]{2,1,0:T(8,128)}) custom-call(f32[3,8,16,128]{3,2,1,0:T(8,128)} %refs_0_.7, f32[3,8,16,128]{3,2,1,0:T(8,128)} %refs_1_.7, f32[8,16,128]{2,1,0:T(8,128)} %refs_2_.7, f32[13,8,16,128]{3,2,1,0:T(8,128)} %refs_3_.7, s32[8,16,128]{2,1,0:T(8,128)} %refs_4_.7, s32[8,16,128]{2,1,0:T(8,128)} %refs_5_.7, ...), custom_call_target="tpu_custom_call" | custom-call | tf_op jit(solution)/shard_map/solve/pallas_call | solution.py:498
Async XLA Ops:
  0.6 1.2 %copy-start = (f32[13,8,16,128]{3,2,1,0:T(8,128)S(1)}, f32[13,8,16,128]{3,2,1,0:T(8,128)}, u32[]{:S(2)}) copy-start(f32[13,8,16,128]{3,2,1,0:T(8,128)} %refs_3_.7) | copy-start | bytes 2555908
  1.8 0.9 %copy-start.1 = (f32[3,8,16,128]{3,2,1,0:T(8,128)S(1)}, f32[3,8,16,128]{3,2,1,0:T(8,128)}, u32[]{:S(2)}) copy-start(f32[3,8,16,128]{3,2,1,0:T(8,128)} %refs_0_.7) | copy-start | bytes 589828
  2.7 0.9 %copy-start.2 = (f32[3,8,16,128]{3,2,1,0:T(8,128)S(1)}, f32[3,8,16,128]{3,2,1,0:T(8,128)}, u32[]{:S(2)}) copy-start(f32[3,8,16,128]{3,2,1,0:T(8,128)} %refs_1_.7) | copy-start | bytes 589828
  3.6 0.8 %copy-start.5 = (f32[8,16,128]{2,1,0:T(8,128)S(1)}, f32[8,16,128]{2,1,0:T(8,128)}, u32[]{:S(2)}) copy-start(f32[8,16,128]{2,1,0:T(8,128)} %refs_2_.7) | copy-start | bytes 196612
  4.5 0.8 %copy-start.6 = (s32[8,16,128]{2,1,0:T(8,128)S(1)}, s32[8,16,128]{2,1,0:T(8,128)}, u32[]{:S(2)}) copy-start(s32[8,16,128]{2,1,0:T(8,128)} %refs_4_.7) | copy-start | bytes 196612
  5.3 0.8 %copy-start.7 = (s32[8,16,128]{2,1,0:T(8,128)S(1)}, s32[8,16,128]{2,1,0:T(8,128)}, u32[]{:S(2)}) copy-start(s32[8,16,128]{2,1,0:T(8,128)} %refs_5_.7) | copy-start | bytes 196612
  7.4 3.9 %collective-permute-start = (f32[8,16,128]{2,1,0:T(8,128)S(1)}, f32[8,16,128]{2,1,0:T(8,128)S(1)}, u32[]{:S(2)}, u32[]{:S(2)}) collective-permute-start(f32[8,16,128]{2,1,0:T(8,128)S(1)} %get-tuple-element.8), channel_id=1, source_target_pairs={{0,1},{2,3},{1,0},{3,2},{4,5},{6,7},{5,4},{7,6},{8,9},{10,11},{9,8... | collective-permute-start | bytes 196616 | tf_op jit(solution)/shard_map/ppermute | solution.py:78
  8.2 5.9 %collective-permute-start.1 = (f32[8,16,128]{2,1,0:T(8,128)S(1)}, f32[8,16,128]{2,1,0:T(8,128)S(1)}, u32[]{:S(2)}, u32[]{:S(2)}) collective-permute-start(f32[8,16,128]{2,1,0:T(8,128)S(1)} %get-tuple-element.9), channel_id=1, source_target_pairs={{1,2},{2,1},{5,6},{6,5},{9,10},{10,9},{13,14},{14,13},{17,18},{18,... | collective-permute-start | bytes 196616 | tf_op jit(solution)/shard_map/ppermute | solution.py:78
  11.3 6.2 %copy-start.8 = (f32[8,16,128]{2,1,0:T(8,128)}, f32[8,16,128]{2,1,0:T(8,128)S(1)}, u32[]{:S(2)}) copy-start(f32[8,16,128]{2,1,0:T(8,128)S(1)} %collective-permute-done.za.refs_6_.refs_9_) | copy-start | bytes 196612
  14.1 3.5 %copy-start.9 = (f32[8,16,128]{2,1,0:T(8,128)}, f32[8,16,128]{2,1,0:T(8,128)S(1)}, u32[]{:S(2)}) copy-start(f32[8,16,128]{2,1,0:T(8,128)S(1)} %collective-permute-done.1.zb.refs_7_.refs_10_) | copy-start | bytes 196612
  14.3 13.8 %collective-permute-start.2 = (f32[88,16,128]{2,1,0:T(8,128)S(1)}, f32[88,16,128]{2,1,0:T(8,128)S(1)}, u32[]{:S(2)}, u32[]{:S(2)}) collective-permute-start(f32[88,16,128]{2,1,0:T(8,128)S(1)} %get-tuple-element.12), channel_id=1, source_target_pairs={{0,8},{16,24},{8,0},{24,16},{1,9},{17,25},{9,1},{25,17},{2,10},{18... | collective-permute-start | bytes 2162696 | tf_op jit(solution)/shard_map/ppermute | solution.py:78
  15.7 15.9 %collective-permute-start.3 = (f32[88,16,128]{2,1,0:T(8,128)S(1)}, f32[88,16,128]{2,1,0:T(8,128)S(1)}, u32[]{:S(2)}, u32[]{:S(2)}) collective-permute-start(f32[88,16,128]{2,1,0:T(8,128)S(1)} %get-tuple-element.13), channel_id=1, source_target_pairs={{8,16},{16,8},{9,17},{17,9},{10,18},{18,10},{11,19},{19,11},{12,20... | collective-permute-start | bytes 2162696 | tf_op jit(solution)/shard_map/ppermute | solution.py:78
  28.1 4.2 %copy-start.3 = (f32[88,16,128]{2,1,0:T(8,128)}, f32[88,16,128]{2,1,0:T(8,128)S(1)}, u32[]{:S(2)}) copy-start(f32[88,16,128]{2,1,0:T(8,128)S(1)} %collective-permute-done.2.refs_0_.refs_11_) | copy-start | bytes 2162692
  31.5 0.9 %copy-start.4 = (f32[88,16,128]{2,1,0:T(8,128)}, f32[88,16,128]{2,1,0:T(8,128)S(1)}, u32[]{:S(2)}) copy-start(f32[88,16,128]{2,1,0:T(8,128)S(1)} %collective-permute-done.3.refs_1_.refs_12_) | copy-start | bytes 2162692
  32.4 15.8 %collective-permute-start.4 = (f32[368,4,128]{2,1,0:T(4,128)S(1)}, f32[368,4,128]{2,1,0:T(4,128)S(1)}, u32[]{:S(2)}, u32[]{:S(2)}) collective-permute-start(f32[368,4,128]{2,1,0:T(4,128)S(1)} %join_y.1), channel_id=1, source_target_pairs={{0,4},{4,0},{1,5},{5,1},{2,6},{6,2},{3,7},{7,3},{8,12},{12,8},{9,1... | collective-permute-start | bytes 2261000 | tf_op jit(solution)/shard_map/ppermute | solution.py:78
  48.2 0.9 %copy-start.10 = (f32[368,4,128]{2,1,0:T(4,128)}, f32[368,4,128]{2,1,0:T(4,128)S(1)}, u32[]{:S(2)}) copy-start(f32[368,4,128]{2,1,0:T(4,128)S(1)} %collective-permute-done.4.refs_13_) | copy-start | bytes 2260996

commit v2 on v0

v2 whole, which is shorter than its diff:
```python
import functools

import jax
import jax.numpy as jnp
from jax import lax
from jax.experimental import pallas as pl
from jax.experimental.pallas import tpu as pltpu
from jax.sharding import PartitionSpec as P

SWEEPS = 4
W = SWEEPS
relax_weight = 0.7

neighbour_offsets = [
    (along_x, along_y, along_z)
    for along_x in (-1, 0, 1)
    for along_y in (-1, 0, 1)
    for along_z in (-1, 0, 1)
    if (along_x, along_y, along_z) != (0, 0, 0)
]
upper_offsets = [offset for offset in neighbour_offsets if offset > (0, 0, 0)]
UP = len(upper_offsets)
FLAT = sum(1 for offset in upper_offsets if offset[0] == 0)
STEP = UP - FLAT

FAR = 5 + STEP
CHANNELS = FAR + FLAT + 4
NEAR = W - 1
XMAIN = CHANNELS * NEAR + FAR
VMEM = pl.BlockSpec(memory_space=pltpu.VMEM)
ANY = pl.BlockSpec(memory_space=pl.ANY)
f32 = jnp.float32


def t_channel(k):
    return FAR + k if k < FLAT else 5 + k - FLAT


def pick(parity, even, odd):
    shape = (even if odd is None else odd).shape
    if even is None:
        even = jnp.zeros(shape, f32)
    if odd is None:
        odd = jnp.zeros(shape, f32)
    return jnp.where(jnp.full(shape, parity, jnp.int32) == 0, even, odd)


def parity_of(axis):
    return lax.rem(lax.axis_index(axis), 2)


def swaps(axis, first, second):
    count = lax.axis_size(axis)
    got = []
    for start, message in ((0, first), (1, second)):
        pairs = [(i, i + 1) for i in range(start, count - 1, 2)]
        if not pairs:
            got.append(None)
            continue
        got.append(lax.ppermute(message, axis, pairs + [(b, a) for a, b in pairs]))
    return got


def lanes_of(shape):
    return lax.broadcasted_iota(jnp.int32, shape, len(shape) - 1)


def span_of(planes):
    return 2 * W * planes


def groups_of(planes, depth):
    per = depth // span_of(planes)
    return per, -(-CHANNELS // per)


def pack_z(axis, *refs):
    state, mass, pore, trans, active, region, local, first, second, flags, sems = refs
    planes, rows, depth = pore.shape
    copies = [
        pltpu.make_async_copy(active, flags.at[0], sems.at[0]),
        pltpu.make_async_copy(region, flags.at[1], sems.at[1]),
        pltpu.make_async_copy(state, local.at[0:3], sems.at[2]),
        pltpu.make_async_copy(trans.at[FLAT:UP], local.at[5:FAR], sems.at[3]),
        pltpu.make_async_copy(trans.at[0:FLAT], local.at[FAR : FAR + FLAT], sems.at[4]),
        pltpu.make_async_copy(mass, local.at[FAR + FLAT : CHANNELS - 1], sems.at[5]),
        pltpu.make_async_copy(pore, local.at[CHANNELS - 1], sems.at[6]),
    ]
    for copy in copies:
        copy.start()
    copies[0].wait()
    copies[1].wait()
    local[3:5] = flags[...].astype(f32)
    for copy in copies[2:]:
        copy.wait()

    per, groups = groups_of(planes, depth)
    even = parity_of(axis)
    lane = lanes_of((8, depth))

    @pl.loop(0, rows // 8)
    def _(tile):
        span = pl.ds(pl.multiple_of(8 * tile, 8), 8)
        for group in range(groups):
            high = jnp.zeros((8, depth), f32)
            low = jnp.zeros((8, depth), f32)
            for c in range(group * per, min(CHANNELS, group * per + per)):
                for x in range(planes):
                    base = (c % per) * span_of(planes) + 2 * W * x
                    values = local[c, x, span, :]
                    here = (lane >= base + W) & (lane < base + 2 * W)
                    high = jnp.where(here, pltpu.roll(values, (base + 2 * W) % depth, 1), high)
                    here = (lane >= base) & (lane < base + W)
                    low = jnp.where(here, pltpu.roll(values, base % depth, 1), low)
            first[group, span, :] = pick(even, high, low)
            second[group, span, :] = pick(even, low, high)


def pack_x(axis, local, *outs):
    planes = local.shape[1]
    even = parity_of(axis)
    for out, up in zip(outs, (even == 0, even != 0)):
        near = jnp.where(up, planes - NEAR, 0)
        far = jnp.where(up, planes - W, W - 1)
        for c in range(CHANNELS):
            for q in range(NEAR):
                out[c * NEAR + q] = local[c, near + q]
            if c < FAR:
                out[CHANNELS * NEAR + c] = local[c, far]


def join_x(za, zb, a_in, b_in, a_out, b_out, columns, sems):
    columns[...] = za[...] + zb[...]
    copies = [
        pltpu.make_async_copy(columns, out.at[pl.ds(XMAIN, columns.shape[0])], sems.at[n])
        for n, out in enumerate((a_out, b_out))
    ]
    for copy in copies:
        copy.start()
    for copy in copies:
        copy.wait()


def put_rows(outs, n, values, even):
    head, tail = values[:W], values[values.shape[0] - W :]
    for out, up, down in zip(outs, (tail, head), (head, tail)):
        out[n] = pick(even, up, down)


def pack_y(axis, local, *outs):
    planes = local.shape[1]
    even = parity_of(axis)
    for c in range(CHANNELS):
        for x in range(planes):
            put_rows(outs, c * planes + x, local[c, x], even)


def join_y(axis, x_axis, count, planes, za, zb, xa, xb, *refs):
    outs, columns = refs[count : 2 * count], refs[2 * count]
    stages, sems = refs[2 * count + 1 : 3 * count + 1], refs[3 * count + 1]
    rows, depth = xa.shape[1:]
    even = parity_of(axis)
    even_x = parity_of(x_axis)
    per, _ = groups_of(planes, depth)
    lane = lanes_of((rows, depth))
    for c in range(CHANNELS):
        group, base = c // per, (c % per) * span_of(planes)
        a, b = xa[XMAIN + group], xb[XMAIN + group]
        own = pltpu.roll(za[group] + zb[group], (2 * W * W - base) % depth, 1)
        below = pltpu.roll(pick(even_x, b, a), (depth - base - 2 * W * (planes - W)) % depth, 1)
        above = pltpu.roll(pick(even_x, a, b), (2 * W * (planes + W) - base) % depth, 1)
        values = jnp.where(lane < 2 * W * W, below, jnp.where(lane < 2 * W * (W + planes), own, above))
        columns[c] = values
        put_rows(stages, 2 * XMAIN + c, values, even)

    @pl.loop(0, XMAIN // 4)
    def _(i):
        for j in range(4):
            n = 4 * i + j
            a, b = xa[n], xb[n]
            put_rows(stages, n, pick(even_x, b, a), even)
            put_rows(stages, XMAIN + n, pick(even_x, a, b), even)

    copies = [
        pltpu.make_async_copy(
            stage, out.at[pl.ds(CHANNELS * planes, 2 * XMAIN + CHANNELS)], sems.at[i]
        )
        for i, (stage, out) in enumerate(zip(stages, outs))
    ]
    for copy in copies:
        copy.start()
    for copy in copies:
        copy.wait()


PRESS, MOB, SLOPE, ACT = 0, 1, 4, 7
SHIFTED = 8


def z_shift(values, columns, plane, step):
    depth = values.shape[-1]
    lane = lanes_of(values.shape)
    if step > 0:
        edge = pltpu.roll(columns, depth - 1 - 2 * W * plane, 1)
        return jnp.where(lane == depth - 1, edge, pltpu.roll(values, depth - 1, 1))
    edge = pltpu.roll(columns, depth - 2 * W * plane - 2 * W + 1, 1)
    return jnp.where(lane == 0, edge, pltpu.roll(values, 1, 1))


def z_shift_columns(values, step):
    return pltpu.roll(values, values.shape[-1] - 1 if step > 0 else 1, 1)


def z_edge(current, values, plane, step):
    lane = lanes_of(values.shape)
    if step > 0:
        at = 2 * W * plane + 2 * W - 1
        return jnp.where(lane == at, pltpu.roll(values, at, 1), current)
    at = 2 * W * plane
    return jnp.where(lane == at, pltpu.roll(values, at + 1, 1), current)


def fill_tables(tables, tabs):
    lane = lanes_of(tabs.shape[1:])
    for n, table in enumerate(tables):
        for c in range(3):
            values = jnp.full(tabs.shape[1:], table[c, 0], f32)
            for level in range(1, table.shape[1]):
                values = jnp.where(lane == level, table[c, level], values)
            tabs[3 * n + c] = values


def properties(get, plane, is_columns, first, tabs, arrays):
    fields, lower, half, weight, accum, centre = arrays
    total = fields.shape[2] - 1
    span = pl.ds(first, 8)
    press, water, gas, active, region = (get(c) for c in range(5))
    index = region.astype(jnp.int32)
    look = [
        jnp.take_along_axis(tabs[n], index, axis=1, mode="promise_in_bounds") for n in range(9)
    ]
    formation, compress, viscous = look[:3], look[3:6], look[6:]
    sat = (water, 1.0 - water - gas, gas)
    expand = [formation[c] * jnp.exp(compress[c] * (press - 0.5)) for c in range(3)]
    mob = [viscous[c] * expand[c] * sat[c] * sat[c] for c in range(3)]
    pore = get(CHANNELS - 1)
    stored = pore * (compress[0] * sat[0] + compress[1] * sat[1] + compress[2] * sat[2])
    stored = jnp.where(active > 0, stored, 1.0)
    for c in range(3):
        weight[c, plane, span, :] = active / (expand[c] * stored)
        accum[c, plane, span, :] = pore * expand[c] * sat[c] - get(FAR + FLAT + c)
    one = [press] + mob + [compress[c] * mob[c] for c in range(3)] + [active]
    for f, values in enumerate(one):
        fields[f, 1, plane, span, :] = values
        for step in (-1, 1):
            if is_columns:
                fields[f, step + 1, plane, span, :] = z_shift_columns(values, step)
            else:
                columns = fields[f, 1, total, span, :]
                fields[f, step + 1, plane, span, :] = z_shift(values, columns, plane, step)
                current = fields[f, step + 1, total, span, :]
                fields[f, step + 1, total, span, :] = z_edge(current, values, plane, step)
    for k, offset in enumerate(upper_offsets):
        values = 0.5 * get(t_channel(k))
        half[k, plane, span, :] = values
        values = values * active
        step = -offset[2]
        if step == 0:
            lower[k, plane, span, :] = values
        elif is_columns:
            centre[k, span, :] = values
            lower[k, plane, span, :] = z_shift_columns(values, step)
        else:
            lower[k, plane, span, :] = z_shift(values, centre[k, span, :], plane, step)
            current = lower[k, total, span, :]
            lower[k, total, span, :] = z_edge(current, values, plane, step)


def x_roll(values, step, is_columns):
    if not is_columns or step == 0:
        return values
    depth = values.shape[-1]
    return pltpu.roll(values, (depth - 2 * W * step) % depth, 1)


def link_cells(plane, is_columns, first, stride, arrays, out, coupling, scale, start):
    fields, lower, half, weight, accum, _ = arrays
    depth = fields.shape[-1]
    here = (0, 0, 0)

    def read(ref, lead, offset):
        dx = 0 if is_columns else offset[0]
        values = ref[(*lead, plane + dx, pl.ds(first + stride * offset[1], 8), slice(None))]
        return x_roll(values, offset[0], is_columns)

    def at(f, offset):
        return read(fields, (f, offset[2] + 1), offset)

    press = at(PRESS, here)
    w = [read(weight, (c,), here) for c in range(3)]
    mob = [at(MOB + c, here) for c in range(3)]
    own_mob = w[0] * mob[0] + w[1] * mob[1] + w[2] * mob[2]
    own_slope = w[0] * at(SLOPE, here) + w[1] * at(SLOPE + 1, here) + w[2] * at(SLOPE + 2, here)
    flux = [jnp.zeros((8, depth), f32) for _ in range(3)]
    drops = jnp.zeros((8, depth), f32)
    means = jnp.ones((8, depth), f32)
    for n, offset in enumerate(neighbour_offsets):
        if offset > here:
            link = read(half, (upper_offsets.index(offset),), here) * at(ACT, offset)
        else:
            k = upper_offsets.index(tuple(-o for o in offset))
            link = read(lower, (k,), offset)
        drop = link * (press - at(PRESS, offset))
        other = [at(MOB + c, offset) for c in range(3)]
        for c in range(3):
            flux[c] = flux[c] + drop * other[c]
        drops = drops + drop
        mean = link * (own_mob + (w[0] * other[0] + w[1] * other[1] + w[2] * other[2]))
        slope = (
            w[0] * at(SLOPE, offset) + w[1] * at(SLOPE + 1, offset) + w[2] * at(SLOPE + 2, offset)
        )
        means = means + mean
        coupling[n, plane, out, :] = drop * slope - mean
    active = at(ACT, here)
    res = [
        active * (read(accum, (c,), here) + (flux[c] + mob[c] * drops)) for c in range(3)
    ]
    rate = relax_weight / (means + own_slope * drops)
    scale[plane, out, :] = rate
    start[plane, out, :] = -rate * (w[0] * res[0] + w[1] * res[1] + w[2] * res[2])
    return res


def inner(x_axis, local, columns, xa, xb, *refs):
    tables, (coupling, scale, start, store) = refs[:3], refs[3:7]
    tabs, arrays = refs[7], refs[8:]
    planes, rows, depth = local.shape[1:]
    total = planes + 2 * W
    even_x = parity_of(x_axis)
    fill_tables(tables, tabs)
    tiles = range(rows // 8)

    def cells(get, plane, is_columns=False):
        for tile in tiles:
            span = slice(8 * tile, 8 * tile + 8)
            properties(lambda c: get(c, span), plane, is_columns, 8 + 8 * tile, tabs, arrays)

    cells(lambda c, span: columns[c, span, :], total, True)

    @pl.loop(0, planes)
    def _(x):
        cells(lambda c, span: local[c, x, span, :], W + x)

    def from_x(n, low):
        a, b = xa, xb
        def get(c, span):
            i = n(c)
            if i is None:
                return jnp.zeros((8, depth), f32)
            u, v = xa[i, span, :], xb[i, span, :]
            return pick(even_x, v, u) if low else pick(even_x, u, v)
        return get

    @pl.loop(0, NEAR)
    def _(q):
        near = lambda c: c * NEAR + q
        cells(from_x(near, True), 1 + q)
        cells(from_x(near, False), W + planes + q)

    far = lambda c: CHANNELS * NEAR + c if c < FAR else None
    cells(from_x(far, True), 0)
    cells(from_x(far, False), total - 1)

    def links(plane, is_columns=False):
        for tile in tiles:
            out = slice(8 * tile, 8 * tile + 8)
            res = link_cells(
                plane, is_columns, 8 + 8 * tile, 1, arrays, out, coupling, scale, start
            )
            if not is_columns:
                for c in range(3):
                    store[c, plane, out, :] = res[c]

    links(total, True)

    @pl.loop(1, total - 1)
    def _(plane):
        links(plane)


RING = 2 * (W + 2)


def finish(axes, count_y, local, columns, xa, xb, *refs):
    tables = refs[:3]
    ys = refs[3 : 3 + count_y]
    coupling, scale, start, store, residual, update = refs[3 + count_y : 9 + count_y]
    tabs, raw, edge_coupling, edge_scale, edge_start, edge_store, sol, edge_sol = refs[
        9 + count_y : 17 + count_y
    ]
    arrays = refs[17 + count_y :]
    planes, rows, depth = local.shape[1:]
    total = planes + 2 * W
    even_x, even_y, _ = (parity_of(axis) for axis in axes)
    fill_tables(tables, tabs)

    def put(c, plane, values, n):
        low = high = jnp.zeros((W, depth), f32)
        if count_y:
            a = ys[0][n]
            b = ys[1][n] if count_y > 1 else None
            low, high = pick(even_y, b, a), pick(even_y, a, b)
        raw[c, plane, pl.ds(0, 2, stride=2), :] = values[rows - 2 :]
        raw[c, plane, pl.ds(4, W, stride=2), :] = high
        raw[c, plane, pl.ds(1, W, stride=2), :] = low
        raw[c, plane, pl.ds(RING - 3, 2, stride=2), :] = values[:2]
        raw[c, plane, RING:16, :] = jnp.zeros((16 - RING, depth), f32)

    base = CHANNELS * planes

    @pl.loop(0, CHANNELS)
    def _(c):
        for x in range(planes):
            put(c, W + x, local[c, x], c * planes + x)
        for q in range(NEAR):
            n = c * NEAR + q
            a, b = xa[n], xb[n]
            put(c, 1 + q, pick(even_x, b, a), base + n)
            put(c, W + planes + q, pick(even_x, a, b), base + XMAIN + n)
        put(c, total, columns[c], base + 2 * XMAIN + c)

    @pl.loop(0, FAR)
    def _(c):
        n = CHANNELS * NEAR + c
        a, b = xa[n], xb[n]
        put(c, 0, pick(even_x, b, a), base + n)
        put(c, total - 1, pick(even_x, a, b), base + XMAIN + n)

    for c in range(FAR, CHANNELS):
        for plane in (0, total - 1):
            raw[c, plane] = jnp.zeros((16, depth), f32)

    def cells(plane, is_columns=False):
        for tile in range(2):
            span = slice(8 * tile, 8 * tile + 8)
            properties(
                lambda c: raw[c, plane, span, :], plane, is_columns, 8 * tile, tabs, arrays
            )

    cells(total, True)

    @pl.loop(0, total)
    def _(plane):
        cells(plane)

    def links(plane, is_columns=False):
        res = link_cells(
            plane, is_columns, 2, 2, arrays, slice(0, 8), edge_coupling, edge_scale, edge_start
        )
        if not is_columns:
            for c in range(3):
                edge_store[c, plane] = res[c]

    links(total, True)

    @pl.loop(1, total - 1)
    def _(plane):
        links(plane)

    tiles = rows // 8

    def put_rows_of(slot, step, plane, mains, edge):
        to = lambda row: (slot, step + 1, plane, slice(row, row + 1), slice(None))
        for tile, values in enumerate(mains):
            sol[slot, step + 1, plane, 8 + 8 * tile : 16 + 8 * tile, :] = values
        edge_sol[slot, step + 1, plane, 2:10, :] = edge
        sol[to(7)] = edge[5:6]
        sol[to(8)] = edge[7:8]
        sol[to(7 + rows)] = edge[0:1]
        sol[to(8 + rows)] = edge[2:3]
        edge_sol[to(0)] = mains[-1][6:7]
        edge_sol[to(RING - 1)] = mains[0][1:2]

    def parts_of(slot, step, plane):
        mains = [
            sol[slot, step + 1, plane, 8 + 8 * tile : 16 + 8 * tile, :] for tile in range(tiles)
        ]
        return mains, edge_sol[slot, step + 1, plane, 2:10, :]

    def put_solution(slot, plane, mains, edge, is_columns=False):
        put_rows_of(slot, 0, plane, mains, edge)
        for step in (-1, 1):
            if is_columns:
                shift = lambda values: z_shift_columns(values, step)
                put_rows_of(slot, step, plane, [shift(values) for values in mains], shift(edge))
                continue
            column_mains, column_edge = parts_of(slot, 0, total)
            put_rows_of(
                slot,
                step,
                plane,
                [z_shift(u, v, plane, step) for u, v in zip(mains, column_mains)],
                z_shift(edge, column_edge, plane, step),
            )
            own_mains, own_edge = parts_of(slot, 0, plane)
            column_mains, column_edge = parts_of(slot, step, total)
            put_rows_of(
                slot,
                step,
                total,
                [z_edge(u, v, plane, step) for u, v in zip(column_mains, own_mains)],
                z_edge(column_edge, own_edge, plane, step),
            )

    def relaxed(slot, plane, tile, is_columns=False):
        if tile is None:
            ref, first, stride, out = edge_sol, 2, 2, slice(0, 8)
            factors = (edge_coupling, edge_scale, edge_start)
        else:
            ref, first, stride, out = sol, 8 + 8 * tile, 1, slice(8 * tile, 8 * tile + 8)
            factors = (coupling, scale, start)

        def get(offset):
            dx = 0 if is_columns else offset[0]
            values = ref[slot, offset[2] + 1, plane + dx, pl.ds(first + stride * offset[1], 8), :]
            return x_roll(values, offset[0], is_columns)

        parts = [jnp.zeros((8, depth), f32) for _ in range(2)]
        for n, offset in enumerate(neighbour_offsets):
            parts[n % 2] = parts[n % 2] + factors[0][n, plane, out, :] * get(offset)
        return (
            (1.0 - relax_weight) * get((0, 0, 0))
            + factors[2][plane, out, :]
            - factors[1][plane, out, :] * (parts[0] + parts[1])
        )

    def first_sweep(plane, is_columns=False):
        mains = [start[plane, 8 * tile : 8 * tile + 8, :] for tile in range(tiles)]
        put_solution(0, plane, mains, edge_start[plane], is_columns)

    first_sweep(total, True)

    @pl.loop(1, total - 1)
    def _(plane):
        first_sweep(plane)

    def sweep_of(slot, plane, is_columns=False):
        mains = [relaxed(slot, plane, tile, is_columns) for tile in range(tiles)]
        put_solution(1 - slot, plane, mains, relaxed(slot, plane, None, is_columns), is_columns)

    for sweep in range(2, SWEEPS):
        slot = sweep % 2
        sweep_of(slot, total, True)

        @pl.loop(sweep, total - sweep)
        def _(plane):
            sweep_of(slot, plane)

    @pl.loop(0, planes)
    def _(x):
        slot, plane = SWEEPS % 2, W + x
        edge = relaxed(slot, plane, None)
        for tile in range(tiles):
            span = slice(8 * tile, 8 * tile + 8)
            update[x, span, :] = relaxed(slot, plane, tile)
            for c in range(3):
                residual[c, x, span, :] = store[c, plane, span, :]
        update[x, 0:1, :] = edge[7:8]
        update[x, rows - 1 : rows, :] = edge[0:1]
        for c in range(3):
            residual[c, x, 0:1, :] = edge_store[c, plane, 7:8, :]
            residual[c, x, rows - 1 : rows, :] = edge_store[c, plane, 0:1, :]


def call(kernel, name, mib, **options):
    return pl.pallas_call(
        kernel,
        name=name,
        compiler_params=pltpu.CompilerParams(vmem_limit_bytes=mib << 20),
        **options,
    )


def cell_arrays(total, height, depth):
    return [
        pltpu.VMEM((SHIFTED, 3, total + 1, height, depth), f32),
        pltpu.VMEM((UP, total + 1, height, depth), f32),
        pltpu.VMEM((UP, total + 1, height, depth), f32),
        pltpu.VMEM((3, total + 1, height, depth), f32),
        pltpu.VMEM((3, total + 1, height, depth), f32),
        pltpu.VMEM((UP, height, depth), f32),
    ]


def body(
    cell_state,
    old_mass,
    pore_volume,
    transmissibility,
    active_mask,
    pvt_region,
    formation_factor,
    compressibility,
    inverse_viscosity,
):
    ax, ay, az = "gx", "gy", "gz"
    planes, rows, depth = pore_volume.shape
    total = planes + 2 * W
    per, groups = groups_of(planes, depth)
    assert per >= 1 and 2 * W * total <= depth and rows % 8 == 0 and RING <= 16
    tables = (formation_factor, compressibility, inverse_viscosity)
    like = lambda *shape: jax.ShapeDtypeStruct(shape, f32)
    fill = lambda shape, got: [jnp.zeros(shape.shape, f32) if one is None else one for one in got]

    z_shape = like(groups, rows, depth)
    local, *z_send = call(
        functools.partial(pack_z, az),
        "pack_z",
        8,
        out_shape=(like(CHANNELS, planes, rows, depth), z_shape, z_shape),
        in_specs=[ANY] * 6,
        out_specs=(VMEM,) * 3,
        scratch_shapes=[
            pltpu.VMEM((2, planes, rows, depth), jnp.int32),
            pltpu.SemaphoreType.DMA((7,)),
        ],
    )(cell_state, old_mass, pore_volume, transmissibility, active_mask, pvt_region)
    za, zb = fill(z_shape, swaps(az, *z_send))

    x_shape = like(XMAIN + groups, rows, depth)
    x_send = call(
        functools.partial(pack_x, ax), "pack_x", 8, out_shape=(x_shape, x_shape)
    )(local)
    x_send = call(
        join_x,
        "join_x",
        8,
        out_shape=(x_shape, x_shape),
        in_specs=[VMEM, VMEM, ANY, ANY],
        out_specs=(ANY, ANY),
        scratch_shapes=[pltpu.VMEM(z_shape.shape, f32), pltpu.SemaphoreType.DMA((2,))],
        input_output_aliases={2: 0, 3: 1},
    )(za, zb, *x_send)
    xa, xb = fill(x_shape, swaps(ax, *x_send))

    count_y = min(lax.axis_size(ay) - 1, 2)
    extra = 2 * XMAIN + CHANNELS
    y_shape = like(CHANNELS * planes + extra, W, depth)
    y_send = ()
    if count_y:
        y_send = call(
            functools.partial(pack_y, ay), "pack_y", 8, out_shape=(y_shape,) * count_y
        )(local)
    *y_send, columns = call(
        functools.partial(join_y, ay, ax, count_y, planes),
        "join_y",
        8,
        out_shape=(y_shape,) * count_y + (like(CHANNELS, rows, depth),),
        in_specs=[VMEM] * 4 + [ANY] * count_y,
        out_specs=(ANY,) * count_y + (VMEM,),
        scratch_shapes=[pltpu.VMEM((extra, W, depth), f32)] * count_y
        + [pltpu.SemaphoreType.DMA((max(count_y, 1),))],
        input_output_aliases={4 + i: i for i in range(count_y)},
    )(za, zb, xa, xb, *y_send)
    ys = swaps(ay, y_send[0], y_send[-1])[:count_y] if count_y else []

    smem = pl.BlockSpec(memory_space=pltpu.SMEM)
    tabs = pltpu.VMEM((9, 8, depth), f32)
    halves = call(
        functools.partial(inner, ax),
        "inner",
        24,
        out_shape=(
            like(2 * UP, total + 1, rows, depth),
            like(total + 1, rows, depth),
            like(total + 1, rows, depth),
            like(3, total, rows, depth),
        ),
        in_specs=[VMEM] * 4 + [smem] * 3,
        out_specs=(VMEM,) * 4,
        scratch_shapes=[tabs] + cell_arrays(total, rows + 16, depth),
    )(local, columns, xa, xb, *tables)

    return call(
        functools.partial(finish, (ax, ay, az), count_y),
        "finish",
        24,
        out_shape=(like(3, planes, rows, depth), like(planes, rows, depth)),
        in_specs=[VMEM] * 4 + [smem] * 3 + [VMEM] * (count_y + 4),
        out_specs=(VMEM, VMEM),
        scratch_shapes=[
            tabs,
            pltpu.VMEM((CHANNELS, total + 1, 16, depth), f32),
            pltpu.VMEM((2 * UP, total + 1, 8, depth), f32),
            pltpu.VMEM((total + 1, 8, depth), f32),
            pltpu.VMEM((total + 1, 8, depth), f32),
            pltpu.VMEM((3, total, 8, depth), f32),
            pltpu.VMEM((2, 3, total + 1, rows + 16, depth), f32),
            pltpu.VMEM((2, 3, total + 1, 16, depth), f32),
        ]
        + cell_arrays(total, 16, depth),
    )(local, columns, xa, xb, *tables, *ys, *halves)


def solution(mesh):
    return jax.shard_map(
        body,
        mesh=mesh,
        in_specs=(
            P(None, "gx", "gy", "gz"),
            P(None, "gx", "gy", "gz"),
            P("gx", "gy", "gz"),
            P(None, "gx", "gy", "gz"),
            P("gx", "gy", "gz"),
            P("gx", "gy", "gz"),
            P(),
            P(),
            P(),
        ),
        out_specs=(P(None, "gx", "gy", "gz"), P("gx", "gy", "gz")),
        check_vma=False,
    )
```

time: 142 us -> 124 us (0.87)
  the two profiles are of different devices: /device:TPU:1 before, /device:TPU:17 now
where the time goes in v2:
time: 124 us
  Pallas kernels  91.9 us (74%)
  waiting for transfers between devices  17.1 us (14%)
  starting transfers between devices  8.33 us (7%)
  local copies, waits for them, and re-layouts  5.54 us (4%)
    pallas_call x1, Pallas kernels, body(): call(functools.partial(finish, (ax, ay, az), count_y), 'finish', 24, out_...  50.3 us
    pallas_call x1, Pallas kernels, body(): call(functools.partial(inner, ax), 'inner', 24, out_shape=(like(2 * UP, t...  38.8 us
    ppermute x5, waiting for transfers between devices, swaps(): got.append(lax.ppermute(message, axis, pairs + [(b, a) for a, b in pairs]))  17.1 us
    ppermute x5, starting transfers between devices, swaps(): got.append(lax.ppermute(message, axis, pairs + [(b, a) for a, b in pairs]))  8.33 us
    unnamed x18, local copies, waits for them, and re-layouts  5.54 us
  transfers between devices with their start and end apart: 5, of which 3 were waited for; matrix products, arithmetic and copies ran while one was open for 0% of the time, Pallas kernels for 32%

profile of v2, /device:TPU:17, one launch (start us, length us, event | category | flops | bytes accessed | tf_op | source)
XLA Modules:
  0.0 123.6 jit_solution(17681149895948666518)
XLA Ops:
  0.6 0.0 copy-start
  0.6 1.1 copy-done
  1.8 0.0 copy-start.1
  1.8 0.9 copy-done.1
  2.7 0.0 copy-start.2
  2.7 0.9 copy-done.2
  3.6 0.0 copy-start.3
  3.6 0.8 copy-done.3
  4.5 0.0 copy-start.4
  4.5 0.8 copy-done.4
  5.3 0.0 copy-start.5
  5.3 0.8 copy-done.5
  6.2 1.8 %pack_z.1 = (f32[22,8,16,128]{3,2,1,0:T(8,128)S(1)}, f32[11,16,128]{2,1,0:T(8,128)S(1)}, f32[11,16,128]{2,1,0:T(8,128)S(1)}) custom-call(f32[3,8,16,128]{3,2,1,0:T(8,128)S(1)} %copy-done.1, f32[3,8,16,128]{3,2,1,0:T(8,128)S(1)} %copy-done.2, f32[8,16,128]{2,1,0:T(8,128)S(1)} %copy-done.3, f32[13,8,16,128]{3,2,1,0:T(8,128)S(1)} %copy-done, ...), custom_call_target="tpu_custom_call" | custom-call | tf_op jit(solution)/shard_map/pack_z/pallas_call | solution.py:616
  8.0 0.7 collective-permute-start
  8.7 3.0 %collective-permute-start.1 = (f32[11,16,128]{2,1,0:T(8,128)S(1)}, f32[11,16,128]{2,1,0:T(8,128)S(1)}, u32[]{:S(2)}, u32[]{:S(2)}) collective-permute-start(f32[11,16,128]{2,1,0:T(8,128)S(1)} %get-tuple-element.17), channel_id=1, source_target_pairs={{1,2},{2,1},{5,6},{6,5},{9,10},{10,9},{13,14},{14,13},{17,18},{18,... | collective-permute-start | bytes 270344 | tf_op jit(solution)/shard_map/ppermute | solution.py:60
  11.7 0.0 copy-start.6
  11.7 0.0 copy-start.7
  11.7 0.0 copy-start.8
  11.8 0.1 pack_x.1
  11.9 0.0 collective-permute-done.za
  11.9 2.9 %collective-permute-done.1.zb = f32[11,16,128]{2,1,0:T(8,128)S(1)} collective-permute-done((f32[11,16,128]{2,1,0:T(8,128)S(1)}, f32[11,16,128]{2,1,0:T(8,128)S(1)}, u32[]{:S(2)}, u32[]{:S(2)}) %collective-permute-start.1) | collective-permute-done | bytes 90144 | tf_op jit(solution)/shard_map/ppermute | solution.py:60
  14.8 0.3 join_x.1
  15.1 1.4 %collective-permute-start.2 = (f32[91,16,128]{2,1,0:T(8,128)S(1)}, f32[91,16,128]{2,1,0:T(8,128)S(1)}, u32[]{:S(2)}, u32[]{:S(2)}) collective-permute-start(f32[91,16,128]{2,1,0:T(8,128)S(1)} %get-tuple-element.20), channel_id=1, source_target_pairs={{0,8},{16,24},{8,0},{24,16},{1,9},{17,25},{9,1},{25,17},{2,10},{18... | collective-permute-start | bytes 2236424 | tf_op jit(solution)/shard_map/ppermute | solution.py:60
  16.5 1.9 %collective-permute-start.3 = (f32[91,16,128]{2,1,0:T(8,128)S(1)}, f32[91,16,128]{2,1,0:T(8,128)S(1)}, u32[]{:S(2)}, u32[]{:S(2)}) collective-permute-start(f32[91,16,128]{2,1,0:T(8,128)S(1)} %get-tuple-element.21), channel_id=1, source_target_pairs={{8,16},{16,8},{9,17},{17,9},{10,18},{18,10},{11,19},{19,11},{12,20... | collective-permute-start | bytes 2236424 | tf_op jit(solution)/shard_map/ppermute | solution.py:60
  18.4 0.1 pack_y.1.refs_0_
  18.5 10.7 %collective-permute-done.2.xa = f32[91,16,128]{2,1,0:T(8,128)S(1)} collective-permute-done((f32[91,16,128]{2,1,0:T(8,128)S(1)}, f32[91,16,128]{2,1,0:T(8,128)S(1)}, u32[]{:S(2)}, u32[]{:S(2)}) %collective-permute-start.2) | collective-permute-done | bytes 745504 | tf_op jit(solution)/shard_map/ppermute | solution.py:60
  29.2 3.5 %collective-permute-done.3.xb = f32[91,16,128]{2,1,0:T(8,128)S(1)} collective-permute-done((f32[91,16,128]{2,1,0:T(8,128)S(1)}, f32[91,16,128]{2,1,0:T(8,128)S(1)}, u32[]{:S(2)}, u32[]{:S(2)}) %collective-permute-start.3) | collective-permute-done | bytes 745504 | tf_op jit(solution)/shard_map/ppermute | solution.py:60
  32.6 0.6 join_y.1
  33.2 1.3 %collective-permute-start.4 = (f32[358,4,128]{2,1,0:T(4,128)S(1)}, f32[358,4,128]{2,1,0:T(4,128)S(1)}, u32[]{:S(2)}, u32[]{:S(2)}) collective-permute-start(f32[358,4,128]{2,1,0:T(4,128)S(1)} %get-tuple-element.23), channel_id=1, source_target_pairs={{0,4},{4,0},{1,5},{5,1},{2,6},{6,2},{3,7},{7,3},{8,12},{12,8},{9,1... | collective-permute-start | bytes 2199560 | tf_op jit(solution)/shard_map/ppermute | solution.py:60
  34.5 0.0 copy-done.6
  34.5 0.0 copy-done.7
  34.5 0.0 copy-done.8
  34.5 38.8 %inner.1 = (f32[26,17,16,128]{3,2,1,0:T(8,128)S(1)}, f32[17,16,128]{2,1,0:T(8,128)S(1)}, f32[17,16,128]{2,1,0:T(8,128)S(1)}, f32[3,16,16,128]{3,2,1,0:T(8,128)S(1)}) custom-call(f32[22,8,16,128]{3,2,1,0:T(8,128)S(1)} %get-tuple-element.15.local, f32[22,16,128]{2,1,0:T(8,128)S(1)} %get-tuple-element.22.columns, f32[91,16,128]{2,1,0:T(8,128)S(1)} %collective-permute-done.2.xa, ...), custom_call_target="tpu_custom_call" | custom-call | tf_op jit(solution)/shard_map/inner/pallas_call | solution.py:669
  73.3 0.0 collective-permute-done.4.refs_3_
  73.3 50.3 %finish.1 = (f32[3,8,16,128]{3,2,1,0:T(8,128)}, f32[8,16,128]{2,1,0:T(8,128)}) custom-call(f32[22,8,16,128]{3,2,1,0:T(8,128)S(1)} %get-tuple-element.15.local, f32[22,16,128]{2,1,0:T(8,128)S(1)} %get-tuple-element.22.columns, f32[91,16,128]{2,1,0:T(8,128)S(1)} %collective-permute-done.2.xa, f32[91,16,128]{2,1,0:T(8,128)S(1)} %collective-permute-done.3.xb, ...), custom_call_target="tpu_custom_call" | custom-call | tf_op jit(solution)/shard_map/finish/pallas_call | solution.py:684
Async XLA Ops:
  0.6 1.2 copy-start
  1.8 0.9 copy-start.1
  2.7 0.9 copy-start.2
  3.6 0.8 copy-start.3
  4.5 0.8 copy-start.4
  5.3 0.8 copy-start.5
  8.0 3.9 %collective-permute-start = (f32[11,16,128]{2,1,0:T(8,128)S(1)}, f32[11,16,128]{2,1,0:T(8,128)S(1)}, u32[]{:S(2)}, u32[]{:S(2)}) collective-permute-start(f32[11,16,128]{2,1,0:T(8,128)S(1)} %get-tuple-element.16), channel_id=1, source_target_pairs={{0,1},{2,3},{1,0},{3,2},{4,5},{6,7},{5,4},{7,6},{8,9},{10,11},{9,8... | collective-permute-start | bytes 270344 | tf_op jit(solution)/shard_map/ppermute | solution.py:60
  8.7 6.1 %collective-permute-start.1 = (f32[11,16,128]{2,1,0:T(8,128)S(1)}, f32[11,16,128]{2,1,0:T(8,128)S(1)}, u32[]{:S(2)}, u32[]{:S(2)}) collective-permute-start(f32[11,16,128]{2,1,0:T(8,128)S(1)} %get-tuple-element.17), channel_id=1, source_target_pairs={{1,2},{2,1},{5,6},{6,5},{9,10},{10,9},{13,14},{14,13},{17,18},{18,... | collective-permute-start | bytes 270344 | tf_op jit(solution)/shard_map/ppermute | solution.py:60
  11.7 22.8 %copy-start.6 = (f32[3,8]{1,0:T(4,128)S(1)}, f32[3,8]{1,0:T(4,128)}, u32[]{:S(2)}) copy-start(f32[3,8]{1,0:T(4,128)} %refs_0_.5) | copy-start | bytes 292
  11.7 22.8 %copy-start.7 = (f32[3,8]{1,0:T(4,128)S(1)}, f32[3,8]{1,0:T(4,128)}, u32[]{:S(2)}) copy-start(f32[3,8]{1,0:T(4,128)} %refs_1_.5) | copy-start | bytes 292
  11.7 22.8 %copy-start.8 = (f32[3,8]{1,0:T(4,128)S(1)}, f32[3,8]{1,0:T(4,128)}, u32[]{:S(2)}) copy-start(f32[3,8]{1,0:T(4,128)} %refs_2_.5) | copy-start | bytes 292
  15.1 14.1 %collective-permute-start.2 = (f32[91,16,128]{2,1,0:T(8,128)S(1)}, f32[91,16,128]{2,1,0:T(8,128)S(1)}, u32[]{:S(2)}, u32[]{:S(2)}) collective-permute-start(f32[91,16,128]{2,1,0:T(8,128)S(1)} %get-tuple-element.20), channel_id=1, source_target_pairs={{0,8},{16,24},{8,0},{24,16},{1,9},{17,25},{9,1},{25,17},{2,10},{18... | collective-permute-start | bytes 2236424 | tf_op jit(solution)/shard_map/ppermute | solution.py:60
  16.5 16.2 %collective-permute-start.3 = (f32[91,16,128]{2,1,0:T(8,128)S(1)}, f32[91,16,128]{2,1,0:T(8,128)S(1)}, u32[]{:S(2)}, u32[]{:S(2)}) collective-permute-start(f32[91,16,128]{2,1,0:T(8,128)S(1)} %get-tuple-element.21), channel_id=1, source_target_pairs={{8,16},{16,8},{9,17},{17,9},{10,18},{18,10},{11,19},{19,11},{12,20... | collective-permute-start | bytes 2236424 | tf_op jit(solution)/shard_map/ppermute | solution.py:60
  33.2 40.1 %collective-permute-start.4 = (f32[358,4,128]{2,1,0:T(4,128)S(1)}, f32[358,4,128]{2,1,0:T(4,128)S(1)}, u32[]{:S(2)}, u32[]{:S(2)}) collective-permute-start(f32[358,4,128]{2,1,0:T(4,128)S(1)} %get-tuple-element.23), channel_id=1, source_target_pairs={{0,4},{4,0},{1,5},{5,1},{2,6},{6,2},{3,7},{7,3},{8,12},{12,8},{9,1... | collective-permute-start | bytes 2199560 | tf_op jit(solution)/shard_map/ppermute | solution.py:60

commit v3 on v2

--- a/solution.py
+++ b/solution.py
@@ -29,6 +29,7 @@
 XMAIN = CHANNELS * NEAR + FAR
 VMEM = pl.BlockSpec(memory_space=pltpu.VMEM)
 ANY = pl.BlockSpec(memory_space=pl.ANY)
+HBM = pl.BlockSpec(memory_space=pltpu.MemorySpace.HBM)
 f32 = jnp.float32
 
 
@@ -230,9 +231,9 @@
             tabs[3 * n + c] = values
 
 
-def properties(get, plane, is_columns, first, tabs, arrays):
-    fields, lower, half, weight, accum, centre = arrays
-    total = fields.shape[2] - 1
+def properties(get, plane, is_columns, first, tabs, arrays, halo):
+    fields, lower, half, weight, accum, _ = halo if is_columns else arrays
+    halo_fields, halo_lower, centre = halo[0], halo[1], halo[5]
     span = pl.ds(first, 8)
     press, water, gas, active, region = (get(c) for c in range(5))
     index = region.astype(jnp.int32)
@@ -256,10 +257,10 @@
             if is_columns:
                 fields[f, step + 1, plane, span, :] = z_shift_columns(values, step)
             else:
-                columns = fields[f, 1, total, span, :]
+                columns = halo_fields[f, 1, 0, span, :]
                 fields[f, step + 1, plane, span, :] = z_shift(values, columns, plane, step)
-                current = fields[f, step + 1, total, span, :]
-                fields[f, step + 1, total, span, :] = z_edge(current, values, plane, step)
+                current = halo_fields[f, step + 1, 0, span, :]
+                halo_fields[f, step + 1, 0, span, :] = z_edge(current, values, plane, step)
     for k, offset in enumerate(upper_offsets):
         values = 0.5 * get(t_channel(k))
         half[k, plane, span, :] = values
@@ -272,8 +273,8 @@
             lower[k, plane, span, :] = z_shift_columns(values, step)
         else:
             lower[k, plane, span, :] = z_shift(values, centre[k, span, :], plane, step)
-            current = lower[k, total, span, :]
-            lower[k, total, span, :] = z_edge(current, values, plane, step)
+            current = halo_lower[k, 0, span, :]
+            halo_lower[k, 0, span, :] = z_edge(current, values, plane, step)
 
 
 def x_roll(values, step, is_columns):
@@ -283,8 +284,9 @@
     return pltpu.roll(values, (depth - 2 * W * step) % depth, 1)
 
 
-def link_cells(plane, is_columns, first, stride, arrays, out, coupling, scale, start):
+def link_cells(plane, is_columns, first, stride, arrays, out, results):
     fields, lower, half, weight, accum, _ = arrays
+    coupling, scale, start = results
     depth = fields.shape[-1]
     here = (0, 0, 0)
 
@@ -332,8 +334,8 @@
 
 
 def inner(x_axis, local, columns, xa, xb, *refs):
-    tables, (coupling, scale, start, store) = refs[:3], refs[3:7]
-    tabs, arrays = refs[7], refs[8:]
+    tables, results, halo_results, store = refs[:3], refs[3:6], refs[6:9], refs[9]
+    tabs, arrays, halo = refs[10], refs[11:17], refs[17:]
     planes, rows, depth = local.shape[1:]
     total = planes + 2 * W
     even_x = parity_of(x_axis)
@@ -343,9 +345,9 @@
     def cells(get, plane, is_columns=False):
         for tile in tiles:
             span = slice(8 * tile, 8 * tile + 8)
-            properties(lambda c: get(c, span), plane, is_columns, 8 + 8 * tile, tabs, arrays)
-
-    cells(lambda c, span: columns[c, span, :], total, True)
+            properties(lambda c: get(c, span), plane, is_columns, 8 + 8 * tile, tabs, arrays, halo)
+
+    cells(lambda c, span: columns[c, span, :], 0, True)
 
     @pl.loop(0, planes)
     def _(x):
@@ -374,14 +376,13 @@
     def links(plane, is_columns=False):
         for tile in tiles:
             out = slice(8 * tile, 8 * tile + 8)
-            res = link_cells(
-                plane, is_columns, 8 + 8 * tile, 1, arrays, out, coupling, scale, start
-            )
+            own = (halo, out, halo_results) if is_columns else (arrays, out, results)
+            res = link_cells(plane, is_columns, 8 + 8 * tile, 1, *own)
             if not is_columns:
                 for c in range(3):
                     store[c, plane, out, :] = res[c]
 
-    links(total, True)
+    links(0, True)
 
     @pl.loop(1, total - 1)
     def _(plane):
@@ -394,11 +395,16 @@
 def finish(axes, count_y, local, columns, xa, xb, *refs):
     tables = refs[:3]
     ys = refs[3 : 3 + count_y]
-    coupling, scale, start, store, residual, update = refs[3 + count_y : 9 + count_y]
-    tabs, raw, edge_coupling, edge_scale, edge_start, edge_store, sol, edge_sol = refs[
-        9 + count_y : 17 + count_y
-    ]
-    arrays = refs[17 + count_y :]
+    results, halo_results, store, residual, update = (
+        refs[3 + count_y : 6 + count_y],
+        refs[6 + count_y : 9 + count_y],
+        *refs[9 + count_y : 12 + count_y],
+    )
+    refs = refs[12 + count_y :]
+    tabs, raw, edge_store = refs[:3]
+    edge_results, edge_halo_results = refs[3:6], refs[6:9]
+    sol, halo_sol, edge_sol, edge_halo_sol = refs[9:13]
+    arrays, halo = refs[13:19], refs[19:]
     planes, rows, depth = local.shape[1:]
     total = planes + 2 * W
     even_x, even_y, _ = (parity_of(axis) for axis in axes)
@@ -443,9 +449,8 @@
     def cells(plane, is_columns=False):
         for tile in range(2):
             span = slice(8 * tile, 8 * tile + 8)
-            properties(
-                lambda c: raw[c, plane, span, :], plane, is_columns, 8 * tile, tabs, arrays
-            )
+            get = lambda c: raw[c, plane, span, :]
+            properties(get, 0 if is_columns else plane, is_columns, 8 * tile, tabs, arrays, halo)
 
     cells(total, True)
 
@@ -454,14 +459,14 @@
         cells(plane)
 
     def links(plane, is_columns=False):
-        res = link_cells(
-            plane, is_columns, 2, 2, arrays, slice(0, 8), edge_coupling, edge_scale, edge_start
-        )
+        out = slice(0, 8)
+        own = (halo, out, edge_halo_results) if is_columns else (arrays, out, edge_results)
+        res = link_cells(plane, is_columns, 2, 2, *own)
         if not is_columns:
             for c in range(3):
                 edge_store[c, plane] = res[c]
 
-    links(total, True)
+    links(0, True)
 
     @pl.loop(1, total - 1)
     def _(plane):
@@ -469,56 +474,54 @@
 
     tiles = rows // 8
 
-    def put_rows_of(slot, step, plane, mains, edge):
-        to = lambda row: (slot, step + 1, plane, slice(row, row + 1), slice(None))
+    row = lax.broadcasted_iota(jnp.int32, (8, depth), 0)
+
+    def merged(mains, edge):
+        first, last = pltpu.roll(edge, 1, 0), pltpu.roll(edge, 7, 0)
+        mains = [jnp.where(row == 0, first, mains[0])] + mains[1:]
+        return mains[:-1] + [jnp.where(row == 7, last, mains[-1])]
+
+    def put_parts(is_columns, slot, step, plane, mains, edge):
+        to, edge_to = (halo_sol, edge_halo_sol) if is_columns else (sol, edge_sol)
         for tile, values in enumerate(mains):
-            sol[slot, step + 1, plane, 8 + 8 * tile : 16 + 8 * tile, :] = values
-        edge_sol[slot, step + 1, plane, 2:10, :] = edge
-        sol[to(7)] = edge[5:6]
-        sol[to(8)] = edge[7:8]
-        sol[to(7 + rows)] = edge[0:1]
-        sol[to(8 + rows)] = edge[2:3]
-        edge_sol[to(0)] = mains[-1][6:7]
-        edge_sol[to(RING - 1)] = mains[0][1:2]
-
-    def parts_of(slot, step, plane):
+            to[slot, step + 1, plane, 8 + 8 * tile : 16 + 8 * tile, :] = values
+        edge_to[slot, step + 1, plane, 2:10, :] = edge
+        to[slot, step + 1, plane, 7:8, :] = edge[5:6]
+        to[slot, step + 1, plane, 8 + rows : 9 + rows, :] = edge[2:3]
+        edge_to[slot, step + 1, plane, 0:1, :] = mains[-1][6:7]
+        edge_to[slot, step + 1, plane, RING - 1 : RING, :] = mains[0][1:2]
+
+    def halo_parts(slot, step):
         mains = [
-            sol[slot, step + 1, plane, 8 + 8 * tile : 16 + 8 * tile, :] for tile in range(tiles)
+            halo_sol[slot, step + 1, 0, 8 + 8 * tile : 16 + 8 * tile, :] for tile in range(tiles)
         ]
-        return mains, edge_sol[slot, step + 1, plane, 2:10, :]
+        return mains, edge_halo_sol[slot, step + 1, 0, 2:10, :]
 
     def put_solution(slot, plane, mains, edge, is_columns=False):
-        put_rows_of(slot, 0, plane, mains, edge)
+        mains = merged(mains, edge)
+        put_parts(is_columns, slot, 0, plane, mains, edge)
         for step in (-1, 1):
             if is_columns:
                 shift = lambda values: z_shift_columns(values, step)
-                put_rows_of(slot, step, plane, [shift(values) for values in mains], shift(edge))
+                put_parts(True, slot, step, plane, [shift(u) for u in mains], shift(edge))
                 continue
-            column_mains, column_edge = parts_of(slot, 0, total)
-            put_rows_of(
-                slot,
-                step,
-                plane,
-                [z_shift(u, v, plane, step) for u, v in zip(mains, column_mains)],
-                z_shift(edge, column_edge, plane, step),
-            )
-            own_mains, own_edge = parts_of(slot, 0, plane)
-            column_mains, column_edge = parts_of(slot, step, total)
-            put_rows_of(
-                slot,
-                step,
-                total,
-                [z_edge(u, v, plane, step) for u, v in zip(column_mains, own_mains)],
-                z_edge(column_edge, own_edge, plane, step),
-            )
+            shift = lambda u, v: z_shift(u, v, plane, step)
+            halo_mains, halo_edge = halo_parts(slot, 0)
+            shifted = [shift(u, v) for u, v in zip(mains, halo_mains)]
+            put_parts(False, slot, step, plane, shifted, shift(edge, halo_edge))
+            shift = lambda u, v: z_edge(u, v, plane, step)
+            halo_mains, halo_edge = halo_parts(slot, step)
+            shifted = [shift(u, v) for u, v in zip(halo_mains, mains)]
+            put_parts(True, slot, step, 0, shifted, shift(halo_edge, edge))
 
     def relaxed(slot, plane, tile, is_columns=False):
         if tile is None:
-            ref, first, stride, out = edge_sol, 2, 2, slice(0, 8)
-            factors = (edge_coupling, edge_scale, edge_start)
+            ref, first, stride, out = (edge_halo_sol if is_columns else edge_sol), 2, 2, slice(0, 8)
+            coupling, scale, start = edge_halo_results if is_columns else edge_results
         else:
-            ref, first, stride, out = sol, 8 + 8 * tile, 1, slice(8 * tile, 8 * tile + 8)
-            factors = (coupling, scale, start)
+            ref, first, stride = (halo_sol if is_columns else sol), 8 + 8 * tile, 1
+            out = slice(8 * tile, 8 * tile + 8)
+            coupling, scale, start = halo_results if is_columns else results
 
         def get(offset):
             dx = 0 if is_columns else offset[0]
@@ -527,18 +530,20 @@
 
         parts = [jnp.zeros((8, depth), f32) for _ in range(2)]
         for n, offset in enumerate(neighbour_offsets):
-            parts[n % 2] = parts[n % 2] + factors[0][n, plane, out, :] * get(offset)
+            parts[n % 2] = parts[n % 2] + coupling[n, plane, out, :] * get(offset)
         return (
             (1.0 - relax_weight) * get((0, 0, 0))
-            + factors[2][plane, out, :]
-            - factors[1][plane, out, :] * (parts[0] + parts[1])
+            + start[plane, out, :]
+            - scale[plane, out, :] * (parts[0] + parts[1])
         )
 
     def first_sweep(plane, is_columns=False):
+        start = (halo_results if is_columns else results)[2]
+        edge = (edge_halo_results if is_columns else edge_results)[2]
         mains = [start[plane, 8 * tile : 8 * tile + 8, :] for tile in range(tiles)]
-        put_solution(0, plane, mains, edge_start[plane], is_columns)
-
-    first_sweep(total, True)
+        put_solution(0, plane, mains, edge[plane], is_columns)
+
+    first_sweep(0, True)
 
     @pl.loop(1, total - 1)
     def _(plane):
@@ -550,7 +555,7 @@
 
     for sweep in range(2, SWEEPS):
         slot = sweep % 2
-        sweep_of(slot, total, True)
+        sweep_of(slot, 0, True)
 
         @pl.loop(sweep, total - sweep)
         def _(plane):
@@ -583,12 +588,24 @@
 
 def cell_arrays(total, height, depth):
     return [
-        pltpu.VMEM((SHIFTED, 3, total + 1, height, depth), f32),
-        pltpu.VMEM((UP, total + 1, height, depth), f32),
-        pltpu.VMEM((UP, total + 1, height, depth), f32),
-        pltpu.VMEM((3, total + 1, height, depth), f32),
-        pltpu.VMEM((3, total + 1, height, depth), f32),
-        pltpu.VMEM((UP, height, depth), f32),
+        pltpu.VMEM(shape, f32)
+        for count in (total, 1)
+        for shape in (
+            (SHIFTED, 3, count, height, depth),
+            (UP, count, height, depth),
+            (UP, count, height, depth),
+            (3, count, height, depth),
+            (3, count, height, depth),
+            (UP, height, depth),
+        )
+    ]
+
+
+def result_shapes(total, height, depth):
+    return [
+        shape
+        for count in (total, 1)
+        for shape in ((2 * UP, count, height, depth), (count, height, depth), (count, height, depth))
     ]
 
 
@@ -618,7 +635,7 @@
         "pack_z",
         8,
         out_shape=(like(CHANNELS, planes, rows, depth), z_shape, z_shape),
-        in_specs=[ANY] * 6,
+        in_specs=[HBM] * 6,
         out_specs=(VMEM,) * 3,
         scratch_shapes=[
             pltpu.VMEM((2, planes, rows, depth), jnp.int32),
@@ -670,14 +687,10 @@
         functools.partial(inner, ax),
         "inner",
         24,
-        out_shape=(
-            like(2 * UP, total + 1, rows, depth),
-            like(total + 1, rows, depth),
-            like(total + 1, rows, depth),
-            like(3, total, rows, depth),
-        ),
+        out_shape=[like(*shape) for shape in result_shapes(total, rows, depth)]
+        + [like(3, total, rows, depth)],
         in_specs=[VMEM] * 4 + [smem] * 3,
-        out_specs=(VMEM,) * 4,
+        out_specs=[VMEM] * 7,
         scratch_shapes=[tabs] + cell_arrays(total, rows + 16, depth),
     )(local, columns, xa, xb, *tables)
 
@@ -686,17 +699,17 @@
         "finish",
         24,
         out_shape=(like(3, planes, rows, depth), like(planes, rows, depth)),
-        in_specs=[VMEM] * 4 + [smem] * 3 + [VMEM] * (count_y + 4),
+        in_specs=[VMEM] * 4 + [smem] * 3 + [VMEM] * (count_y + 7),
         out_specs=(VMEM, VMEM),
         scratch_shapes=[
             tabs,
             pltpu.VMEM((CHANNELS, total + 1, 16, depth), f32),
-            pltpu.VMEM((2 * UP, total + 1, 8, depth), f32),
-            pltpu.VMEM((total + 1, 8, depth), f32),
-            pltpu.VMEM((total + 1, 8, depth), f32),
             pltpu.VMEM((3, total, 8, depth), f32),
-            pltpu.VMEM((2, 3, total + 1, rows + 16, depth), f32),
-            pltpu.VMEM((2, 3, total + 1, 16, depth), f32),
+            *(pltpu.VMEM(shape, f32) for shape in result_shapes(total, 8, depth)),
+            pltpu.VMEM((2, 3, total, rows + 16, depth), f32),
+            pltpu.VMEM((2, 3, 1, rows + 16, depth), f32),
+            pltpu.VMEM((2, 3, total, 16, depth), f32),
+            pltpu.VMEM((2, 3, 1, 16, depth), f32),
         ]
         + cell_arrays(total, 16, depth),
     )(local, columns, xa, xb, *tables, *ys, *halves)

time: 124 us -> 63.9 us (0.52)
  Pallas kernels: 91.9 us -> 28.1 us
  waiting for transfers between devices: 17.1 us -> 20.9 us
    pallas_call x1, Pallas kernels: 50.3 us -> 15.1 us  [body(): call(functools.partial(finish, (ax, ay, az), count_y), 'finish', 24, out_...]
    pallas_call x1, Pallas kernels: 38.8 us -> 10.1 us  [body(): call(functools.partial(inner, ax), 'inner', 24, out_shape=[like(*shape) f...]
    ppermute x5, waiting for transfers between devices: 17.1 us -> 20.9 us  [swaps(): got.append(lax.ppermute(message, axis, pairs + [(b, a) for a, b in pairs]))]
  transfers between devices with their start and end apart: 5 -> 5, of which waited for: 3 -> 4; matrix products, arithmetic and copies ran while one was open for 0% -> 0% of each run, Pallas kernels for 32% -> 16%
where the time goes in v3:
time: 63.9 us; the launch traced here: 63.6 us
  Pallas kernels  28.1 us (44%)
  waiting for transfers between devices  20.9 us (33%)
  starting transfers between devices  8.33 us (13%)
  local copies, waits for them, and re-layouts  5.54 us (9%)
  between operations  0.74 us (1%)
    ppermute x5, waiting for transfers between devices, swaps(): got.append(lax.ppermute(message, axis, pairs + [(b, a) for a, b in pairs]))  20.9 us
    pallas_call x1, Pallas kernels, body(): call(functools.partial(finish, (ax, ay, az), count_y), 'finish', 24, out_...  15.1 us
    pallas_call x1, Pallas kernels, body(): call(functools.partial(inner, ax), 'inner', 24, out_shape=[like(*shape) f...  10.1 us
    ppermute x5, starting transfers between devices, swaps(): got.append(lax.ppermute(message, axis, pairs + [(b, a) for a, b in pairs]))  8.33 us
    unnamed x18, local copies, waits for them, and re-layouts  5.54 us
    pallas_call x1, Pallas kernels, body(): call(functools.partial(pack_z, az), 'pack_z', 8, out_shape=(like(CHANNELS...  1.79 us
  transfers between devices with their start and end apart: 5, of which 4 were waited for; matrix products, arithmetic and copies ran while one was open for 0% of the time, Pallas kernels for 16%

profile of v3, /device:TPU:17, one launch (start us, length us, event | category | flops | bytes accessed | tf_op | source)
XLA Modules:
  0.0 63.6 jit_solution(5874863691679180092)
XLA Ops:
  0.6 0.0 copy-start
  0.6 1.1 %copy-done = f32[13,8,16,128]{3,2,1,0:T(8,128)S(1)} copy-done((f32[13,8,16,128]{3,2,1,0:T(8,128)S(1)}, f32[13,8,16,128]{3,2,1,0:T(8,128)}, u32[]{:S(2)}) %copy-start) | copy-done | bytes 851992
  1.8 0.0 copy-start.1
  1.8 0.9 %copy-done.1 = f32[3,8,16,128]{3,2,1,0:T(8,128)S(1)} copy-done((f32[3,8,16,128]{3,2,1,0:T(8,128)S(1)}, f32[3,8,16,128]{3,2,1,0:T(8,128)}, u32[]{:S(2)}) %copy-start.1) | copy-done | bytes 196632
  2.7 0.0 copy-start.2
  2.7 0.9 %copy-done.2 = f32[3,8,16,128]{3,2,1,0:T(8,128)S(1)} copy-done((f32[3,8,16,128]{3,2,1,0:T(8,128)S(1)}, f32[3,8,16,128]{3,2,1,0:T(8,128)}, u32[]{:S(2)}) %copy-start.2) | copy-done | bytes 196632
  3.6 0.0 copy-start.3
  3.6 0.8 %copy-done.3 = f32[8,16,128]{2,1,0:T(8,128)S(1)} copy-done((f32[8,16,128]{2,1,0:T(8,128)S(1)}, f32[8,16,128]{2,1,0:T(8,128)}, u32[]{:S(2)}) %copy-start.3) | copy-done | bytes 65560
  4.5 0.0 copy-start.4
  4.5 0.8 %copy-done.4 = s32[8,16,128]{2,1,0:T(8,128)S(1)} copy-done((s32[8,16,128]{2,1,0:T(8,128)S(1)}, s32[8,16,128]{2,1,0:T(8,128)}, u32[]{:S(2)}) %copy-start.4) | copy-done | bytes 65560
  5.3 0.0 copy-start.5
  5.3 0.8 %copy-done.5 = s32[8,16,128]{2,1,0:T(8,128)S(1)} copy-done((s32[8,16,128]{2,1,0:T(8,128)S(1)}, s32[8,16,128]{2,1,0:T(8,128)}, u32[]{:S(2)}) %copy-start.5) | copy-done | bytes 65560
  6.2 1.8 %pack_z.1 = (f32[22,8,16,128]{3,2,1,0:T(8,128)S(1)}, f32[11,16,128]{2,1,0:T(8,128)S(1)}, f32[11,16,128]{2,1,0:T(8,128)S(1)}) custom-call(f32[3,8,16,128]{3,2,1,0:T(8,128)S(1)} %copy-done.1, f32[3,8,16,128]{3,2,1,0:T(8,128)S(1)} %copy-done.2, f32[8,16,128]{2,1,0:T(8,128)S(1)} %copy-done.3, f32[13,8,16,128]{3,2,1,0:T(8,128)S(1)} %copy-done, ...), custom_call_target="tpu_custom_call" | custom-call | tf_op jit(solution)/shard_map/pack_z/pallas_call | solution.py:633
  8.0 0.7 %collective-permute-start = (f32[11,16,128]{2,1,0:T(8,128)S(1)}, f32[11,16,128]{2,1,0:T(8,128)S(1)}, u32[]{:S(2)}, u32[]{:S(2)}) collective-permute-start(f32[11,16,128]{2,1,0:T(8,128)S(1)} %get-tuple-element.19), channel_id=1, source_target_pairs={{0,1},{2,3},{1,0},{3,2},{4,5},{6,7},{5,4},{7,6},{8,9},{10,11},{9,8... | collective-permute-start | bytes 270344 | tf_op jit(solution)/shard_map/ppermute | solution.py:61
  8.7 3.0 %collective-permute-start.1 = (f32[11,16,128]{2,1,0:T(8,128)S(1)}, f32[11,16,128]{2,1,0:T(8,128)S(1)}, u32[]{:S(2)}, u32[]{:S(2)}) collective-permute-start(f32[11,16,128]{2,1,0:T(8,128)S(1)} %get-tuple-element.20), channel_id=1, source_target_pairs={{1,2},{2,1},{5,6},{6,5},{9,10},{10,9},{13,14},{14,13},{17,18},{18,... | collective-permute-start | bytes 270344 | tf_op jit(solution)/shard_map/ppermute | solution.py:61
  11.7 0.1 pack_x.1
  11.8 0.0 copy-start.6
  11.8 0.0 copy-start.7
  11.9 0.0 copy-start.8
  11.9 0.0 collective-permute-done.za
  11.9 2.9 %collective-permute-done.1.zb = f32[11,16,128]{2,1,0:T(8,128)S(1)} collective-permute-done((f32[11,16,128]{2,1,0:T(8,128)S(1)}, f32[11,16,128]{2,1,0:T(8,128)S(1)}, u32[]{:S(2)}, u32[]{:S(2)}) %collective-permute-start.1) | collective-permute-done | bytes 90144 | tf_op jit(solution)/shard_map/ppermute | solution.py:61
  14.8 0.3 join_x.1
  15.1 1.4 %collective-permute-start.2 = (f32[91,16,128]{2,1,0:T(8,128)S(1)}, f32[91,16,128]{2,1,0:T(8,128)S(1)}, u32[]{:S(2)}, u32[]{:S(2)}) collective-permute-start(f32[91,16,128]{2,1,0:T(8,128)S(1)} %get-tuple-element.23), channel_id=1, source_target_pairs={{0,8},{16,24},{8,0},{24,16},{1,9},{17,25},{9,1},{25,17},{2,10},{18... | collective-permute-start | bytes 2236424 | tf_op jit(solution)/shard_map/ppermute | solution.py:61
  16.5 1.9 %collective-permute-start.3 = (f32[91,16,128]{2,1,0:T(8,128)S(1)}, f32[91,16,128]{2,1,0:T(8,128)S(1)}, u32[]{:S(2)}, u32[]{:S(2)}) collective-permute-start(f32[91,16,128]{2,1,0:T(8,128)S(1)} %get-tuple-element.24), channel_id=1, source_target_pairs={{8,16},{16,8},{9,17},{17,9},{10,18},{18,10},{11,19},{19,11},{12,20... | collective-permute-start | bytes 2236424 | tf_op jit(solution)/shard_map/ppermute | solution.py:61
  18.4 0.1 pack_y.1.refs_0_
  18.5 10.7 %collective-permute-done.2.xa = f32[91,16,128]{2,1,0:T(8,128)S(1)} collective-permute-done((f32[91,16,128]{2,1,0:T(8,128)S(1)}, f32[91,16,128]{2,1,0:T(8,128)S(1)}, u32[]{:S(2)}, u32[]{:S(2)}) %collective-permute-start.2) | collective-permute-done | bytes 745504 | tf_op jit(solution)/shard_map/ppermute | solution.py:61
  29.2 3.5 %collective-permute-done.3.xb = f32[91,16,128]{2,1,0:T(8,128)S(1)} collective-permute-done((f32[91,16,128]{2,1,0:T(8,128)S(1)}, f32[91,16,128]{2,1,0:T(8,128)S(1)}, u32[]{:S(2)}, u32[]{:S(2)}) %collective-permute-start.3) | collective-permute-done | bytes 745504 | tf_op jit(solution)/shard_map/ppermute | solution.py:61
  32.6 0.6 join_y.1
  33.2 1.3 %collective-permute-start.4 = (f32[358,4,128]{2,1,0:T(4,128)S(1)}, f32[358,4,128]{2,1,0:T(4,128)S(1)}, u32[]{:S(2)}, u32[]{:S(2)}) collective-permute-start(f32[358,4,128]{2,1,0:T(4,128)S(1)} %get-tuple-element.26), channel_id=1, source_target_pairs={{0,4},{4,0},{1,5},{5,1},{2,6},{6,2},{3,7},{7,3},{8,12},{12,8},{9,1... | collective-permute-start | bytes 2199560 | tf_op jit(solution)/shard_map/ppermute | solution.py:61
  34.5 0.0 copy-done.6
  34.5 0.0 copy-done.7
  34.5 0.0 copy-done.8
  34.5 10.1 %inner.1 = (f32[26,16,16,128]{3,2,1,0:T(8,128)S(1)}, f32[16,16,128]{2,1,0:T(8,128)S(1)}, f32[16,16,128]{2,1,0:T(8,128)S(1)}, f32[26,1,16,128]{3,2,1,0:T(8,128)S(...) custom-call(f32[22,8,16,128]{3,2,1,0:T(8,128)S(1)} %get-tuple-element.18.local, ...), custom_call_target="tpu_custom_call" | custom-call | tf_op jit(solution)/shard_map/inner/pallas_call | solution.py:686
  44.6 3.8 %collective-permute-done.4.refs_3_ = f32[358,4,128]{2,1,0:T(4,128)S(1)} collective-permute-done((f32[358,4,128]{2,1,0:T(4,128)S(1)}, f32[358,4,128]{2,1,0:T(4,128)S(1)}, u32[]{:S(2)}, u32[]{:S(2)}) %collective-permute-start.4) | collective-permute-done | bytes 733216 | tf_op jit(solution)/shard_map/ppermute | solution.py:61
  48.4 15.1 %finish.1 = (f32[3,8,16,128]{3,2,1,0:T(8,128)}, f32[8,16,128]{2,1,0:T(8,128)}) custom-call(f32[22,8,16,128]{3,2,1,0:T(8,128)S(1)} %get-tuple-element.18.local, f32[22,16,128]{2,1,0:T(8,128)S(1)} %get-tuple-element.25.columns, f32[91,16,128]{2,1,0:T(8,128)S(1)} %collective-permute-done.2.xa, f32[91,16,128]{2,1,0:T(8,128)S(1)} %collective-permute-done.3.xb, ...), custom_call_target="tpu_custom_call" | custom-call | tf_op jit(solution)/shard_map/finish/pallas_call | solution.py:697
Async XLA Ops:
  0.6 1.2 %copy-start = (f32[13,8,16,128]{3,2,1,0:T(8,128)S(1)}, f32[13,8,16,128]{3,2,1,0:T(8,128)}, u32[]{:S(2)}) copy-start(f32[13,8,16,128]{3,2,1,0:T(8,128)} %refs_3_.1) | copy-start | bytes 2555908
  1.8 0.9 %copy-start.1 = (f32[3,8,16,128]{3,2,1,0:T(8,128)S(1)}, f32[3,8,16,128]{3,2,1,0:T(8,128)}, u32[]{:S(2)}) copy-start(f32[3,8,16,128]{3,2,1,0:T(8,128)} %refs_0_.3) | copy-start | bytes 589828
  2.7 0.9 %copy-start.2 = (f32[3,8,16,128]{3,2,1,0:T(8,128)S(1)}, f32[3,8,16,128]{3,2,1,0:T(8,128)}, u32[]{:S(2)}) copy-start(f32[3,8,16,128]{3,2,1,0:T(8,128)} %refs_1_.3) | copy-start | bytes 589828
  3.6 0.8 %copy-start.3 = (f32[8,16,128]{2,1,0:T(8,128)S(1)}, f32[8,16,128]{2,1,0:T(8,128)}, u32[]{:S(2)}) copy-start(f32[8,16,128]{2,1,0:T(8,128)} %refs_2_.3) | copy-start | bytes 196612
  4.5 0.8 %copy-start.4 = (s32[8,16,128]{2,1,0:T(8,128)S(1)}, s32[8,16,128]{2,1,0:T(8,128)}, u32[]{:S(2)}) copy-start(s32[8,16,128]{2,1,0:T(8,128)} %refs_4_.1) | copy-start | bytes 196612
  5.3 0.8 %copy-start.5 = (s32[8,16,128]{2,1,0:T(8,128)S(1)}, s32[8,16,128]{2,1,0:T(8,128)}, u32[]{:S(2)}) copy-start(s32[8,16,128]{2,1,0:T(8,128)} %refs_5_.1) | copy-start | bytes 196612
  8.0 3.9 %collective-permute-start = (f32[11,16,128]{2,1,0:T(8,128)S(1)}, f32[11,16,128]{2,1,0:T(8,128)S(1)}, u32[]{:S(2)}, u32[]{:S(2)}) collective-permute-start(f32[11,16,128]{2,1,0:T(8,128)S(1)} %get-tuple-element.19), channel_id=1, source_target_pairs={{0,1},{2,3},{1,0},{3,2},{4,5},{6,7},{5,4},{7,6},{8,9},{10,11},{9,8... | collective-permute-start | bytes 270344 | tf_op jit(solution)/shard_map/ppermute | solution.py:61
  8.7 6.1 %collective-permute-start.1 = (f32[11,16,128]{2,1,0:T(8,128)S(1)}, f32[11,16,128]{2,1,0:T(8,128)S(1)}, u32[]{:S(2)}, u32[]{:S(2)}) collective-permute-start(f32[11,16,128]{2,1,0:T(8,128)S(1)} %get-tuple-element.20), channel_id=1, source_target_pairs={{1,2},{2,1},{5,6},{6,5},{9,10},{10,9},{13,14},{14,13},{17,18},{18,... | collective-permute-start | bytes 270344 | tf_op jit(solution)/shard_map/ppermute | solution.py:61
  11.8 22.7 %copy-start.6 = (f32[3,8]{1,0:T(4,128)S(1)}, f32[3,8]{1,0:T(4,128)}, u32[]{:S(2)}) copy-start(f32[3,8]{1,0:T(4,128)} %refs_0_.5) | copy-start | bytes 292
  11.8 22.7 %copy-start.7 = (f32[3,8]{1,0:T(4,128)S(1)}, f32[3,8]{1,0:T(4,128)}, u32[]{:S(2)}) copy-start(f32[3,8]{1,0:T(4,128)} %refs_1_.5) | copy-start | bytes 292
  11.9 22.7 %copy-start.8 = (f32[3,8]{1,0:T(4,128)S(1)}, f32[3,8]{1,0:T(4,128)}, u32[]{:S(2)}) copy-start(f32[3,8]{1,0:T(4,128)} %refs_2_.5) | copy-start | bytes 292
  15.1 14.1 %collective-permute-start.2 = (f32[91,16,128]{2,1,0:T(8,128)S(1)}, f32[91,16,128]{2,1,0:T(8,128)S(1)}, u32[]{:S(2)}, u32[]{:S(2)}) collective-permute-start(f32[91,16,128]{2,1,0:T(8,128)S(1)} %get-tuple-element.23), channel_id=1, source_target_pairs={{0,8},{16,24},{8,0},{24,16},{1,9},{17,25},{9,1},{25,17},{2,10},{18... | collective-permute-start | bytes 2236424 | tf_op jit(solution)/shard_map/ppermute | solution.py:61
  16.5 16.2 %collective-permute-start.3 = (f32[91,16,128]{2,1,0:T(8,128)S(1)}, f32[91,16,128]{2,1,0:T(8,128)S(1)}, u32[]{:S(2)}, u32[]{:S(2)}) collective-permute-start(f32[91,16,128]{2,1,0:T(8,128)S(1)} %get-tuple-element.24), channel_id=1, source_target_pairs={{8,16},{16,8},{9,17},{17,9},{10,18},{18,10},{11,19},{19,11},{12,20... | collective-permute-start | bytes 2236424 | tf_op jit(solution)/shard_map/ppermute | solution.py:61
  33.2 15.2 %collective-permute-start.4 = (f32[358,4,128]{2,1,0:T(4,128)S(1)}, f32[358,4,128]{2,1,0:T(4,128)S(1)}, u32[]{:S(2)}, u32[]{:S(2)}) collective-permute-start(f32[358,4,128]{2,1,0:T(4,128)S(1)} %get-tuple-element.26), channel_id=1, source_target_pairs={{0,4},{4,0},{1,5},{5,1},{2,6},{6,2},{3,7},{7,3},{8,12},{12,8},{9,1... | collective-permute-start | bytes 2199560 | tf_op jit(solution)/shard_map/ppermute | solution.py:61

commit v4 on v3

--- a/solution.py
+++ b/solution.py
@@ -403,8 +403,8 @@
     refs = refs[12 + count_y :]
     tabs, raw, edge_store = refs[:3]
     edge_results, edge_halo_results = refs[3:6], refs[6:9]
-    sol, halo_sol, edge_sol, edge_halo_sol = refs[9:13]
-    arrays, halo = refs[13:19], refs[19:]
+    sols, halo_sols, edge_sols, edge_halo_sols = (refs[9 + 2 * i : 11 + 2 * i] for i in range(4))
+    arrays, halo = refs[17:23], refs[23:]
     planes, rows, depth = local.shape[1:]
     total = planes + 2 * W
     even_x, even_y, _ = (parity_of(axis) for axis in axes)
@@ -454,7 +454,7 @@
 
     cells(total, True)
 
-    @pl.loop(0, total)
+    @pl.loop(0, total, unroll=2)
     def _(plane):
         cells(plane)
 
@@ -482,20 +482,22 @@
         return mains[:-1] + [jnp.where(row == 7, last, mains[-1])]
 
     def put_parts(is_columns, slot, step, plane, mains, edge):
-        to, edge_to = (halo_sol, edge_halo_sol) if is_columns else (sol, edge_sol)
+        to, edge_to = (
+            (halo_sols[slot], edge_halo_sols[slot]) if is_columns else (sols[slot], edge_sols[slot])
+        )
         for tile, values in enumerate(mains):
-            to[slot, step + 1, plane, 8 + 8 * tile : 16 + 8 * tile, :] = values
-        edge_to[slot, step + 1, plane, 2:10, :] = edge
-        to[slot, step + 1, plane, 7:8, :] = edge[5:6]
-        to[slot, step + 1, plane, 8 + rows : 9 + rows, :] = edge[2:3]
-        edge_to[slot, step + 1, plane, 0:1, :] = mains[-1][6:7]
-        edge_to[slot, step + 1, plane, RING - 1 : RING, :] = mains[0][1:2]
+            to[step + 1, plane, 8 + 8 * tile : 16 + 8 * tile, :] = values
+        edge_to[step + 1, plane, 2:10, :] = edge
+        to[step + 1, plane, 7:8, :] = edge[5:6]
+        to[step + 1, plane, 8 + rows : 9 + rows, :] = edge[2:3]
+        edge_to[step + 1, plane, 0:1, :] = mains[-1][6:7]
+        edge_to[step + 1, plane, RING - 1 : RING, :] = mains[0][1:2]
 
     def halo_parts(slot, step):
         mains = [
-            halo_sol[slot, step + 1, 0, 8 + 8 * tile : 16 + 8 * tile, :] for tile in range(tiles)
+            halo_sols[slot][step + 1, 0, 8 + 8 * tile : 16 + 8 * tile, :] for tile in range(tiles)
         ]
-        return mains, edge_halo_sol[slot, step + 1, 0, 2:10, :]
+        return mains, edge_halo_sols[slot][step + 1, 0, 2:10, :]
 
     def put_solution(slot, plane, mains, edge, is_columns=False):
         mains = merged(mains, edge)
@@ -516,16 +518,18 @@
 
     def relaxed(slot, plane, tile, is_columns=False):
         if tile is None:
-            ref, first, stride, out = (edge_halo_sol if is_columns else edge_sol), 2, 2, slice(0, 8)
+            ref = (edge_halo_sols if is_columns else edge_sols)[slot]
+            first, stride, out = 2, 2, slice(0, 8)
             coupling, scale, start = edge_halo_results if is_columns else edge_results
         else:
-            ref, first, stride = (halo_sol if is_columns else sol), 8 + 8 * tile, 1
+            ref = (halo_sols if is_columns else sols)[slot]
+            first, stride = 8 + 8 * tile, 1
             out = slice(8 * tile, 8 * tile + 8)
             coupling, scale, start = halo_results if is_columns else results
 
         def get(offset):
             dx = 0 if is_columns else offset[0]
-            values = ref[slot, offset[2] + 1, plane + dx, pl.ds(first + stride * offset[1], 8), :]
+            values = ref[offset[2] + 1, plane + dx, pl.ds(first + stride * offset[1], 8), :]
             return x_roll(values, offset[0], is_columns)
 
         parts = [jnp.zeros((8, depth), f32) for _ in range(2)]
@@ -545,7 +549,7 @@
 
     first_sweep(0, True)
 
-    @pl.loop(1, total - 1)
+    @pl.loop(1, total - 1, unroll=2)
     def _(plane):
         first_sweep(plane)
 
@@ -557,11 +561,11 @@
         slot = sweep % 2
         sweep_of(slot, 0, True)
 
-        @pl.loop(sweep, total - sweep)
+        @pl.loop(sweep, total - sweep, unroll=2)
         def _(plane):
             sweep_of(slot, plane)
 
-    @pl.loop(0, planes)
+    @pl.loop(0, planes, unroll=2)
     def _(x):
         slot, plane = SWEEPS % 2, W + x
         edge = relaxed(slot, plane, None)
@@ -629,6 +633,7 @@
     like = lambda *shape: jax.ShapeDtypeStruct(shape, f32)
     fill = lambda shape, got: [jnp.zeros(shape.shape, f32) if one is None else one for one in got]
 
+    arguments = (cell_state, old_mass, pore_volume, transmissibility, active_mask, pvt_region)
     z_shape = like(groups, rows, depth)
     local, *z_send = call(
         functools.partial(pack_z, az),
@@ -641,7 +646,7 @@
             pltpu.VMEM((2, planes, rows, depth), jnp.int32),
             pltpu.SemaphoreType.DMA((7,)),
         ],
-    )(cell_state, old_mass, pore_volume, transmissibility, active_mask, pvt_region)
+    )(*(pltpu.with_memory_space_constraint(array, pltpu.MemorySpace.HBM) for array in arguments))
     za, zb = fill(z_shape, swaps(az, *z_send))
 
     x_shape = like(XMAIN + groups, rows, depth)
@@ -706,10 +711,10 @@
             pltpu.VMEM((CHANNELS, total + 1, 16, depth), f32),
             pltpu.VMEM((3, total, 8, depth), f32),
             *(pltpu.VMEM(shape, f32) for shape in result_shapes(total, 8, depth)),
-            pltpu.VMEM((2, 3, total, rows + 16, depth), f32),
-            pltpu.VMEM((2, 3, 1, rows + 16, depth), f32),
-            pltpu.VMEM((2, 3, total, 16, depth), f32),
-            pltpu.VMEM((2, 3, 1, 16, depth), f32),
+            *[pltpu.VMEM((3, total, rows + 16, depth), f32)] * 2,
+            *[pltpu.VMEM((3, 1, rows + 16, depth), f32)] * 2,
+            *[pltpu.VMEM((3, total, 16, depth), f32)] * 2,
+            *[pltpu.VMEM((3, 1, 16, depth), f32)] * 2,
         ]
         + cell_arrays(total, 16, depth),
     )(local, columns, xa, xb, *tables, *ys, *halves)

time: 63.9 us -> 56.8 us (0.89)
  local copies, waits for them, and re-layouts: 5.54 us -> 0.02 us
  Pallas kernels: 28.1 us -> 26.6 us
    unnamed x18 -> x6, local copies, waits for them, and re-layouts: 5.54 us -> 0.02 us
    pallas_call x1, Pallas kernels: 15.1 us -> 13.3 us  [body(): call(functools.partial(finish, (ax, ay, az), count_y), 'finish', 24, out_...]
  transfers between devices with their start and end apart: 5 -> 5, of which waited for: 4 -> 4; matrix products, arithmetic and copies ran while one was open for 0% -> 0% of each run, Pallas kernels for 16% -> 18%
where the time goes in v4:
time: 56.8 us; the launch traced here: 56.6 us
  Pallas kernels  26.6 us (47%)
  waiting for transfers between devices  20.9 us (37%)
  starting transfers between devices  8.33 us (15%)
  between operations  0.73 us (1%)
    ppermute x5, waiting for transfers between devices, swaps(): got.append(lax.ppermute(message, axis, pairs + [(b, a) for a, b in pairs]))  20.9 us
    pallas_call x1, Pallas kernels, body(): call(functools.partial(finish, (ax, ay, az), count_y), 'finish', 24, out_...  13.3 us
    pallas_call x1, Pallas kernels, body(): call(functools.partial(inner, ax), 'inner', 24, out_shape=[like(*shape) f...  10.1 us
    ppermute x5, starting transfers between devices, swaps(): got.append(lax.ppermute(message, axis, pairs + [(b, a) for a, b in pairs]))  8.33 us
    pallas_call x1, Pallas kernels, body(): call(functools.partial(pack_z, az), 'pack_z', 8, out_shape=(like(CHANNELS...  2.26 us
  transfers between devices with their start and end apart: 5, of which 4 were waited for; matrix products, arithmetic and copies ran while one was open for 0% of the time, Pallas kernels for 18%

profile of v4, /device:TPU:17, one launch (start us, length us, event | category | flops | bytes accessed | tf_op | source)
XLA Modules:
  0.0 56.6 jit_solution(13098159634050453845)
XLA Ops:
  0.6 2.3 %pack_z.1 = (f32[22,8,16,128]{3,2,1,0:T(8,128)S(1)}, f32[11,16,128]{2,1,0:T(8,128)S(1)}, f32[11,16,128]{2,1,0:T(8,128)S(1)}) custom-call(f32[3,8,16,128]{3,2,1,0:T(8,128)} %refs_0_.3, f32[3,8,16,128]{3,2,1,0:T(8,128)} %refs_1_.3, f32[8,16,128]{2,1,0:T(8,128)} %refs_2_.3, f32[13,8,16,128]{3,2,1,0:T(8,128)} %refs_3_.1, s32[8,16,128]{2,1,0:T(8,128)} %refs_4_.1, ...), custom_call_target="tpu_custom_call" | custom-call | tf_op jit(solution)/shard_map/pack_z/pallas_call | solution.py:638
  2.9 0.7 %collective-permute-start = (f32[11,16,128]{2,1,0:T(8,128)S(1)}, f32[11,16,128]{2,1,0:T(8,128)S(1)}, u32[]{:S(2)}, u32[]{:S(2)}) collective-permute-start(f32[11,16,128]{2,1,0:T(8,128)S(1)} %get-tuple-element.19), channel_id=1, source_target_pairs={{0,1},{2,3},{1,0},{3,2},{4,5},{6,7},{5,4},{7,6},{8,9},{10,11},{9,8... | collective-permute-start | bytes 270344 | tf_op jit(solution)/shard_map/ppermute | solution.py:61
  3.6 3.0 %collective-permute-start.1 = (f32[11,16,128]{2,1,0:T(8,128)S(1)}, f32[11,16,128]{2,1,0:T(8,128)S(1)}, u32[]{:S(2)}, u32[]{:S(2)}) collective-permute-start(f32[11,16,128]{2,1,0:T(8,128)S(1)} %get-tuple-element.20), channel_id=1, source_target_pairs={{1,2},{2,1},{5,6},{6,5},{9,10},{10,9},{13,14},{14,13},{17,18},{18,... | collective-permute-start | bytes 270344 | tf_op jit(solution)/shard_map/ppermute | solution.py:61
  6.7 0.1 pack_x.1
  6.8 0.0 copy-start
  6.8 0.0 copy-start.1
  6.8 0.0 copy-start.2
  6.8 0.0 collective-permute-done.za
  6.8 2.9 %collective-permute-done.1.zb = f32[11,16,128]{2,1,0:T(8,128)S(1)} collective-permute-done((f32[11,16,128]{2,1,0:T(8,128)S(1)}, f32[11,16,128]{2,1,0:T(8,128)S(1)}, u32[]{:S(2)}, u32[]{:S(2)}) %collective-permute-start.1) | collective-permute-done | bytes 90144 | tf_op jit(solution)/shard_map/ppermute | solution.py:61
  9.8 0.3 join_x.1
  10.0 1.4 %collective-permute-start.2 = (f32[91,16,128]{2,1,0:T(8,128)S(1)}, f32[91,16,128]{2,1,0:T(8,128)S(1)}, u32[]{:S(2)}, u32[]{:S(2)}) collective-permute-start(f32[91,16,128]{2,1,0:T(8,128)S(1)} %get-tuple-element.23), channel_id=1, source_target_pairs={{0,8},{16,24},{8,0},{24,16},{1,9},{17,25},{9,1},{25,17},{2,10},{18... | collective-permute-start | bytes 2236424 | tf_op jit(solution)/shard_map/ppermute | solution.py:61
  11.4 1.9 %collective-permute-start.3 = (f32[91,16,128]{2,1,0:T(8,128)S(1)}, f32[91,16,128]{2,1,0:T(8,128)S(1)}, u32[]{:S(2)}, u32[]{:S(2)}) collective-permute-start(f32[91,16,128]{2,1,0:T(8,128)S(1)} %get-tuple-element.24), channel_id=1, source_target_pairs={{8,16},{16,8},{9,17},{17,9},{10,18},{18,10},{11,19},{19,11},{12,20... | collective-permute-start | bytes 2236424 | tf_op jit(solution)/shard_map/ppermute | solution.py:61
  13.3 0.1 pack_y.1.refs_0_
  13.4 10.7 %collective-permute-done.2.xa = f32[91,16,128]{2,1,0:T(8,128)S(1)} collective-permute-done((f32[91,16,128]{2,1,0:T(8,128)S(1)}, f32[91,16,128]{2,1,0:T(8,128)S(1)}, u32[]{:S(2)}, u32[]{:S(2)}) %collective-permute-start.2) | collective-permute-done | bytes 745504 | tf_op jit(solution)/shard_map/ppermute | solution.py:61
  24.1 3.5 %collective-permute-done.3.xb = f32[91,16,128]{2,1,0:T(8,128)S(1)} collective-permute-done((f32[91,16,128]{2,1,0:T(8,128)S(1)}, f32[91,16,128]{2,1,0:T(8,128)S(1)}, u32[]{:S(2)}, u32[]{:S(2)}) %collective-permute-start.3) | collective-permute-done | bytes 745504 | tf_op jit(solution)/shard_map/ppermute | solution.py:61
  27.6 0.6 join_y.1
  28.1 1.3 %collective-permute-start.4 = (f32[358,4,128]{2,1,0:T(4,128)S(1)}, f32[358,4,128]{2,1,0:T(4,128)S(1)}, u32[]{:S(2)}, u32[]{:S(2)}) collective-permute-start(f32[358,4,128]{2,1,0:T(4,128)S(1)} %get-tuple-element.26), channel_id=1, source_target_pairs={{0,4},{4,0},{1,5},{5,1},{2,6},{6,2},{3,7},{7,3},{8,12},{12,8},{9,1... | collective-permute-start | bytes 2199560 | tf_op jit(solution)/shard_map/ppermute | solution.py:61
  29.5 0.0 copy-done
  29.5 0.0 copy-done.1
  29.5 0.0 copy-done.2
  29.5 10.1 %inner.1 = (f32[26,16,16,128]{3,2,1,0:T(8,128)S(1)}, f32[16,16,128]{2,1,0:T(8,128)S(1)}, f32[16,16,128]{2,1,0:T(8,128)S(1)}, f32[26,1,16,128]{3,2,1,0:T(8,128)S(...) custom-call(f32[22,8,16,128]{3,2,1,0:T(8,128)S(1)} %get-tuple-element.18.local, ...), custom_call_target="tpu_custom_call" | custom-call | tf_op jit(solution)/shard_map/inner/pallas_call | solution.py:691
  39.6 3.8 %collective-permute-done.4.refs_3_ = f32[358,4,128]{2,1,0:T(4,128)S(1)} collective-permute-done((f32[358,4,128]{2,1,0:T(4,128)S(1)}, f32[358,4,128]{2,1,0:T(4,128)S(1)}, u32[]{:S(2)}, u32[]{:S(2)}) %collective-permute-start.4) | collective-permute-done | bytes 733216 | tf_op jit(solution)/shard_map/ppermute | solution.py:61
  43.4 13.3 %finish.1 = (f32[3,8,16,128]{3,2,1,0:T(8,128)}, f32[8,16,128]{2,1,0:T(8,128)}) custom-call(f32[22,8,16,128]{3,2,1,0:T(8,128)S(1)} %get-tuple-element.18.local, f32[22,16,128]{2,1,0:T(8,128)S(1)} %get-tuple-element.25.columns, f32[91,16,128]{2,1,0:T(8,128)S(1)} %collective-permute-done.2.xa, f32[91,16,128]{2,1,0:T(8,128)S(1)} %collective-permute-done.3.xb, ...), custom_call_target="tpu_custom_call" | custom-call | tf_op jit(solution)/shard_map/finish/pallas_call | solution.py:702
Async XLA Ops:
  2.9 3.9 %collective-permute-start = (f32[11,16,128]{2,1,0:T(8,128)S(1)}, f32[11,16,128]{2,1,0:T(8,128)S(1)}, u32[]{:S(2)}, u32[]{:S(2)}) collective-permute-start(f32[11,16,128]{2,1,0:T(8,128)S(1)} %get-tuple-element.19), channel_id=1, source_target_pairs={{0,1},{2,3},{1,0},{3,2},{4,5},{6,7},{5,4},{7,6},{8,9},{10,11},{9,8... | collective-permute-start | bytes 270344 | tf_op jit(solution)/shard_map/ppermute | solution.py:61
  3.6 6.1 %collective-permute-start.1 = (f32[11,16,128]{2,1,0:T(8,128)S(1)}, f32[11,16,128]{2,1,0:T(8,128)S(1)}, u32[]{:S(2)}, u32[]{:S(2)}) collective-permute-start(f32[11,16,128]{2,1,0:T(8,128)S(1)} %get-tuple-element.20), channel_id=1, source_target_pairs={{1,2},{2,1},{5,6},{6,5},{9,10},{10,9},{13,14},{14,13},{17,18},{18,... | collective-permute-start | bytes 270344 | tf_op jit(solution)/shard_map/ppermute | solution.py:61
  6.8 22.7 %copy-start = (f32[3,8]{1,0:T(4,128)S(1)}, f32[3,8]{1,0:T(4,128)}, u32[]{:S(2)}) copy-start(f32[3,8]{1,0:T(4,128)} %refs_0_.5) | copy-start | bytes 292
  6.8 22.7 %copy-start.1 = (f32[3,8]{1,0:T(4,128)S(1)}, f32[3,8]{1,0:T(4,128)}, u32[]{:S(2)}) copy-start(f32[3,8]{1,0:T(4,128)} %refs_1_.5) | copy-start | bytes 292
  6.8 22.7 %copy-start.2 = (f32[3,8]{1,0:T(4,128)S(1)}, f32[3,8]{1,0:T(4,128)}, u32[]{:S(2)}) copy-start(f32[3,8]{1,0:T(4,128)} %refs_2_.5) | copy-start | bytes 292
  10.0 14.1 %collective-permute-start.2 = (f32[91,16,128]{2,1,0:T(8,128)S(1)}, f32[91,16,128]{2,1,0:T(8,128)S(1)}, u32[]{:S(2)}, u32[]{:S(2)}) collective-permute-start(f32[91,16,128]{2,1,0:T(8,128)S(1)} %get-tuple-element.23), channel_id=1, source_target_pairs={{0,8},{16,24},{8,0},{24,16},{1,9},{17,25},{9,1},{25,17},{2,10},{18... | collective-permute-start | bytes 2236424 | tf_op jit(solution)/shard_map/ppermute | solution.py:61
  11.4 16.2 %collective-permute-start.3 = (f32[91,16,128]{2,1,0:T(8,128)S(1)}, f32[91,16,128]{2,1,0:T(8,128)S(1)}, u32[]{:S(2)}, u32[]{:S(2)}) collective-permute-start(f32[91,16,128]{2,1,0:T(8,128)S(1)} %get-tuple-element.24), channel_id=1, source_target_pairs={{8,16},{16,8},{9,17},{17,9},{10,18},{18,10},{11,19},{19,11},{12,20... | collective-permute-start | bytes 2236424 | tf_op jit(solution)/shard_map/ppermute | solution.py:61
  28.1 15.2 %collective-permute-start.4 = (f32[358,4,128]{2,1,0:T(4,128)S(1)}, f32[358,4,128]{2,1,0:T(4,128)S(1)}, u32[]{:S(2)}, u32[]{:S(2)}) collective-permute-start(f32[358,4,128]{2,1,0:T(4,128)S(1)} %get-tuple-element.26), channel_id=1, source_target_pairs={{0,4},{4,0},{1,5},{5,1},{2,6},{6,2},{3,7},{7,3},{8,12},{12,8},{9,1... | collective-permute-start | bytes 2199560 | tf_op jit(solution)/shard_map/ppermute | solution.py:61

commit v5 on v4

--- a/solution.py
+++ b/solution.py
@@ -1,4 +1,5 @@
 import functools
+import itertools
 
 import jax
 import jax.numpy as jnp
@@ -24,7 +25,8 @@
 STEP = UP - FLAT
 
 FAR = 5 + STEP
-CHANNELS = FAR + FLAT + 4
+CHANNELS = FAR + FLAT + 2
+STORAGE, OWN = FAR + FLAT, FAR + FLAT + 1
 NEAR = W - 1
 XMAIN = CHANNELS * NEAR + FAR
 VMEM = pl.BlockSpec(memory_space=pltpu.VMEM)
@@ -75,24 +77,62 @@
     return per, -(-CHANNELS // per)
 
 
+def lookups(tabs, region, numbers):
+    index = region.astype(jnp.int32)
+    return [
+        jnp.take_along_axis(tabs[n], index, axis=1, mode="promise_in_bounds") for n in numbers
+    ]
+
+
 def pack_z(axis, *refs):
-    state, mass, pore, trans, active, region, local, first, second, flags, sems = refs
+    state, mass, pore, trans, active, region, *tables = refs[:9]
+    local, accum, tabs, first, second = refs[9:14]
+    flags, masses, pores, small, sems = refs[14:]
     planes, rows, depth = pore.shape
     copies = [
         pltpu.make_async_copy(active, flags.at[0], sems.at[0]),
         pltpu.make_async_copy(region, flags.at[1], sems.at[1]),
         pltpu.make_async_copy(state, local.at[0:3], sems.at[2]),
-        pltpu.make_async_copy(trans.at[FLAT:UP], local.at[5:FAR], sems.at[3]),
-        pltpu.make_async_copy(trans.at[0:FLAT], local.at[FAR : FAR + FLAT], sems.at[4]),
-        pltpu.make_async_copy(mass, local.at[FAR + FLAT : CHANNELS - 1], sems.at[5]),
-        pltpu.make_async_copy(pore, local.at[CHANNELS - 1], sems.at[6]),
+        pltpu.make_async_copy(mass, masses, sems.at[3]),
+        pltpu.make_async_copy(pore, pores, sems.at[4]),
     ]
+    copies += [
+        pltpu.make_async_copy(table, small.at[n], sems.at[5 + n]) for n, table in enumerate(tables)
+    ]
+    late = [
+        pltpu.make_async_copy(trans.at[FLAT:UP], local.at[5:FAR], sems.at[8]),
+        pltpu.make_async_copy(trans.at[0:FLAT], local.at[FAR : FAR + FLAT], sems.at[9]),
+    ]
+    for copy in copies + late:
+        copy.start()
     for copy in copies:
-        copy.start()
-    copies[0].wait()
-    copies[1].wait()
-    local[3:5] = flags[...].astype(f32)
-    for copy in copies[2:]:
+        copy.wait()
+    regions = tables[0].shape[1]
+    for n in range(3):
+        for c in range(3):
+            tabs[3 * n + c, :, 0:regions] = jnp.broadcast_to(small[n, c : c + 1, :], (8, regions))
+    for x in range(planes):
+        for tile in range(rows // 8):
+            span = slice(8 * tile, 8 * tile + 8)
+            on = flags[0, x, span, :].astype(f32)
+            level = flags[1, x, span, :]
+            local[3, x, span, :] = on
+            local[4, x, span, :] = level.astype(f32)
+            press, water, gas = (local[c, x, span, :] for c in range(3))
+            look = lookups(tabs, level, range(6))
+            sat = (water, 1.0 - water - gas, gas)
+            expand = [look[c] * jnp.exp(look[3 + c] * (press - 0.5)) for c in range(3)]
+            volume = pores[x, span, :]
+            stored = volume * (look[3] * sat[0] + look[4] * sat[1] + look[5] * sat[2])
+            stored = jnp.where(on > 0, stored, 1.0)
+            own = jnp.zeros((8, depth), f32)
+            for c in range(3):
+                value = volume * expand[c] * sat[c] - masses[c, x, span, :]
+                accum[c, x, span, :] = value
+                own = own + value / (expand[c] * stored)
+            local[STORAGE, x, span, :] = stored
+            local[OWN, x, span, :] = on * own
+    for copy in late:
         copy.wait()
 
     per, groups = groups_of(planes, depth)
@@ -130,10 +170,25 @@
                 out[CHANNELS * NEAR + c] = local[c, far]
 
 
-def join_x(za, zb, a_in, b_in, a_out, b_out, columns, sems):
-    columns[...] = za[...] + zb[...]
+def join_x(axis, planes, za, zb, a_in, b_in, a_out, b_out, columns, sems):
+    rows, depth = za.shape[1:]
+    even = parity_of(axis)
+    per, _ = groups_of(planes, depth)
+    per_x, groups_x = groups_of(W, depth)
+    lane = lanes_of((rows, depth))
+    for group in range(groups_x):
+        sides = [jnp.zeros((rows, depth), f32) for _ in range(2)]
+        for c in range(group * per_x, min(CHANNELS, group * per_x + per_x)):
+            values = za[c // per] + zb[c // per]
+            to = (c % per_x) * span_of(W)
+            here = (lane >= to) & (lane < to + span_of(W))
+            for n, plane in enumerate((planes - W, 0)):
+                source = (c % per) * span_of(planes) + 2 * W * plane
+                sides[n] = jnp.where(here, pltpu.roll(values, (to - source) % depth, 1), sides[n])
+        columns[0, group] = pick(even, *sides)
+        columns[1, group] = pick(even, *sides[::-1])
     copies = [
-        pltpu.make_async_copy(columns, out.at[pl.ds(XMAIN, columns.shape[0])], sems.at[n])
+        pltpu.make_async_copy(columns.at[n], out.at[pl.ds(XMAIN, groups_x)], sems.at[n])
         for n, out in enumerate((a_out, b_out))
     ]
     for copy in copies:
@@ -163,21 +218,23 @@
     even = parity_of(axis)
     even_x = parity_of(x_axis)
     per, _ = groups_of(planes, depth)
+    per_x, _ = groups_of(W, depth)
     lane = lanes_of((rows, depth))
     for c in range(CHANNELS):
         group, base = c // per, (c % per) * span_of(planes)
+        own = pltpu.roll(za[group] + zb[group], (2 * W * W - base) % depth, 1)
+        group, base = c // per_x, (c % per_x) * span_of(W)
         a, b = xa[XMAIN + group], xb[XMAIN + group]
-        own = pltpu.roll(za[group] + zb[group], (2 * W * W - base) % depth, 1)
-        below = pltpu.roll(pick(even_x, b, a), (depth - base - 2 * W * (planes - W)) % depth, 1)
+        below = pltpu.roll(pick(even_x, b, a), (depth - base) % depth, 1)
         above = pltpu.roll(pick(even_x, a, b), (2 * W * (planes + W) - base) % depth, 1)
         values = jnp.where(lane < 2 * W * W, below, jnp.where(lane < 2 * W * (W + planes), own, above))
         columns[c] = values
         put_rows(stages, 2 * XMAIN + c, values, even)
 
-    @pl.loop(0, XMAIN // 4)
+    @pl.loop(0, XMAIN // 2)
     def _(i):
-        for j in range(4):
-            n = 4 * i + j
+        for j in range(2):
+            n = 2 * i + j
             a, b = xa[n], xb[n]
             put_rows(stages, n, pick(even_x, b, a), even)
             put_rows(stages, XMAIN + n, pick(even_x, a, b), even)
@@ -221,60 +278,40 @@
     return jnp.where(lane == at, pltpu.roll(values, at + 1, 1), current)
 
 
-def fill_tables(tables, tabs):
-    lane = lanes_of(tabs.shape[1:])
-    for n, table in enumerate(tables):
-        for c in range(3):
-            values = jnp.full(tabs.shape[1:], table[c, 0], f32)
-            for level in range(1, table.shape[1]):
-                values = jnp.where(lane == level, table[c, level], values)
-            tabs[3 * n + c] = values
-
-
-def properties(get, plane, is_columns, first, tabs, arrays, halo):
-    fields, lower, half, weight, accum, _ = halo if is_columns else arrays
-    halo_fields, halo_lower, centre = halo[0], halo[1], halo[5]
-    span = pl.ds(first, 8)
+def properties(get, plane, is_columns, put, tabs, arrays, halo, centre, span):
+    fields, lower, half, weight, base = halo if is_columns else arrays
+    halo_fields, halo_lower = halo[:2]
     press, water, gas, active, region = (get(c) for c in range(5))
-    index = region.astype(jnp.int32)
-    look = [
-        jnp.take_along_axis(tabs[n], index, axis=1, mode="promise_in_bounds") for n in range(9)
-    ]
+    look = lookups(tabs, region, range(9))
     formation, compress, viscous = look[:3], look[3:6], look[6:]
     sat = (water, 1.0 - water - gas, gas)
     expand = [formation[c] * jnp.exp(compress[c] * (press - 0.5)) for c in range(3)]
     mob = [viscous[c] * expand[c] * sat[c] * sat[c] for c in range(3)]
-    pore = get(CHANNELS - 1)
-    stored = pore * (compress[0] * sat[0] + compress[1] * sat[1] + compress[2] * sat[2])
-    stored = jnp.where(active > 0, stored, 1.0)
+    stored = get(STORAGE)
+    stored = jnp.where(stored > 0, stored, 1.0)
     for c in range(3):
-        weight[c, plane, span, :] = active / (expand[c] * stored)
-        accum[c, plane, span, :] = pore * expand[c] * sat[c] - get(FAR + FLAT + c)
+        put(weight, (c, plane), active / (expand[c] * stored))
+    put(base, (plane,), get(OWN))
+    shifts = []
     one = [press] + mob + [compress[c] * mob[c] for c in range(3)] + [active]
     for f, values in enumerate(one):
-        fields[f, 1, plane, span, :] = values
-        for step in (-1, 1):
-            if is_columns:
-                fields[f, step + 1, plane, span, :] = z_shift_columns(values, step)
-            else:
-                columns = halo_fields[f, 1, 0, span, :]
-                fields[f, step + 1, plane, span, :] = z_shift(values, columns, plane, step)
-                current = halo_fields[f, step + 1, 0, span, :]
-                halo_fields[f, step + 1, 0, span, :] = z_edge(current, values, plane, step)
+        put(fields, (f, 1, plane), values)
+        shifts += [(0, (f, step + 1), step, values, f) for step in (-1, 1)]
     for k, offset in enumerate(upper_offsets):
         values = 0.5 * get(t_channel(k))
-        half[k, plane, span, :] = values
+        put(half, (k, plane), values)
         values = values * active
-        step = -offset[2]
-        if step == 0:
-            lower[k, plane, span, :] = values
-        elif is_columns:
-            centre[k, span, :] = values
-            lower[k, plane, span, :] = z_shift_columns(values, step)
+        if offset[2] == 0:
+            put(lower, (k, plane), values)
         else:
-            lower[k, plane, span, :] = z_shift(values, centre[k, span, :], plane, step)
-            current = halo_lower[k, 0, span, :]
-            halo_lower[k, 0, span, :] = z_edge(current, values, plane, step)
+            shifts.append((1, (k,), -offset[2], values, SHIFTED + k))
+    for array, lead, step, values, slot in shifts:
+        if is_columns:
+            centre[slot, span, :] = values
+            put((fields, lower)[array], (*lead, 0), z_shift_columns(values, step))
+        else:
+            put((fields, lower)[array], (*lead, plane), z_shift(values, centre[slot, span, :], plane, step))
+            put((halo_fields, halo_lower)[array], (*lead, 0), None, lambda now: z_edge(now, values, plane, step))
 
 
 def x_roll(values, step, is_columns):
@@ -285,7 +322,7 @@
 
 
 def link_cells(plane, is_columns, first, stride, arrays, out, results):
-    fields, lower, half, weight, accum, _ = arrays
+    fields, lower, half, weight, base = arrays
     coupling, scale, start = results
     depth = fields.shape[-1]
     here = (0, 0, 0)
@@ -323,29 +360,32 @@
         )
         means = means + mean
         coupling[n, plane, out, :] = drop * slope - mean
-    active = at(ACT, here)
-    res = [
-        active * (read(accum, (c,), here) + (flux[c] + mob[c] * drops)) for c in range(3)
-    ]
+    flux = [flux[c] + mob[c] * drops for c in range(3)]
     rate = relax_weight / (means + own_slope * drops)
+    right = read(base, (), here) + (w[0] * flux[0] + w[1] * flux[1] + w[2] * flux[2])
     scale[plane, out, :] = rate
-    start[plane, out, :] = -rate * (w[0] * res[0] + w[1] * res[1] + w[2] * res[2])
-    return res
+    start[plane, out, :] = -rate * right
+    return flux
 
 
 def inner(x_axis, local, columns, xa, xb, *refs):
-    tables, results, halo_results, store = refs[:3], refs[3:6], refs[6:9], refs[9]
-    tabs, arrays, halo = refs[10], refs[11:17], refs[17:]
+    tabs, results, halo_results, store = refs[0], refs[1:4], refs[4:7], refs[7]
+    edges, arrays, halo, centre = refs[8:18], refs[18:23], refs[23:28], refs[28]
     planes, rows, depth = local.shape[1:]
     total = planes + 2 * W
     even_x = parity_of(x_axis)
-    fill_tables(tables, tabs)
     tiles = range(rows // 8)
 
     def cells(get, plane, is_columns=False):
         for tile in tiles:
             span = slice(8 * tile, 8 * tile + 8)
-            properties(lambda c: get(c, span), plane, is_columns, 8 + 8 * tile, tabs, arrays, halo)
+            to = slice(8 + 8 * tile, 16 + 8 * tile)
+
+            def put(ref, lead, values, change=None):
+                at = (*lead, to, slice(None))
+                ref[at] = values if change is None else change(ref[at])
+
+            properties(lambda c: get(c, span), plane, is_columns, put, tabs, arrays, halo, centre, span)
 
     cells(lambda c, span: columns[c, span, :], 0, True)
 
@@ -373,6 +413,20 @@
     cells(from_x(far, True), 0)
     cells(from_x(far, False), total - 1)
 
+    def hand_on(sources, targets, plane):
+        for source, target in zip(sources, targets):
+            for lead in itertools.product(*(range(n) for n in source.shape[:-3])):
+                last = source[(*lead, plane, slice(6 + rows, 8 + rows), slice(None))]
+                head = source[(*lead, plane, slice(8, 10), slice(None))]
+                target[(*lead, plane, pl.ds(0, 2, stride=2), slice(None))] = last
+                target[(*lead, plane, pl.ds(RING - 3, 2, stride=2), slice(None))] = head
+
+    hand_on(halo, edges[5:], 0)
+
+    @pl.loop(0, total)
+    def _(plane):
+        hand_on(arrays, edges[:5], plane)
+
     def links(plane, is_columns=False):
         for tile in tiles:
             out = slice(8 * tile, 8 * tile + 8)
@@ -392,65 +446,61 @@
 RING = 2 * (W + 2)
 
 
-def finish(axes, count_y, local, columns, xa, xb, *refs):
-    tables = refs[:3]
-    ys = refs[3 : 3 + count_y]
-    results, halo_results, store, residual, update = (
-        refs[3 + count_y : 6 + count_y],
-        refs[6 + count_y : 9 + count_y],
-        *refs[9 + count_y : 12 + count_y],
-    )
-    refs = refs[12 + count_y :]
-    tabs, raw, edge_store = refs[:3]
-    edge_results, edge_halo_results = refs[3:6], refs[6:9]
-    sols, halo_sols, edge_sols, edge_halo_sols = (refs[9 + 2 * i : 11 + 2 * i] for i in range(4))
-    arrays, halo = refs[17:23], refs[23:]
+def finish(axis, count_y, local, *refs):
+    tabs, accum, ys = refs[0], refs[1], refs[2 : 2 + count_y]
+    refs = refs[2 + count_y :]
+    results, halo_results, store = refs[:3], refs[3:6], refs[6]
+    residual, update = refs[17:19]
+    arrays, halo = refs[19:24], refs[24:29]
+    edge_store, raw, centre = refs[29:32]
+    edge_results, edge_halo_results = refs[32:35], refs[35:38]
+    sols, halo_sols, edge_sols, edge_halo_sols = (refs[38 + 2 * i : 40 + 2 * i] for i in range(4))
     planes, rows, depth = local.shape[1:]
     total = planes + 2 * W
-    even_x, even_y, _ = (parity_of(axis) for axis in axes)
-    fill_tables(tables, tabs)
-
-    def put(c, plane, values, n):
+    even_y = parity_of(axis)
+
+    def halo_rows(c, plane, n):
         low = high = jnp.zeros((W, depth), f32)
         if count_y:
             a = ys[0][n]
             b = ys[1][n] if count_y > 1 else None
             low, high = pick(even_y, b, a), pick(even_y, a, b)
-        raw[c, plane, pl.ds(0, 2, stride=2), :] = values[rows - 2 :]
-        raw[c, plane, pl.ds(4, W, stride=2), :] = high
-        raw[c, plane, pl.ds(1, W, stride=2), :] = low
-        raw[c, plane, pl.ds(RING - 3, 2, stride=2), :] = values[:2]
-        raw[c, plane, RING:16, :] = jnp.zeros((16 - RING, depth), f32)
+        raw[c, plane, 0:W, :] = low
+        raw[c, plane, W : 2 * W, :] = high
 
     base = CHANNELS * planes
 
     @pl.loop(0, CHANNELS)
     def _(c):
         for x in range(planes):
-            put(c, W + x, local[c, x], c * planes + x)
+            halo_rows(c, W + x, c * planes + x)
         for q in range(NEAR):
-            n = c * NEAR + q
-            a, b = xa[n], xb[n]
-            put(c, 1 + q, pick(even_x, b, a), base + n)
-            put(c, W + planes + q, pick(even_x, a, b), base + XMAIN + n)
-        put(c, total, columns[c], base + 2 * XMAIN + c)
+            halo_rows(c, 1 + q, base + c * NEAR + q)
+            halo_rows(c, W + planes + q, base + XMAIN + c * NEAR + q)
+        halo_rows(c, total, base + 2 * XMAIN + c)
 
     @pl.loop(0, FAR)
     def _(c):
-        n = CHANNELS * NEAR + c
-        a, b = xa[n], xb[n]
-        put(c, 0, pick(even_x, b, a), base + n)
-        put(c, total - 1, pick(even_x, a, b), base + XMAIN + n)
+        halo_rows(c, 0, base + CHANNELS * NEAR + c)
+        halo_rows(c, total - 1, base + XMAIN + CHANNELS * NEAR + c)
 
     for c in range(FAR, CHANNELS):
         for plane in (0, total - 1):
-            raw[c, plane] = jnp.zeros((16, depth), f32)
+            raw[c, plane] = jnp.zeros((2 * W, depth), f32)
 
     def cells(plane, is_columns=False):
-        for tile in range(2):
-            span = slice(8 * tile, 8 * tile + 8)
-            get = lambda c: raw[c, plane, span, :]
-            properties(get, 0 if is_columns else plane, is_columns, 8 * tile, tabs, arrays, halo)
+        def put(ref, lead, values, change=None):
+            low = (*lead, pl.ds(1, W, stride=2), slice(None))
+            high = (*lead, pl.ds(4, W, stride=2), slice(None))
+            if change is not None:
+                values = change(jnp.concatenate([ref[low], ref[high]], axis=0))
+            ref[low] = values[:W]
+            ref[high] = values[W:]
+
+        get = lambda c: raw[c, plane, :, :]
+        properties(
+            get, 0 if is_columns else plane, is_columns, put, tabs, arrays, halo, centre, slice(0, 8)
+        )
 
     cells(total, True)
 
@@ -572,13 +622,17 @@
         for tile in range(tiles):
             span = slice(8 * tile, 8 * tile + 8)
             update[x, span, :] = relaxed(slot, plane, tile)
+            active = local[3, x, span, :]
             for c in range(3):
-                residual[c, x, span, :] = store[c, plane, span, :]
-        update[x, 0:1, :] = edge[7:8]
-        update[x, rows - 1 : rows, :] = edge[0:1]
-        for c in range(3):
-            residual[c, x, 0:1, :] = edge_store[c, plane, 7:8, :]
-            residual[c, x, rows - 1 : rows, :] = edge_store[c, plane, 0:1, :]
+                flow = store[c, plane, span, :]
+                residual[c, x, span, :] = active * (accum[c, x, span, :] + flow)
+        for row_of, edge_row in ((0, 7), (rows - 1, 0)):
+            to, source = slice(row_of, row_of + 1), slice(edge_row, edge_row + 1)
+            update[x, to, :] = edge[source]
+            active = local[3, x, to, :]
+            for c in range(3):
+                flow = edge_store[c, plane, source, :]
+                residual[c, x, to, :] = active * (accum[c, x, to, :] + flow)
 
 
 def call(kernel, name, mib, **options):
@@ -590,18 +644,11 @@
     )
 
 
-def cell_arrays(total, height, depth):
+def cell_shapes(total, height, depth):
     return [
-        pltpu.VMEM(shape, f32)
+        (*lead, count, height, depth)
         for count in (total, 1)
-        for shape in (
-            (SHIFTED, 3, count, height, depth),
-            (UP, count, height, depth),
-            (UP, count, height, depth),
-            (3, count, height, depth),
-            (3, count, height, depth),
-            (UP, height, depth),
-        )
+        for lead in ((SHIFTED, 3), (UP,), (UP,), (3,), ())
     ]
 
 
@@ -633,34 +680,45 @@
     like = lambda *shape: jax.ShapeDtypeStruct(shape, f32)
     fill = lambda shape, got: [jnp.zeros(shape.shape, f32) if one is None else one for one in got]
 
-    arguments = (cell_state, old_mass, pore_volume, transmissibility, active_mask, pvt_region)
+    arguments = (
+        *(cell_state, old_mass, pore_volume, transmissibility, active_mask, pvt_region),
+        *tables,
+    )
     z_shape = like(groups, rows, depth)
-    local, *z_send = call(
+    cells = like(3, planes, rows, depth)
+    local, accum, tabs, *z_send = call(
         functools.partial(pack_z, az),
         "pack_z",
         8,
-        out_shape=(like(CHANNELS, planes, rows, depth), z_shape, z_shape),
-        in_specs=[HBM] * 6,
-        out_specs=(VMEM,) * 3,
+        out_shape=(like(CHANNELS, planes, rows, depth), cells, like(9, 8, depth), z_shape, z_shape),
+        in_specs=[HBM] * 9,
+        out_specs=(VMEM,) * 5,
         scratch_shapes=[
             pltpu.VMEM((2, planes, rows, depth), jnp.int32),
-            pltpu.SemaphoreType.DMA((7,)),
+            pltpu.VMEM(cells.shape, f32),
+            pltpu.VMEM((planes, rows, depth), f32),
+            pltpu.VMEM((3, *formation_factor.shape), f32),
+            pltpu.SemaphoreType.DMA((10,)),
         ],
     )(*(pltpu.with_memory_space_constraint(array, pltpu.MemorySpace.HBM) for array in arguments))
     za, zb = fill(z_shape, swaps(az, *z_send))
 
-    x_shape = like(XMAIN + groups, rows, depth)
+    _, groups_x = groups_of(W, depth)
+    x_shape = like(XMAIN + groups_x, rows, depth)
     x_send = call(
         functools.partial(pack_x, ax), "pack_x", 8, out_shape=(x_shape, x_shape)
     )(local)
     x_send = call(
-        join_x,
+        functools.partial(join_x, ax, planes),
         "join_x",
         8,
         out_shape=(x_shape, x_shape),
         in_specs=[VMEM, VMEM, ANY, ANY],
         out_specs=(ANY, ANY),
-        scratch_shapes=[pltpu.VMEM(z_shape.shape, f32), pltpu.SemaphoreType.DMA((2,))],
+        scratch_shapes=[
+            pltpu.VMEM((2, groups_x, rows, depth), f32),
+            pltpu.SemaphoreType.DMA((2,)),
+        ],
         input_output_aliases={2: 0, 3: 1},
     )(za, zb, *x_send)
     xa, xb = fill(x_shape, swaps(ax, *x_send))
@@ -686,38 +744,43 @@
     )(za, zb, xa, xb, *y_send)
     ys = swaps(ay, y_send[0], y_send[-1])[:count_y] if count_y else []
 
-    smem = pl.BlockSpec(memory_space=pltpu.SMEM)
-    tabs = pltpu.VMEM((9, 8, depth), f32)
+    vmem = lambda shapes: [pltpu.VMEM(shape, f32) for shape in shapes]
+    flow = (3, total, rows, depth)
+    edges = cell_shapes(total, 16, depth)
+    shapes = result_shapes(total, rows, depth) + [flow] + edges
     halves = call(
         functools.partial(inner, ax),
         "inner",
         24,
-        out_shape=[like(*shape) for shape in result_shapes(total, rows, depth)]
-        + [like(3, total, rows, depth)],
-        in_specs=[VMEM] * 4 + [smem] * 3,
-        out_specs=[VMEM] * 7,
-        scratch_shapes=[tabs] + cell_arrays(total, rows + 16, depth),
-    )(local, columns, xa, xb, *tables)
-
-    return call(
-        functools.partial(finish, (ax, ay, az), count_y),
+        out_shape=[like(*shape) for shape in shapes],
+        in_specs=[VMEM] * 5,
+        out_specs=[VMEM] * len(shapes),
+        scratch_shapes=vmem(cell_shapes(total, rows + 16, depth) + [(SHIFTED + UP, rows, depth)]),
+    )(local, columns, xa, xb, tabs)
+
+    solutions = [
+        (3, count, height, depth) for height in (rows + 16, 16) for count in (total, 1) for _ in range(2)
+    ]
+    before = 3 + count_y + 7
+    residual, update, *_ = call(
+        functools.partial(finish, ay, count_y),
         "finish",
         24,
-        out_shape=(like(3, planes, rows, depth), like(planes, rows, depth)),
-        in_specs=[VMEM] * 4 + [smem] * 3 + [VMEM] * (count_y + 7),
-        out_specs=(VMEM, VMEM),
-        scratch_shapes=[
-            tabs,
-            pltpu.VMEM((CHANNELS, total + 1, 16, depth), f32),
-            pltpu.VMEM((3, total, 8, depth), f32),
-            *(pltpu.VMEM(shape, f32) for shape in result_shapes(total, 8, depth)),
-            *[pltpu.VMEM((3, total, rows + 16, depth), f32)] * 2,
-            *[pltpu.VMEM((3, 1, rows + 16, depth), f32)] * 2,
-            *[pltpu.VMEM((3, total, 16, depth), f32)] * 2,
-            *[pltpu.VMEM((3, 1, 16, depth), f32)] * 2,
-        ]
-        + cell_arrays(total, 16, depth),
-    )(local, columns, xa, xb, *tables, *ys, *halves)
+        out_shape=[cells, like(planes, rows, depth)] + [like(*shape) for shape in edges],
+        in_specs=[VMEM] * (before + len(edges)),
+        out_specs=[VMEM] * (2 + len(edges)),
+        scratch_shapes=vmem(
+            [
+                (3, total, 8, depth),
+                (CHANNELS, total + 1, 2 * W, depth),
+                (SHIFTED + UP, 2 * W, depth),
+                *result_shapes(total, 8, depth),
+                *solutions,
+            ]
+        ),
+        input_output_aliases={before + i: 2 + i for i in range(len(edges))},
+    )(local, tabs, accum, *ys, *halves)
+    return residual, update
 
 
 def solution(mesh):

time: 56.8 us -> 49.8 us (0.88)
  waiting for transfers between devices: 20.9 us -> 17.3 us
  Pallas kernels: 26.6 us -> 23.3 us
    pallas_call x2, Pallas kernels: 13.5 us -> 9.76 us  [the longest x1 9.52 us: body(): call(functools.partial(finish, ay, count_y), 'finish', 24, out_shape=[cel...]
    ppermute x5, waiting for transfers between devices: 20.9 us -> 17.3 us  [swaps(): got.append(lax.ppermute(message, axis, pairs + [(b, a) for a, b in pairs]))]
  transfers between devices with their start and end apart: 5 -> 5, of which waited for: 4 -> 4; matrix products, arithmetic and copies ran while one was open for 0% -> 0% of each run, Pallas kernels for 18% -> 21%
where the time goes in v5:
time: 49.8 us; the launch traced here: 49.6 us
  Pallas kernels  23.3 us (47%)
  waiting for transfers between devices  17.3 us (35%)
  starting transfers between devices  8.33 us (17%)
  between operations  0.71 us (1%)
    ppermute x5, waiting for transfers between devices, swaps(): got.append(lax.ppermute(message, axis, pairs + [(b, a) for a, b in pairs]))  17.3 us
    pallas_call x1, Pallas kernels, body(): call(functools.partial(inner, ax), 'inner', 24, out_shape=[like(*shape) f...  10.5 us
    pallas_call x1, Pallas kernels, body(): call(functools.partial(finish, ay, count_y), 'finish', 24, out_shape=[cel...  9.52 us
    ppermute x5, starting transfers between devices, swaps(): got.append(lax.ppermute(message, axis, pairs + [(b, a) for a, b in pairs]))  8.33 us
    pallas_call x1, Pallas kernels, body(): call(functools.partial(pack_z, az), 'pack_z', 8, out_shape=(like(CHANNELS...  2.33 us
  transfers between devices with their start and end apart: 5, of which 4 were waited for; matrix products, arithmetic and copies ran while one was open for 0% of the time, Pallas kernels for 21%

profile of v5, /device:TPU:17, one launch (start us, length us, event | category | flops | bytes accessed | tf_op | source)
XLA Modules:
  0.0 49.6 jit_solution(16579734072260067406)
XLA Ops:
  0.6 2.3 %pack_z.1 = (f32[20,8,16,128]{3,2,1,0:T(8,128)S(1)}, f32[3,8,16,128]{3,2,1,0:T(8,128)S(1)}, f32[9,8,128]{2,1,0:T(8,128)S(1)}, f32[10,16,128]{2,1,0:T(8,128)S(1)}, f32[10,16,128]{2,1,0:T(8,128)S(1)}) custom-call(f32[3,8,16,128]{3,2,1,0:T(8,128)} %refs_0_.1, f32[3,8,16,128]{3,2,1,0:T(8,128)} %refs_1_.1, f32[8,16,128]{2,1,0:T(8,128)} %refs_2_.1, ...), custom_call_target="tpu_custom_call" | custom-call | tf_op jit(solution)/shard_map/pack_z/pallas_call | solution.py:689
  3.0 0.7 %collective-permute-start = (f32[10,16,128]{2,1,0:T(8,128)S(1)}, f32[10,16,128]{2,1,0:T(8,128)S(1)}, u32[]{:S(2)}, u32[]{:S(2)}) collective-permute-start(f32[10,16,128]{2,1,0:T(8,128)S(1)} %get-tuple-element.35), channel_id=1, source_target_pairs={{0,1},{2,3},{1,0},{3,2},{4,5},{6,7},{5,4},{7,6},{8,9},{10,11},{9,8... | collective-permute-start | bytes 245768 | tf_op jit(solution)/shard_map/ppermute | solution.py:63
  3.7 3.0 %collective-permute-start.1 = (f32[10,16,128]{2,1,0:T(8,128)S(1)}, f32[10,16,128]{2,1,0:T(8,128)S(1)}, u32[]{:S(2)}, u32[]{:S(2)}) collective-permute-start(f32[10,16,128]{2,1,0:T(8,128)S(1)} %get-tuple-element.36), channel_id=1, source_target_pairs={{1,2},{2,1},{5,6},{6,5},{9,10},{10,9},{13,14},{14,13},{17,18},{18,... | collective-permute-start | bytes 245768 | tf_op jit(solution)/shard_map/ppermute | solution.py:63
  6.7 0.1 pack_x.1
  6.8 0.0 collective-permute-done.za
  6.9 2.9 %collective-permute-done.1.zb = f32[10,16,128]{2,1,0:T(8,128)S(1)} collective-permute-done((f32[10,16,128]{2,1,0:T(8,128)S(1)}, f32[10,16,128]{2,1,0:T(8,128)S(1)}, u32[]{:S(2)}, u32[]{:S(2)}) %collective-permute-start.1) | collective-permute-done | bytes 81952 | tf_op jit(solution)/shard_map/ppermute | solution.py:63
  9.8 0.2 join_x.1
  10.0 1.4 %collective-permute-start.2 = (f32[79,16,128]{2,1,0:T(8,128)S(1)}, f32[79,16,128]{2,1,0:T(8,128)S(1)}, u32[]{:S(2)}, u32[]{:S(2)}) collective-permute-start(f32[79,16,128]{2,1,0:T(8,128)S(1)} %get-tuple-element.39), channel_id=1, source_target_pairs={{0,8},{16,24},{8,0},{24,16},{1,9},{17,25},{9,1},{25,17},{2,10},{18... | collective-permute-start | bytes 1941512 | tf_op jit(solution)/shard_map/ppermute | solution.py:63
  11.4 1.9 %collective-permute-start.3 = (f32[79,16,128]{2,1,0:T(8,128)S(1)}, f32[79,16,128]{2,1,0:T(8,128)S(1)}, u32[]{:S(2)}, u32[]{:S(2)}) collective-permute-start(f32[79,16,128]{2,1,0:T(8,128)S(1)} %get-tuple-element.40), channel_id=1, source_target_pairs={{8,16},{16,8},{9,17},{17,9},{10,18},{18,10},{11,19},{19,11},{12,20... | collective-permute-start | bytes 1941512 | tf_op jit(solution)/shard_map/ppermute | solution.py:63
  13.3 0.1 pack_y.1.refs_0_
  13.4 8.7 %collective-permute-done.2.xa = f32[79,16,128]{2,1,0:T(8,128)S(1)} collective-permute-done((f32[79,16,128]{2,1,0:T(8,128)S(1)}, f32[79,16,128]{2,1,0:T(8,128)S(1)}, u32[]{:S(2)}, u32[]{:S(2)}) %collective-permute-start.2) | collective-permute-done | bytes 647200 | tf_op jit(solution)/shard_map/ppermute | solution.py:63
  22.0 3.5 %collective-permute-done.3.xb = f32[79,16,128]{2,1,0:T(8,128)S(1)} collective-permute-done((f32[79,16,128]{2,1,0:T(8,128)S(1)}, f32[79,16,128]{2,1,0:T(8,128)S(1)}, u32[]{:S(2)}, u32[]{:S(2)}) %collective-permute-start.3) | collective-permute-done | bytes 647200 | tf_op jit(solution)/shard_map/ppermute | solution.py:63
  25.5 0.6 %join_y.1 = (f32[328,4,128]{2,1,0:T(4,128)S(1)}, f32[20,16,128]{2,1,0:T(8,128)S(1)}) custom-call(f32[10,16,128]{2,1,0:T(8,128)S(1)} %collective-permute-done.za, f32[10,16,128]{2,1,0:T(8,128)S(1)} %collective-permute-done.1.zb, f32[79,16,128]{2,1,0:T(8,128)S(1)} %collective-permute-done.2.xa, ...), custom_call_target="tpu_custom_call", output_to_operand_aliasing={{0}: (4, {})} | custom-call | tf_op jit(solution)/shard_map/join_y/pallas_call | solution.py:734
  26.1 1.3 %collective-permute-start.4 = (f32[328,4,128]{2,1,0:T(4,128)S(1)}, f32[328,4,128]{2,1,0:T(4,128)S(1)}, u32[]{:S(2)}, u32[]{:S(2)}) collective-permute-start(f32[328,4,128]{2,1,0:T(4,128)S(1)} %get-tuple-element.41), channel_id=1, source_target_pairs={{0,4},{4,0},{1,5},{5,1},{2,6},{6,2},{3,7},{7,3},{8,12},{12,8},{9,1... | collective-permute-start | bytes 2015240 | tf_op jit(solution)/shard_map/ppermute | solution.py:63
  27.4 10.5 %inner.1 = (f32[26,16,16,128]{3,2,1,0:T(8,128)S(1)}, f32[16,16,128]{2,1,0:T(8,128)S(1)}, f32[16,16,128]{2,1,0:T(8,128)S(1)}, f32[26,1,16,128]{3,2,1,0:T(8,128)S(...) custom-call(f32[20,8,16,128]{3,2,1,0:T(8,128)S(1)} %get-tuple-elemen, ...), custom_call_target="tpu_custom_call" | custom-call | tf_op jit(solution)/shard_map/inner/pallas_call | solution.py:751
  37.8 2.2 %collective-permute-done.4.refs_2_ = f32[328,4,128]{2,1,0:T(4,128)S(1)} collective-permute-done((f32[328,4,128]{2,1,0:T(4,128)S(1)}, f32[328,4,128]{2,1,0:T(4,128)S(1)}, u32[]{:S(2)}, u32[]{:S(2)}) %collective-permute-start.4) | collective-permute-done | bytes 671776 | tf_op jit(solution)/shard_map/ppermute | solution.py:63
  40.1 9.5 %finish.1 = (f32[3,8,16,128]{3,2,1,0:T(8,128)}, f32[8,16,128]{2,1,0:T(8,128)}, f32[8,3,16,16,128]{4,3,2,1,0:T(8,128)S(1)}, f32[13,16,16,128]{3,2,1,0:T(8,128)S(1...) custom-call(f32[20,8,16,128]{3,2,1,0:T(8,128)S(1)} %get-tuple-elemen, ...), custom_call_target="tpu_custom_call", output_to_operand_aliasing={{2}: (11, {}), {3}: (12, {}), {4}: (13, {}), {5}: (14, {}),... | custom-call | tf_op jit(solution)/shard_map/finish/pallas_call | solution.py:765
Async XLA Ops:
  3.0 3.9 %collective-permute-start = (f32[10,16,128]{2,1,0:T(8,128)S(1)}, f32[10,16,128]{2,1,0:T(8,128)S(1)}, u32[]{:S(2)}, u32[]{:S(2)}) collective-permute-start(f32[10,16,128]{2,1,0:T(8,128)S(1)} %get-tuple-element.35), channel_id=1, source_target_pairs={{0,1},{2,3},{1,0},{3,2},{4,5},{6,7},{5,4},{7,6},{8,9},{10,11},{9,8... | collective-permute-start | bytes 245768 | tf_op jit(solution)/shard_map/ppermute | solution.py:63
  3.7 6.0 %collective-permute-start.1 = (f32[10,16,128]{2,1,0:T(8,128)S(1)}, f32[10,16,128]{2,1,0:T(8,128)S(1)}, u32[]{:S(2)}, u32[]{:S(2)}) collective-permute-start(f32[10,16,128]{2,1,0:T(8,128)S(1)} %get-tuple-element.36), channel_id=1, source_target_pairs={{1,2},{2,1},{5,6},{6,5},{9,10},{10,9},{13,14},{14,13},{17,18},{18,... | collective-permute-start | bytes 245768 | tf_op jit(solution)/shard_map/ppermute | solution.py:63
  10.0 12.0 %collective-permute-start.2 = (f32[79,16,128]{2,1,0:T(8,128)S(1)}, f32[79,16,128]{2,1,0:T(8,128)S(1)}, u32[]{:S(2)}, u32[]{:S(2)}) collective-permute-start(f32[79,16,128]{2,1,0:T(8,128)S(1)} %get-tuple-element.39), channel_id=1, source_target_pairs={{0,8},{16,24},{8,0},{24,16},{1,9},{17,25},{9,1},{25,17},{2,10},{18... | collective-permute-start | bytes 1941512 | tf_op jit(solution)/shard_map/ppermute | solution.py:63
  11.4 14.1 %collective-permute-start.3 = (f32[79,16,128]{2,1,0:T(8,128)S(1)}, f32[79,16,128]{2,1,0:T(8,128)S(1)}, u32[]{:S(2)}, u32[]{:S(2)}) collective-permute-start(f32[79,16,128]{2,1,0:T(8,128)S(1)} %get-tuple-element.40), channel_id=1, source_target_pairs={{8,16},{16,8},{9,17},{17,9},{10,18},{18,10},{11,19},{19,11},{12,20... | collective-permute-start | bytes 1941512 | tf_op jit(solution)/shard_map/ppermute | solution.py:63
  26.1 14.0 %collective-permute-start.4 = (f32[328,4,128]{2,1,0:T(4,128)S(1)}, f32[328,4,128]{2,1,0:T(4,128)S(1)}, u32[]{:S(2)}, u32[]{:S(2)}) collective-permute-start(f32[328,4,128]{2,1,0:T(4,128)S(1)} %get-tuple-element.41), channel_id=1, source_target_pairs={{0,4},{4,0},{1,5},{5,1},{2,6},{6,2},{3,7},{7,3},{8,12},{12,8},{9,1... | collective-permute-start | bytes 2015240 | tf_op jit(solution)/shard_map/ppermute | solution.py:63

commit v6 on v5

--- a/solution.py
+++ b/solution.py
@@ -170,7 +170,18 @@
                 out[CHANNELS * NEAR + c] = local[c, far]
 
 
-def join_x(axis, planes, za, zb, a_in, b_in, a_out, b_out, columns, sems):
+def put_rows(outs, n, values, even):
+    head, tail = values[:W], values[values.shape[0] - W :]
+    for out, up, down in zip(outs, (tail, head), (head, tail)):
+        out[n] = pick(even, up, down)
+
+
+def join_x(axis, y_axis, za, zb, local, *outs):
+    planes = local.shape[1]
+    even_y = parity_of(y_axis)
+    for c in range(CHANNELS):
+        for x in range(planes):
+            put_rows(outs[2:], c * planes + x, local[c, x], even_y)
     rows, depth = za.shape[1:]
     even = parity_of(axis)
     per, _ = groups_of(planes, depth)
@@ -185,35 +196,13 @@
             for n, plane in enumerate((planes - W, 0)):
                 source = (c % per) * span_of(planes) + 2 * W * plane
                 sides[n] = jnp.where(here, pltpu.roll(values, (to - source) % depth, 1), sides[n])
-        columns[0, group] = pick(even, *sides)
-        columns[1, group] = pick(even, *sides[::-1])
-    copies = [
-        pltpu.make_async_copy(columns.at[n], out.at[pl.ds(XMAIN, groups_x)], sems.at[n])
-        for n, out in enumerate((a_out, b_out))
-    ]
-    for copy in copies:
-        copy.start()
-    for copy in copies:
-        copy.wait()
-
-
-def put_rows(outs, n, values, even):
-    head, tail = values[:W], values[values.shape[0] - W :]
-    for out, up, down in zip(outs, (tail, head), (head, tail)):
-        out[n] = pick(even, up, down)
-
-
-def pack_y(axis, local, *outs):
-    planes = local.shape[1]
-    even = parity_of(axis)
-    for c in range(CHANNELS):
-        for x in range(planes):
-            put_rows(outs, c * planes + x, local[c, x], even)
-
-
-def join_y(axis, x_axis, count, planes, za, zb, xa, xb, *refs):
-    outs, columns = refs[count : 2 * count], refs[2 * count]
-    stages, sems = refs[2 * count + 1 : 3 * count + 1], refs[3 * count + 1]
+        outs[0][group] = pick(even, *sides)
+        outs[1][group] = pick(even, *sides[::-1])
+
+
+def join_y(axis, x_axis, planes, za, zb, xa, xb, ca, cb, *refs):
+    count = len(refs) // 2
+    columns, *outs = refs[count:]
     rows, depth = xa.shape[1:]
     even = parity_of(axis)
     even_x = parity_of(x_axis)
@@ -224,31 +213,20 @@
         group, base = c // per, (c % per) * span_of(planes)
         own = pltpu.roll(za[group] + zb[group], (2 * W * W - base) % depth, 1)
         group, base = c // per_x, (c % per_x) * span_of(W)
-        a, b = xa[XMAIN + group], xb[XMAIN + group]
+        a, b = ca[group], cb[group]
         below = pltpu.roll(pick(even_x, b, a), (depth - base) % depth, 1)
         above = pltpu.roll(pick(even_x, a, b), (2 * W * (planes + W) - base) % depth, 1)
         values = jnp.where(lane < 2 * W * W, below, jnp.where(lane < 2 * W * (W + planes), own, above))
         columns[c] = values
-        put_rows(stages, 2 * XMAIN + c, values, even)
+        put_rows(outs, 2 * XMAIN + c, values, even)
 
     @pl.loop(0, XMAIN // 2)
     def _(i):
         for j in range(2):
             n = 2 * i + j
             a, b = xa[n], xb[n]
-            put_rows(stages, n, pick(even_x, b, a), even)
-            put_rows(stages, XMAIN + n, pick(even_x, a, b), even)
-
-    copies = [
-        pltpu.make_async_copy(
-            stage, out.at[pl.ds(CHANNELS * planes, 2 * XMAIN + CHANNELS)], sems.at[i]
-        )
-        for i, (stage, out) in enumerate(zip(stages, outs))
-    ]
-    for copy in copies:
-        copy.start()
-    for copy in copies:
-        copy.wait()
+            put_rows(outs, n, pick(even_x, b, a), even)
+            put_rows(outs, XMAIN + n, pick(even_x, a, b), even)
 
 
 PRESS, MOB, SLOPE, ACT = 0, 1, 4, 7
@@ -447,8 +425,8 @@
 
 
 def finish(axis, count_y, local, *refs):
-    tabs, accum, ys = refs[0], refs[1], refs[2 : 2 + count_y]
-    refs = refs[2 + count_y :]
+    tabs, accum, ys, more_ys = refs[0], refs[1], refs[2 : 2 + count_y], refs[2 + count_y : 2 + 2 * count_y]
+    refs = refs[2 + 2 * count_y :]
     results, halo_results, store = refs[:3], refs[3:6], refs[6]
     residual, update = refs[17:19]
     arrays, halo = refs[19:24], refs[24:29]
@@ -459,30 +437,28 @@
     total = planes + 2 * W
     even_y = parity_of(axis)
 
-    def halo_rows(c, plane, n):
+    def halo_rows(c, plane, sources, n):
         low = high = jnp.zeros((W, depth), f32)
         if count_y:
-            a = ys[0][n]
-            b = ys[1][n] if count_y > 1 else None
+            a = sources[0][n]
+            b = sources[1][n] if count_y > 1 else None
             low, high = pick(even_y, b, a), pick(even_y, a, b)
         raw[c, plane, 0:W, :] = low
         raw[c, plane, W : 2 * W, :] = high
 
-    base = CHANNELS * planes
-
     @pl.loop(0, CHANNELS)
     def _(c):
         for x in range(planes):
-            halo_rows(c, W + x, c * planes + x)
+            halo_rows(c, W + x, ys, c * planes + x)
         for q in range(NEAR):
-            halo_rows(c, 1 + q, base + c * NEAR + q)
-            halo_rows(c, W + planes + q, base + XMAIN + c * NEAR + q)
-        halo_rows(c, total, base + 2 * XMAIN + c)
+            halo_rows(c, 1 + q, more_ys, c * NEAR + q)
+            halo_rows(c, W + planes + q, more_ys, XMAIN + c * NEAR + q)
+        halo_rows(c, total, more_ys, 2 * XMAIN + c)
 
     @pl.loop(0, FAR)
     def _(c):
-        halo_rows(c, 0, base + CHANNELS * NEAR + c)
-        halo_rows(c, total - 1, base + XMAIN + CHANNELS * NEAR + c)
+        halo_rows(c, 0, more_ys, CHANNELS * NEAR + c)
+        halo_rows(c, total - 1, more_ys, XMAIN + CHANNELS * NEAR + c)
 
     for c in range(FAR, CHANNELS):
         for plane in (0, total - 1):
@@ -703,46 +679,33 @@
     )(*(pltpu.with_memory_space_constraint(array, pltpu.MemorySpace.HBM) for array in arguments))
     za, zb = fill(z_shape, swaps(az, *z_send))
 
-    _, groups_x = groups_of(W, depth)
-    x_shape = like(XMAIN + groups_x, rows, depth)
-    x_send = call(
-        functools.partial(pack_x, ax), "pack_x", 8, out_shape=(x_shape, x_shape)
-    )(local)
-    x_send = call(
-        functools.partial(join_x, ax, planes),
+    x_shape = like(XMAIN, rows, depth)
+    x_send = call(functools.partial(pack_x, ax), "pack_x", 8, out_shape=(x_shape, x_shape))(local)
+    xa, xb = fill(x_shape, swaps(ax, *x_send))
+
+    count_y = min(lax.axis_size(ay) - 1, 2)
+    ys, more_ys = [], []
+    c_shape = like(groups_of(W, depth)[1], rows, depth)
+    sent = call(
+        functools.partial(join_x, ax, ay),
         "join_x",
         8,
-        out_shape=(x_shape, x_shape),
-        in_specs=[VMEM, VMEM, ANY, ANY],
-        out_specs=(ANY, ANY),
-        scratch_shapes=[
-            pltpu.VMEM((2, groups_x, rows, depth), f32),
-            pltpu.SemaphoreType.DMA((2,)),
-        ],
-        input_output_aliases={2: 0, 3: 1},
-    )(za, zb, *x_send)
-    xa, xb = fill(x_shape, swaps(ax, *x_send))
-
-    count_y = min(lax.axis_size(ay) - 1, 2)
-    extra = 2 * XMAIN + CHANNELS
-    y_shape = like(CHANNELS * planes + extra, W, depth)
-    y_send = ()
+        out_shape=(c_shape, c_shape) + (like(CHANNELS * planes, W, depth),) * count_y,
+    )(za, zb, local)
+    c_send, y_send = sent[:2], sent[2:]
+    ca, cb = fill(c_shape, swaps(ax, *c_send))
     if count_y:
-        y_send = call(
-            functools.partial(pack_y, ay), "pack_y", 8, out_shape=(y_shape,) * count_y
-        )(local)
-    *y_send, columns = call(
-        functools.partial(join_y, ay, ax, count_y, planes),
+        ys = swaps(ay, y_send[0], y_send[-1])[:count_y]
+    columns, *y_send = call(
+        functools.partial(join_y, ay, ax, planes),
         "join_y",
         8,
-        out_shape=(y_shape,) * count_y + (like(CHANNELS, rows, depth),),
-        in_specs=[VMEM] * 4 + [ANY] * count_y,
-        out_specs=(ANY,) * count_y + (VMEM,),
-        scratch_shapes=[pltpu.VMEM((extra, W, depth), f32)] * count_y
-        + [pltpu.SemaphoreType.DMA((max(count_y, 1),))],
-        input_output_aliases={4 + i: i for i in range(count_y)},
-    )(za, zb, xa, xb, *y_send)
-    ys = swaps(ay, y_send[0], y_send[-1])[:count_y] if count_y else []
+        out_shape=(like(CHANNELS, rows, depth),)
+        + (like(2 * XMAIN + CHANNELS, W, depth),) * count_y,
+        in_specs=[VMEM] * 6 + [ANY] * count_y,
+    )(za, zb, xa, xb, ca, cb, *ys)
+    if count_y:
+        more_ys = swaps(ay, y_send[0], y_send[-1])[:count_y]
 
     vmem = lambda shapes: [pltpu.VMEM(shape, f32) for shape in shapes]
     flow = (3, total, rows, depth)
@@ -761,7 +724,7 @@
     solutions = [
         (3, count, height, depth) for height in (rows + 16, 16) for count in (total, 1) for _ in range(2)
     ]
-    before = 3 + count_y + 7
+    before = 3 + 2 * count_y + 7
     residual, update, *_ = call(
         functools.partial(finish, ay, count_y),
         "finish",
@@ -779,7 +742,7 @@
             ]
         ),
         input_output_aliases={before + i: 2 + i for i in range(len(edges))},
-    )(local, tabs, accum, *ys, *halves)
+    )(local, tabs, accum, *ys, *more_ys, *halves)
     return residual, update
 
 

time: 49.8 us -> 44.7 us (0.90)
  the two profiles are of different devices: /device:TPU:17 before, /device:TPU:16 now
where the time goes in v6:
time: 44.7 us; the launch traced here: 44.6 us
  Pallas kernels  22.9 us (51%)
  starting transfers between devices  11.4 us (26%)
  waiting for transfers between devices  9.62 us (22%)
  between operations  0.72 us (2%)
    ppermute x8, starting transfers between devices, swaps(): got.append(lax.ppermute(message, axis, pairs + [(b, a) for a, b in pairs]))  11.4 us
    pallas_call x1, Pallas kernels, body(): call(functools.partial(inner, ax), 'inner', 24, out_shape=[like(*shape) f...  10.4 us
    ppermute x8, waiting for transfers between devices, swaps(): got.append(lax.ppermute(message, axis, pairs + [(b, a) for a, b in pairs]))  9.62 us
    pallas_call x1, Pallas kernels, body(): call(functools.partial(finish, ay, count_y), 'finish', 24, out_shape=[cel...  9.46 us
    pallas_call x1, Pallas kernels, body(): call(functools.partial(pack_z, az), 'pack_z', 8, out_shape=(like(CHANNELS...  2.33 us
  transfers between devices with their start and end apart: 8, of which 3 were waited for; matrix products, arithmetic and copies ran while one was open for 0% of the time, Pallas kernels for 24%

profile of v6, /device:TPU:16, one launch (start us, length us, event | category | flops | bytes accessed | tf_op | source)
XLA Modules:
  0.0 44.6 jit_solution(13565187846806194037)
XLA Ops:
  0.6 2.3 %pack_z.1 = (f32[20,8,16,128]{3,2,1,0:T(8,128)S(1)}, f32[3,8,16,128]{3,2,1,0:T(8,128)S(1)}, f32[9,8,128]{2,1,0:T(8,128)S(1)}, f32[10,16,128]{2,1,0:T(8,128)S(1)}, f32[10,16,128]{2,1,0:T(8,128)S(1)}) custom-call(f32[3,8,16,128]{3,2,1,0:T(8,128)} %refs_0_.1, f32[3,8,16,128]{3,2,1,0:T(8,128)} %refs_1_.1, f32[8,16,128]{2,1,0:T(8,128)} %refs_2_.1, ...), custom_call_target="tpu_custom_call" | custom-call | tf_op jit(solution)/shard_map/pack_z/pallas_call | solution.py:665
  3.0 0.1 pack_x.1
  3.1 1.6 %collective-permute-start.3 = (f32[74,16,128]{2,1,0:T(8,128)S(1)}, f32[74,16,128]{2,1,0:T(8,128)S(1)}, u32[]{:S(2)}, u32[]{:S(2)}) collective-permute-start(f32[74,16,128]{2,1,0:T(8,128)S(1)} %get-tuple-element.39), channel_id=1, source_target_pairs={{0,8},{16,24},{8,0},{24,16},{1,9},{17,25},{9,1},{25,17},{2,10},{18... | collective-permute-start | bytes 1818632 | tf_op jit(solution)/shard_map/ppermute | solution.py:63
  4.7 1.9 %collective-permute-start.4 = (f32[74,16,128]{2,1,0:T(8,128)S(1)}, f32[74,16,128]{2,1,0:T(8,128)S(1)}, u32[]{:S(2)}, u32[]{:S(2)}) collective-permute-start(f32[74,16,128]{2,1,0:T(8,128)S(1)} %get-tuple-element.40), channel_id=1, source_target_pairs={{8,16},{16,8},{9,17},{17,9},{10,18},{18,10},{11,19},{19,11},{12,20... | collective-permute-start | bytes 1818632 | tf_op jit(solution)/shard_map/ppermute | solution.py:63
  6.6 0.1 collective-permute-start
  6.7 0.7 %collective-permute-start.1 = (f32[10,16,128]{2,1,0:T(8,128)S(1)}, f32[10,16,128]{2,1,0:T(8,128)S(1)}, u32[]{:S(2)}, u32[]{:S(2)}) collective-permute-start(f32[10,16,128]{2,1,0:T(8,128)S(1)} %get-tuple-element.37), channel_id=1, source_target_pairs={{1,2},{2,1},{5,6},{6,5},{9,10},{10,9},{13,14},{14,13},{17,18},{18,... | collective-permute-start | bytes 245768 | tf_op jit(solution)/shard_map/ppermute | solution.py:63
  7.4 0.6 %collective-permute-done.za = f32[10,16,128]{2,1,0:T(8,128)S(1)} collective-permute-done((f32[10,16,128]{2,1,0:T(8,128)S(1)}, f32[10,16,128]{2,1,0:T(8,128)S(1)}, u32[]{:S(2)}, u32[]{:S(2)}) %collective-permute-start) | collective-permute-done | bytes 81952 | tf_op jit(solution)/shard_map/ppermute | solution.py:63
  8.0 0.0 collective-permute-done.1.zb
  8.0 0.1 join_x.1
  8.1 1.6 %collective-permute-start.2 = (f32[160,4,128]{2,1,0:T(4,128)S(1)}, f32[160,4,128]{2,1,0:T(4,128)S(1)}, u32[]{:S(2)}, u32[]{:S(2)}) collective-permute-start(f32[160,4,128]{2,1,0:T(4,128)S(1)} %get-tuple-element.38), channel_id=1, source_target_pairs={{0,4},{4,0},{1,5},{5,1},{2,6},{6,2},{3,7},{7,3},{8,12},{12,8},{9,1... | collective-permute-start | bytes 983048 | tf_op jit(solution)/shard_map/ppermute | solution.py:63
  9.7 0.0 collective-permute-start.5
  9.7 3.9 %collective-permute-start.6 = (f32[5,16,128]{2,1,0:T(8,128)S(1)}, f32[5,16,128]{2,1,0:T(8,128)S(1)}, u32[]{:S(2)}, u32[]{:S(2)}) collective-permute-start(f32[5,16,128]{2,1,0:T(8,128)S(1)} %get-tuple-element.42), channel_id=1, source_target_pairs={{8,16},{16,8},{9,17},{17,9},{10,18},{18,10},{11,19},{19,11},{12,20... | collective-permute-start | bytes 122888 | tf_op jit(solution)/shard_map/ppermute | solution.py:63
  13.6 5.8 %collective-permute-done.5.ca = f32[5,16,128]{2,1,0:T(8,128)S(1)} collective-permute-done((f32[5,16,128]{2,1,0:T(8,128)S(1)}, f32[5,16,128]{2,1,0:T(8,128)S(1)}, u32[]{:S(2)}, u32[]{:S(2)}) %collective-permute-start.5) | collective-permute-done | bytes 40992 | tf_op jit(solution)/shard_map/ppermute | solution.py:63
  19.4 3.2 %collective-permute-done.6.cb = f32[5,16,128]{2,1,0:T(8,128)S(1)} collective-permute-done((f32[5,16,128]{2,1,0:T(8,128)S(1)}, f32[5,16,128]{2,1,0:T(8,128)S(1)}, u32[]{:S(2)}, u32[]{:S(2)}) %collective-permute-start.6) | collective-permute-done | bytes 40992 | tf_op jit(solution)/shard_map/ppermute | solution.py:63
  22.6 0.0 collective-permute-done.2.refs_0_.refs_2_
  22.6 0.0 collective-permute-done.3.xa
  22.6 0.0 collective-permute-done.4.xb
  22.6 0.4 join_y.1
  23.1 1.6 %collective-permute-start.7 = (f32[168,4,128]{2,1,0:T(4,128)S(1)}, f32[168,4,128]{2,1,0:T(4,128)S(1)}, u32[]{:S(2)}, u32[]{:S(2)}) collective-permute-start(f32[168,4,128]{2,1,0:T(4,128)S(1)} %get-tuple-element.43), channel_id=1, source_target_pairs={{0,4},{4,0},{1,5},{5,1},{2,6},{6,2},{3,7},{7,3},{8,12},{12,8},{9,1... | collective-permute-start | bytes 1032200 | tf_op jit(solution)/shard_map/ppermute | solution.py:63
  24.6 10.4 %inner.1 = (f32[26,16,16,128]{3,2,1,0:T(8,128)S(1)}, f32[16,16,128]{2,1,0:T(8,128)S(1)}, f32[16,16,128]{2,1,0:T(8,128)S(1)}, f32[26,1,16,128]{3,2,1,0:T(8,128)S(...) custom-call(f32[20,8,16,128]{3,2,1,0:T(8,128)S(1)} %get-tuple-elemen, ...), custom_call_target="tpu_custom_call" | custom-call | tf_op jit(solution)/shard_map/inner/pallas_call | solution.py:714
  35.1 0.0 collective-permute-done.7.refs_3_
  35.1 9.5 %finish.1 = (f32[3,8,16,128]{3,2,1,0:T(8,128)}, f32[8,16,128]{2,1,0:T(8,128)}, f32[8,3,16,16,128]{4,3,2,1,0:T(8,128)S(1)}, f32[13,16,16,128]{3,2,1,0:T(8,128)S(1...) custom-call(f32[20,8,16,128]{3,2,1,0:T(8,128)S(1)} %get-tuple-elemen, ...), custom_call_target="tpu_custom_call", output_to_operand_aliasing={{2}: (12, {}), {3}: (13, {}), {4}: (14, {}), {5}: (15, {}),... | custom-call | tf_op jit(solution)/shard_map/finish/pallas_call | solution.py:728
Async XLA Ops:
  3.1 19.5 %collective-permute-start.3 = (f32[74,16,128]{2,1,0:T(8,128)S(1)}, f32[74,16,128]{2,1,0:T(8,128)S(1)}, u32[]{:S(2)}, u32[]{:S(2)}) collective-permute-start(f32[74,16,128]{2,1,0:T(8,128)S(1)} %get-tuple-element.39), channel_id=1, source_target_pairs={{0,8},{16,24},{8,0},{24,16},{1,9},{17,25},{9,1},{25,17},{2,10},{18... | collective-permute-start | bytes 1818632 | tf_op jit(solution)/shard_map/ppermute | solution.py:63
  4.7 17.9 %collective-permute-start.4 = (f32[74,16,128]{2,1,0:T(8,128)S(1)}, f32[74,16,128]{2,1,0:T(8,128)S(1)}, u32[]{:S(2)}, u32[]{:S(2)}) collective-permute-start(f32[74,16,128]{2,1,0:T(8,128)S(1)} %get-tuple-element.40), channel_id=1, source_target_pairs={{8,16},{16,8},{9,17},{17,9},{10,18},{18,10},{11,19},{19,11},{12,20... | collective-permute-start | bytes 1818632 | tf_op jit(solution)/shard_map/ppermute | solution.py:63
  6.6 1.3 %collective-permute-start = (f32[10,16,128]{2,1,0:T(8,128)S(1)}, f32[10,16,128]{2,1,0:T(8,128)S(1)}, u32[]{:S(2)}, u32[]{:S(2)}) collective-permute-start(f32[10,16,128]{2,1,0:T(8,128)S(1)} %get-tuple-element.36), channel_id=1, source_target_pairs={{0,1},{2,3},{1,0},{3,2},{4,5},{6,7},{5,4},{7,6},{8,9},{10,11},{9,8... | collective-permute-start | bytes 245768 | tf_op jit(solution)/shard_map/ppermute | solution.py:63
  6.7 1.3 %collective-permute-start.1 = (f32[10,16,128]{2,1,0:T(8,128)S(1)}, f32[10,16,128]{2,1,0:T(8,128)S(1)}, u32[]{:S(2)}, u32[]{:S(2)}) collective-permute-start(f32[10,16,128]{2,1,0:T(8,128)S(1)} %get-tuple-element.37), channel_id=1, source_target_pairs={{1,2},{2,1},{5,6},{6,5},{9,10},{10,9},{13,14},{14,13},{17,18},{18,... | collective-permute-start | bytes 245768 | tf_op jit(solution)/shard_map/ppermute | solution.py:63
  8.1 14.5 %collective-permute-start.2 = (f32[160,4,128]{2,1,0:T(4,128)S(1)}, f32[160,4,128]{2,1,0:T(4,128)S(1)}, u32[]{:S(2)}, u32[]{:S(2)}) collective-permute-start(f32[160,4,128]{2,1,0:T(4,128)S(1)} %get-tuple-element.38), channel_id=1, source_target_pairs={{0,4},{4,0},{1,5},{5,1},{2,6},{6,2},{3,7},{7,3},{8,12},{12,8},{9,1... | collective-permute-start | bytes 983048 | tf_op jit(solution)/shard_map/ppermute | solution.py:63
  9.7 9.8 %collective-permute-start.5 = (f32[5,16,128]{2,1,0:T(8,128)S(1)}, f32[5,16,128]{2,1,0:T(8,128)S(1)}, u32[]{:S(2)}, u32[]{:S(2)}) collective-permute-start(f32[5,16,128]{2,1,0:T(8,128)S(1)} %get-tuple-element.41), channel_id=1, source_target_pairs={{0,8},{16,24},{8,0},{24,16},{1,9},{17,25},{9,1},{25,17},{2,10},{18... | collective-permute-start | bytes 122888 | tf_op jit(solution)/shard_map/ppermute | solution.py:63
  9.7 12.9 %collective-permute-start.6 = (f32[5,16,128]{2,1,0:T(8,128)S(1)}, f32[5,16,128]{2,1,0:T(8,128)S(1)}, u32[]{:S(2)}, u32[]{:S(2)}) collective-permute-start(f32[5,16,128]{2,1,0:T(8,128)S(1)} %get-tuple-element.42), channel_id=1, source_target_pairs={{8,16},{16,8},{9,17},{17,9},{10,18},{18,10},{11,19},{19,11},{12,20... | collective-permute-start | bytes 122888 | tf_op jit(solution)/shard_map/ppermute | solution.py:63
  23.1 12.0 %collective-permute-start.7 = (f32[168,4,128]{2,1,0:T(4,128)S(1)}, f32[168,4,128]{2,1,0:T(4,128)S(1)}, u32[]{:S(2)}, u32[]{:S(2)}) collective-permute-start(f32[168,4,128]{2,1,0:T(4,128)S(1)} %get-tuple-element.43), channel_id=1, source_target_pairs={{0,4},{4,0},{1,5},{5,1},{2,6},{6,2},{3,7},{7,3},{8,12},{12,8},{9,1... | collective-permute-start | bytes 1032200 | tf_op jit(solution)/shard_map/ppermute | solution.py:63

commit v7 on v6

--- a/solution.py
+++ b/solution.py
@@ -206,12 +206,10 @@
     rows, depth = xa.shape[1:]
     even = parity_of(axis)
     even_x = parity_of(x_axis)
-    per, _ = groups_of(planes, depth)
     per_x, _ = groups_of(W, depth)
     lane = lanes_of((rows, depth))
     for c in range(CHANNELS):
-        group, base = c // per, (c % per) * span_of(planes)
-        own = pltpu.roll(za[group] + zb[group], (2 * W * W - base) % depth, 1)
+        own = own_columns(c, za, zb, planes, slice(0, rows))
         group, base = c // per_x, (c % per_x) * span_of(W)
         a, b = ca[group], cb[group]
         below = pltpu.roll(pick(even_x, b, a), (depth - base) % depth, 1)
@@ -346,39 +344,91 @@
     return flux
 
 
-def inner(x_axis, local, columns, xa, xb, *refs):
-    tabs, results, halo_results, store = refs[0], refs[1:4], refs[4:7], refs[7]
-    edges, arrays, halo, centre = refs[8:18], refs[18:23], refs[23:28], refs[28]
-    planes, rows, depth = local.shape[1:]
-    total = planes + 2 * W
-    even_x = parity_of(x_axis)
-    tiles = range(rows // 8)
-
+def row_cells(tiles, tabs, arrays, halo, centre):
     def cells(get, plane, is_columns=False):
-        for tile in tiles:
-            span = slice(8 * tile, 8 * tile + 8)
-            to = slice(8 + 8 * tile, 16 + 8 * tile)
+        for tile in range(tiles):
+            span, to = slice(8 * tile, 8 * tile + 8), slice(8 + 8 * tile, 16 + 8 * tile)
 
             def put(ref, lead, values, change=None):
                 at = (*lead, to, slice(None))
                 ref[at] = values if change is None else change(ref[at])
 
-            properties(lambda c: get(c, span), plane, is_columns, put, tabs, arrays, halo, centre, span)
-
-    cells(lambda c, span: columns[c, span, :], 0, True)
+            properties(
+                lambda c: get(c, span), plane, is_columns, put, tabs, arrays, halo, centre, span
+            )
+
+    return cells
+
+
+def row_links(tiles, plane, is_columns, arrays, results, store=None):
+    for tile in range(tiles):
+        out = slice(8 * tile, 8 * tile + 8)
+        flow = link_cells(plane, is_columns, 8 + 8 * tile, 1, arrays, out, results)
+        if store is not None:
+            for c in range(3):
+                store[c, plane, out, :] = flow[c]
+
+
+def own_columns(c, za, zb, planes, span):
+    depth = za.shape[-1]
+    per, _ = groups_of(planes, depth)
+    group, base = c // per, (c % per) * span_of(planes)
+    return pltpu.roll(za[group, span, :] + zb[group, span, :], (2 * W * W - base) % depth, 1)
+
+
+def among_own(planes, shape):
+    lane = lanes_of(shape)
+    return (lane >= 2 * W * W) & (lane < 2 * W * (W + planes))
+
+
+def inner_local(local, za, zb, tabs, *refs):
+    arrays, results, store, parts = refs[:5], refs[5:8], refs[8], refs[9:11]
+    halo, centre = (*parts, *refs[11:14]), refs[14]
+    planes, rows, depth = local.shape[1:]
+    tiles = rows // 8
+    cells = row_cells(tiles, tabs, arrays, halo, centre)
+
+    def columns(c, span):
+        values = own_columns(c, za, zb, planes, span)
+        return jnp.where(among_own(planes, values.shape), values, 0.0)
+
+    cells(columns, 0, True)
 
     @pl.loop(0, planes)
     def _(x):
         cells(lambda c, span: local[c, x, span, :], W + x)
 
+    @pl.loop(W + 1, W + planes - 1)
+    def _(plane):
+        row_links(tiles, plane, False, arrays, results, store)
+
+
+def inner(x_axis, planes, columns, xa, xb, tabs, *refs):
+    parts, refs = refs[:2], refs[11:]
+    results, halo_results, store = refs[:3], refs[3:6], refs[6]
+    edges, arrays, halo, centre = refs[7:17], refs[17:22], refs[22:27], refs[27]
+    rows, depth = xa.shape[1:]
+    total = planes + 2 * W
+    even_x = parity_of(x_axis)
+    tiles = rows // 8
+    cells = row_cells(tiles, tabs, arrays, halo, centre)
+
+    cells(lambda c, span: columns[c, span, :], 0, True)
+    own = among_own(planes, (8, depth))
+    for array, part in zip(halo, parts):
+        for lead in itertools.product(*(range(n) for n in part.shape[:-2])):
+            for tile in range(tiles):
+                at = (*lead, slice(8 + 8 * tile, 16 + 8 * tile), slice(None))
+                array[at] = jnp.where(own, part[at], array[at])
+
     def from_x(n, low):
-        a, b = xa, xb
         def get(c, span):
             i = n(c)
             if i is None:
                 return jnp.zeros((8, depth), f32)
             u, v = xa[i, span, :], xb[i, span, :]
             return pick(even_x, v, u) if low else pick(even_x, u, v)
+
         return get
 
     @pl.loop(0, NEAR)
@@ -405,20 +455,12 @@
     def _(plane):
         hand_on(arrays, edges[:5], plane)
 
-    def links(plane, is_columns=False):
-        for tile in tiles:
-            out = slice(8 * tile, 8 * tile + 8)
-            own = (halo, out, halo_results) if is_columns else (arrays, out, results)
-            res = link_cells(plane, is_columns, 8 + 8 * tile, 1, *own)
-            if not is_columns:
-                for c in range(3):
-                    store[c, plane, out, :] = res[c]
-
-    links(0, True)
-
-    @pl.loop(1, total - 1)
-    def _(plane):
-        links(plane)
+    row_links(tiles, 0, True, halo, halo_results)
+
+    @pl.loop(0, W)
+    def _(n):
+        row_links(tiles, 1 + n, False, arrays, results, store)
+        row_links(tiles, W + planes - 1 + n, False, arrays, results, store)
 
 
 RING = 2 * (W + 2)
@@ -696,30 +738,46 @@
     ca, cb = fill(c_shape, swaps(ax, *c_send))
     if count_y:
         ys = swaps(ay, y_send[0], y_send[-1])[:count_y]
+    vmem = lambda shapes: [pltpu.VMEM(shape, f32) for shape in shapes]
+    flow = (3, total, rows, depth)
+    tall = cell_shapes(total, rows + 16, depth)
+    wide = result_shapes(total, rows, depth)
+    centre = (SHIFTED + UP, rows, depth)
+    shapes = tall[:5] + wide[:3] + [flow] + tall[5:7]
+    found = call(
+        inner_local,
+        "inner_local",
+        16,
+        out_shape=[like(*shape) for shape in shapes],
+        in_specs=[VMEM] * 4,
+        out_specs=[VMEM] * len(shapes),
+        scratch_shapes=vmem(tall[7:] + [centre]),
+    )(local, za, zb, tabs)
+    arrays, found, parts = found[:5], found[5:9], found[9:]
+
     columns, *y_send = call(
         functools.partial(join_y, ay, ax, planes),
         "join_y",
         8,
         out_shape=(like(CHANNELS, rows, depth),)
         + (like(2 * XMAIN + CHANNELS, W, depth),) * count_y,
-        in_specs=[VMEM] * 6 + [ANY] * count_y,
-    )(za, zb, xa, xb, ca, cb, *ys)
+        in_specs=[VMEM] * 6 + [ANY] * (count_y + 1),
+    )(za, zb, xa, xb, ca, cb, *ys, parts[1])
     if count_y:
         more_ys = swaps(ay, y_send[0], y_send[-1])[:count_y]
 
-    vmem = lambda shapes: [pltpu.VMEM(shape, f32) for shape in shapes]
-    flow = (3, total, rows, depth)
     edges = cell_shapes(total, 16, depth)
-    shapes = result_shapes(total, rows, depth) + [flow] + edges
+    shapes = wide + [flow] + edges + tall[:5]
     halves = call(
-        functools.partial(inner, ax),
+        functools.partial(inner, ax, planes),
         "inner",
-        24,
+        16,
         out_shape=[like(*shape) for shape in shapes],
-        in_specs=[VMEM] * 5,
+        in_specs=[VMEM] * 15,
         out_specs=[VMEM] * len(shapes),
-        scratch_shapes=vmem(cell_shapes(total, rows + 16, depth) + [(SHIFTED + UP, rows, depth)]),
-    )(local, columns, xa, xb, tabs)
+        scratch_shapes=vmem(tall[5:] + [centre]),
+        input_output_aliases={6: 0, 7: 1, 8: 2, 9: 6, **{10 + i: 17 + i for i in range(5)}},
+    )(columns, xa, xb, tabs, *parts, *found, *arrays)[:17]
 
     solutions = [
         (3, count, height, depth) for height in (rows + 16, 16) for count in (total, 1) for _ in range(2)

time: 44.7 us -> 43 us (0.962)
  the two profiles are of different devices: /device:TPU:16 before, /device:TPU:17 now
where the time goes in v7:
time: 43 us; the launch traced here: 42.4 us
  Pallas kernels  23 us (53%)
  starting transfers between devices  12.5 us (29%)
  waiting for transfers between devices  6.2 us (14%)
  between operations  0.75 us (2%)
    ppermute x8, starting transfers between devices, swaps(): got.append(lax.ppermute(message, axis, pairs + [(b, a) for a, b in pairs]))  12.5 us
    pallas_call x1, Pallas kernels, body(): call(functools.partial(finish, ay, count_y), 'finish', 24, out_shape=[cel...  9.4 us
    ppermute x8, waiting for transfers between devices, swaps(): got.append(lax.ppermute(message, axis, pairs + [(b, a) for a, b in pairs]))  6.2 us
    pallas_call x1, Pallas kernels, body(): call(functools.partial(inner, ax, planes), 'inner', 16, out_shape=[like(*...  6.03 us
    pallas_call x1, Pallas kernels, body(): call(inner_local, 'inner_local', 16, out_shape=[like(*shape) for shape in...  4.58 us
    pallas_call x1, Pallas kernels, body(): call(functools.partial(pack_z, az), 'pack_z', 8, out_shape=(like(CHANNELS...  2.33 us
  transfers between devices with their start and end apart: 8, of which 2 were waited for; matrix products, arithmetic and copies ran while one was open for 0% of the time, Pallas kernels for 25%

profile of v7, /device:TPU:17, one launch (start us, length us, event | category | flops | bytes accessed | tf_op | source)
XLA Modules:
  0.0 42.4 jit_solution(505625065591014681)
XLA Ops:
  0.6 2.3 %pack_z.1 = (f32[20,8,16,128]{3,2,1,0:T(8,128)S(1)}, f32[3,8,16,128]{3,2,1,0:T(8,128)S(1)}, f32[9,8,128]{2,1,0:T(8,128)S(1)}, f32[10,16,128]{2,1,0:T(8,128)S(1)}, f32[10,16,128]{2,1,0:T(8,128)S(1)}) custom-call(f32[3,8,16,128]{3,2,1,0:T(8,128)} %refs_0_.1, f32[3,8,16,128]{3,2,1,0:T(8,128)} %refs_1_.1, f32[8,16,128]{2,1,0:T(8,128)} %refs_2_.1, ...), custom_call_target="tpu_custom_call" | custom-call | tf_op jit(solution)/shard_map/pack_z/pallas_call | solution.py:707
  3.0 0.1 pack_x.1
  3.1 1.4 %collective-permute-start.3 = (f32[74,16,128]{2,1,0:T(8,128)S(1)}, f32[74,16,128]{2,1,0:T(8,128)S(1)}, u32[]{:S(2)}, u32[]{:S(2)}) collective-permute-start(f32[74,16,128]{2,1,0:T(8,128)S(1)} %get-tuple-element.50), channel_id=1, source_target_pairs={{0,8},{16,24},{8,0},{24,16},{1,9},{17,25},{9,1},{25,17},{2,10},{18... | collective-permute-start | bytes 1818632 | tf_op jit(solution)/shard_map/ppermute | solution.py:63
  4.4 1.9 %collective-permute-start.4 = (f32[74,16,128]{2,1,0:T(8,128)S(1)}, f32[74,16,128]{2,1,0:T(8,128)S(1)}, u32[]{:S(2)}, u32[]{:S(2)}) collective-permute-start(f32[74,16,128]{2,1,0:T(8,128)S(1)} %get-tuple-element.51), channel_id=1, source_target_pairs={{8,16},{16,8},{9,17},{17,9},{10,18},{18,10},{11,19},{19,11},{12,20... | collective-permute-start | bytes 1818632 | tf_op jit(solution)/shard_map/ppermute | solution.py:63
  6.4 1.0 %collective-permute-start = (f32[10,16,128]{2,1,0:T(8,128)S(1)}, f32[10,16,128]{2,1,0:T(8,128)S(1)}, u32[]{:S(2)}, u32[]{:S(2)}) collective-permute-start(f32[10,16,128]{2,1,0:T(8,128)S(1)} %get-tuple-element.47), channel_id=1, source_target_pairs={{0,1},{2,3},{1,0},{3,2},{4,5},{6,7},{5,4},{7,6},{8,9},{10,11},{9,8... | collective-permute-start | bytes 245768 | tf_op jit(solution)/shard_map/ppermute | solution.py:63
  7.4 3.0 %collective-permute-start.1 = (f32[10,16,128]{2,1,0:T(8,128)S(1)}, f32[10,16,128]{2,1,0:T(8,128)S(1)}, u32[]{:S(2)}, u32[]{:S(2)}) collective-permute-start(f32[10,16,128]{2,1,0:T(8,128)S(1)} %get-tuple-element.48), channel_id=1, source_target_pairs={{1,2},{2,1},{5,6},{6,5},{9,10},{10,9},{13,14},{14,13},{17,18},{18,... | collective-permute-start | bytes 245768 | tf_op jit(solution)/shard_map/ppermute | solution.py:63
  10.4 0.0 collective-permute-done.za
  10.4 3.0 %collective-permute-done.1.zb = f32[10,16,128]{2,1,0:T(8,128)S(1)} collective-permute-done((f32[10,16,128]{2,1,0:T(8,128)S(1)}, f32[10,16,128]{2,1,0:T(8,128)S(1)}, u32[]{:S(2)}, u32[]{:S(2)}) %collective-permute-start.1) | collective-permute-done | bytes 81952 | tf_op jit(solution)/shard_map/ppermute | solution.py:63
  13.4 0.1 join_x.1
  13.5 1.3 %collective-permute-start.2 = (f32[160,4,128]{2,1,0:T(4,128)S(1)}, f32[160,4,128]{2,1,0:T(4,128)S(1)}, u32[]{:S(2)}, u32[]{:S(2)}) collective-permute-start(f32[160,4,128]{2,1,0:T(4,128)S(1)} %get-tuple-element.49), channel_id=1, source_target_pairs={{0,4},{4,0},{1,5},{5,1},{2,6},{6,2},{3,7},{7,3},{8,12},{12,8},{9,1... | collective-permute-start | bytes 983048 | tf_op jit(solution)/shard_map/ppermute | solution.py:63
  14.8 0.0 collective-permute-start.5
  14.8 3.6 %collective-permute-start.6 = (f32[5,16,128]{2,1,0:T(8,128)S(1)}, f32[5,16,128]{2,1,0:T(8,128)S(1)}, u32[]{:S(2)}, u32[]{:S(2)}) collective-permute-start(f32[5,16,128]{2,1,0:T(8,128)S(1)} %get-tuple-element.53), channel_id=1, source_target_pairs={{8,16},{16,8},{9,17},{17,9},{10,18},{18,10},{11,19},{19,11},{12,20... | collective-permute-start | bytes 122888 | tf_op jit(solution)/shard_map/ppermute | solution.py:63
  18.5 4.6 %inner_local.1 = (f32[8,3,16,32,128]{4,3,2,1,0:T(8,128)S(1)}, f32[13,16,32,128]{3,2,1,0:T(8,128)S(1)}, f32[13,16,32,128]{3,2,1,0:T(8,128)S(1)}, f32[3,16,32,128]...) custom-call(f32[20,8,16,128]{3,2,1,0:T(8,128)S(1)} %get-tuple-elemen, ...), custom_call_target="tpu_custom_call" | custom-call | tf_op jit(solution)/shard_map/inner_local/pallas_call | solution.py:747
  23.1 0.0 collective-permute-done.5.ca
  23.1 0.0 collective-permute-done.6.cb
  23.1 0.0 collective-permute-done.2.refs_0_.refs_2_
  23.1 0.0 collective-permute-done.3.xa
  23.1 0.0 collective-permute-done.4.xb
  23.1 0.4 join_y.1
  23.5 0.3 collective-permute-start.7
  23.8 6.0 %inner.1 = (f32[26,16,16,128]{3,2,1,0:T(8,128)S(1)}, f32[16,16,128]{2,1,0:T(8,128)S(1)}, f32[16,16,128]{2,1,0:T(8,128)S(1)}, f32[26,1,16,128]{3,2,1,0:T(8,128)S(...) custom-call(f32[20,16,128]{2,1,0:T(8,128)S(1)} %get-tuple-element.56, ...), custom_call_target="tpu_custom_call", output_to_operand_aliasing={{0}: (6, {}), {1}: (7, {}), {2}: (8, {}), {6}: (9, {}), {17... | custom-call | tf_op jit(solution)/shard_map/inner/pallas_call | solution.py:771
  29.9 3.2 %collective-permute-done.7.refs_3_ = f32[168,4,128]{2,1,0:T(4,128)S(1)} collective-permute-done((f32[168,4,128]{2,1,0:T(4,128)S(1)}, f32[168,4,128]{2,1,0:T(4,128)S(1)}, u32[]{:S(2)}, u32[]{:S(2)}) %collective-permute-start.7) | collective-permute-done | bytes 344096 | tf_op jit(solution)/shard_map/ppermute | solution.py:63
  33.0 9.4 %finish.1 = (f32[3,8,16,128]{3,2,1,0:T(8,128)}, f32[8,16,128]{2,1,0:T(8,128)}, f32[8,3,16,16,128]{4,3,2,1,0:T(8,128)S(1)}, f32[13,16,16,128]{3,2,1,0:T(8,128)S(1...) custom-call(f32[20,8,16,128]{3,2,1,0:T(8,128)S(1)} %get-tuple-elemen, ...), custom_call_target="tpu_custom_call", output_to_operand_aliasing={{2}: (12, {}), {3}: (13, {}), {4}: (14, {}), {5}: (15, {}),... | custom-call | tf_op jit(solution)/shard_map/finish/pallas_call | solution.py:786
Async XLA Ops:
  3.1 20.0 %collective-permute-start.3 = (f32[74,16,128]{2,1,0:T(8,128)S(1)}, f32[74,16,128]{2,1,0:T(8,128)S(1)}, u32[]{:S(2)}, u32[]{:S(2)}) collective-permute-start(f32[74,16,128]{2,1,0:T(8,128)S(1)} %get-tuple-element.50), channel_id=1, source_target_pairs={{0,8},{16,24},{8,0},{24,16},{1,9},{17,25},{9,1},{25,17},{2,10},{18... | collective-permute-start | bytes 1818632 | tf_op jit(solution)/shard_map/ppermute | solution.py:63
  4.4 18.7 %collective-permute-start.4 = (f32[74,16,128]{2,1,0:T(8,128)S(1)}, f32[74,16,128]{2,1,0:T(8,128)S(1)}, u32[]{:S(2)}, u32[]{:S(2)}) collective-permute-start(f32[74,16,128]{2,1,0:T(8,128)S(1)} %get-tuple-element.51), channel_id=1, source_target_pairs={{8,16},{16,8},{9,17},{17,9},{10,18},{18,10},{11,19},{19,11},{12,20... | collective-permute-start | bytes 1818632 | tf_op jit(solution)/shard_map/ppermute | solution.py:63
  6.4 4.0 %collective-permute-start = (f32[10,16,128]{2,1,0:T(8,128)S(1)}, f32[10,16,128]{2,1,0:T(8,128)S(1)}, u32[]{:S(2)}, u32[]{:S(2)}) collective-permute-start(f32[10,16,128]{2,1,0:T(8,128)S(1)} %get-tuple-element.47), channel_id=1, source_target_pairs={{0,1},{2,3},{1,0},{3,2},{4,5},{6,7},{5,4},{7,6},{8,9},{10,11},{9,8... | collective-permute-start | bytes 245768 | tf_op jit(solution)/shard_map/ppermute | solution.py:63
  7.4 6.0 %collective-permute-start.1 = (f32[10,16,128]{2,1,0:T(8,128)S(1)}, f32[10,16,128]{2,1,0:T(8,128)S(1)}, u32[]{:S(2)}, u32[]{:S(2)}) collective-permute-start(f32[10,16,128]{2,1,0:T(8,128)S(1)} %get-tuple-element.48), channel_id=1, source_target_pairs={{1,2},{2,1},{5,6},{6,5},{9,10},{10,9},{13,14},{14,13},{17,18},{18,... | collective-permute-start | bytes 245768 | tf_op jit(solution)/shard_map/ppermute | solution.py:63
  13.5 9.6 %collective-permute-start.2 = (f32[160,4,128]{2,1,0:T(4,128)S(1)}, f32[160,4,128]{2,1,0:T(4,128)S(1)}, u32[]{:S(2)}, u32[]{:S(2)}) collective-permute-start(f32[160,4,128]{2,1,0:T(4,128)S(1)} %get-tuple-element.49), channel_id=1, source_target_pairs={{0,4},{4,0},{1,5},{5,1},{2,6},{6,2},{3,7},{7,3},{8,12},{12,8},{9,1... | collective-permute-start | bytes 983048 | tf_op jit(solution)/shard_map/ppermute | solution.py:63
  14.8 8.2 %collective-permute-start.5 = (f32[5,16,128]{2,1,0:T(8,128)S(1)}, f32[5,16,128]{2,1,0:T(8,128)S(1)}, u32[]{:S(2)}, u32[]{:S(2)}) collective-permute-start(f32[5,16,128]{2,1,0:T(8,128)S(1)} %get-tuple-element.52), channel_id=1, source_target_pairs={{0,8},{16,24},{8,0},{24,16},{1,9},{17,25},{9,1},{25,17},{2,10},{18... | collective-permute-start | bytes 122888 | tf_op jit(solution)/shard_map/ppermute | solution.py:63
  14.8 8.2 %collective-permute-start.6 = (f32[5,16,128]{2,1,0:T(8,128)S(1)}, f32[5,16,128]{2,1,0:T(8,128)S(1)}, u32[]{:S(2)}, u32[]{:S(2)}) collective-permute-start(f32[5,16,128]{2,1,0:T(8,128)S(1)} %get-tuple-element.53), channel_id=1, source_target_pairs={{8,16},{16,8},{9,17},{17,9},{10,18},{18,10},{11,19},{19,11},{12,20... | collective-permute-start | bytes 122888 | tf_op jit(solution)/shard_map/ppermute | solution.py:63
  23.5 9.5 %collective-permute-start.7 = (f32[168,4,128]{2,1,0:T(4,128)S(1)}, f32[168,4,128]{2,1,0:T(4,128)S(1)}, u32[]{:S(2)}, u32[]{:S(2)}) collective-permute-start(f32[168,4,128]{2,1,0:T(4,128)S(1)} %get-tuple-element.55), channel_id=1, source_target_pairs={{0,4},{4,0},{1,5},{5,1},{2,6},{6,2},{3,7},{7,3},{8,12},{12,8},{9,1... | collective-permute-start | bytes 1032200 | tf_op jit(solution)/shard_map/ppermute | solution.py:63

commit v8 on v7

--- a/solution.py
+++ b/solution.py
@@ -182,6 +182,8 @@
     for c in range(CHANNELS):
         for x in range(planes):
             put_rows(outs[2:], c * planes + x, local[c, x], even_y)
+    for group in range(za.shape[0]):
+        put_rows(outs[2:], CHANNELS * planes + group, za[group] + zb[group], even_y)
     rows, depth = za.shape[1:]
     even = parity_of(axis)
     per, _ = groups_of(planes, depth)
@@ -254,7 +256,7 @@
     return jnp.where(lane == at, pltpu.roll(values, at + 1, 1), current)
 
 
-def properties(get, plane, is_columns, put, tabs, arrays, halo, centre, span):
+def properties(get, plane, is_columns, put, tabs, arrays, halo, centre, span, done=None):
     fields, lower, half, weight, base = halo if is_columns else arrays
     halo_fields, halo_lower = halo[:2]
     press, water, gas, active, region = (get(c) for c in range(5))
@@ -284,7 +286,12 @@
     for array, lead, step, values, slot in shifts:
         if is_columns:
             centre[slot, span, :] = values
-            put((fields, lower)[array], (*lead, 0), z_shift_columns(values, step))
+            shifted = z_shift_columns(values, step)
+            if done is None:
+                put((fields, lower)[array], (*lead, 0), shifted)
+            else:
+                keep = lambda now: jnp.where(done, now, shifted)
+                put((fields, lower)[array], (*lead, 0), None, keep)
         else:
             put((fields, lower)[array], (*lead, plane), z_shift(values, centre[slot, span, :], plane, step))
             put((halo_fields, halo_lower)[array], (*lead, 0), None, lambda now: z_edge(now, values, plane, step))
@@ -466,79 +473,115 @@
 RING = 2 * (W + 2)
 
 
+def put_ring(ref, lead, values, change=None):
+    low = (*lead, pl.ds(1, W, stride=2), slice(None))
+    high = (*lead, pl.ds(4, W, stride=2), slice(None))
+    if change is not None:
+        values = change(jnp.concatenate([ref[low], ref[high]], axis=0))
+    ref[low] = values[:W]
+    ref[high] = values[W:]
+
+
+def halo_rows(even_y, sources, n, target, at):
+    shape = target.shape[-1:]
+    low = high = jnp.zeros((W, *shape), f32)
+    if sources:
+        a = sources[0][n]
+        b = sources[1][n] if len(sources) > 1 else None
+        low, high = pick(even_y, b, a), pick(even_y, a, b)
+    target[(*at, slice(0, W), slice(None))] = low
+    target[(*at, slice(W, 2 * W), slice(None))] = high
+
+
+def ring_links(plane, is_columns, arrays, results, store):
+    flow = link_cells(plane, is_columns, 2, 2, arrays, slice(0, 8), results)
+    if not is_columns:
+        for c in range(3):
+            store[c, plane] = flow[c]
+
+
+def finish_local(axis, count_y, planes, tabs, *refs):
+    ys, refs = refs[:count_y], refs[count_y + 10 :]
+    arrays, halo, results, store = refs[:5], refs[5:10], refs[10:13], refs[13]
+    raw, packed, centre = refs[14:]
+    depth = raw.shape[-1]
+    even_y = parity_of(axis)
+    per, groups = groups_of(planes, depth)
+    for group in range(groups):
+        halo_rows(even_y, ys, CHANNELS * planes + group, packed, (group,))
+
+    @pl.loop(0, CHANNELS)
+    def _(c):
+        for x in range(planes):
+            halo_rows(even_y, ys, c * planes + x, raw, (c, x))
+
+    def cells(get, plane, is_columns=False):
+        span = slice(0, 2 * W)
+        properties(get, plane, is_columns, put_ring, tabs, arrays, halo, centre, span)
+
+    own = among_own(planes, (2 * W, depth))
+
+    def columns(c):
+        base = (c % per) * span_of(planes)
+        return jnp.where(own, pltpu.roll(packed[c // per], (2 * W * W - base) % depth, 1), 0.0)
+
+    cells(columns, 0, True)
+
+    @pl.loop(0, planes, unroll=2)
+    def _(x):
+        cells(lambda c: raw[c, x], W + x)
+
+    @pl.loop(W + 1, W + planes - 1)
+    def _(plane):
+        ring_links(plane, False, arrays, results, store)
+
+
 def finish(axis, count_y, local, *refs):
-    tabs, accum, ys, more_ys = refs[0], refs[1], refs[2 : 2 + count_y], refs[2 + count_y : 2 + 2 * count_y]
-    refs = refs[2 + 2 * count_y :]
+    tabs, accum, more_ys, refs = refs[0], refs[1], refs[2 : 2 + count_y], refs[2 + count_y :]
     results, halo_results, store = refs[:3], refs[3:6], refs[6]
-    residual, update = refs[17:19]
-    arrays, halo = refs[19:24], refs[24:29]
-    edge_store, raw, centre = refs[29:32]
-    edge_results, edge_halo_results = refs[32:35], refs[35:38]
-    sols, halo_sols, edge_sols, edge_halo_sols = (refs[38 + 2 * i : 40 + 2 * i] for i in range(4))
+    residual, update = refs[21:23]
+    arrays, halo = refs[23:28], refs[28:33]
+    edge_results, edge_store = refs[33:36], refs[36]
+    raw, centre, edge_halo_results = refs[37], refs[38], refs[39:42]
+    sols, halo_sols, edge_sols, edge_halo_sols = (refs[42 + 2 * i : 44 + 2 * i] for i in range(4))
     planes, rows, depth = local.shape[1:]
     total = planes + 2 * W
     even_y = parity_of(axis)
 
-    def halo_rows(c, plane, sources, n):
-        low = high = jnp.zeros((W, depth), f32)
-        if count_y:
-            a = sources[0][n]
-            b = sources[1][n] if count_y > 1 else None
-            low, high = pick(even_y, b, a), pick(even_y, a, b)
-        raw[c, plane, 0:W, :] = low
-        raw[c, plane, W : 2 * W, :] = high
-
     @pl.loop(0, CHANNELS)
     def _(c):
-        for x in range(planes):
-            halo_rows(c, W + x, ys, c * planes + x)
         for q in range(NEAR):
-            halo_rows(c, 1 + q, more_ys, c * NEAR + q)
-            halo_rows(c, W + planes + q, more_ys, XMAIN + c * NEAR + q)
-        halo_rows(c, total, more_ys, 2 * XMAIN + c)
+            halo_rows(even_y, more_ys, c * NEAR + q, raw, (c, 1 + q))
+            halo_rows(even_y, more_ys, XMAIN + c * NEAR + q, raw, (c, W + q))
+        halo_rows(even_y, more_ys, 2 * XMAIN + c, raw, (c, 2 * W))
 
     @pl.loop(0, FAR)
     def _(c):
-        halo_rows(c, 0, more_ys, CHANNELS * NEAR + c)
-        halo_rows(c, total - 1, more_ys, XMAIN + CHANNELS * NEAR + c)
+        halo_rows(even_y, more_ys, CHANNELS * NEAR + c, raw, (c, 0))
+        halo_rows(even_y, more_ys, XMAIN + CHANNELS * NEAR + c, raw, (c, 2 * W - 1))
 
     for c in range(FAR, CHANNELS):
-        for plane in (0, total - 1):
-            raw[c, plane] = jnp.zeros((2 * W, depth), f32)
-
-    def cells(plane, is_columns=False):
-        def put(ref, lead, values, change=None):
-            low = (*lead, pl.ds(1, W, stride=2), slice(None))
-            high = (*lead, pl.ds(4, W, stride=2), slice(None))
-            if change is not None:
-                values = change(jnp.concatenate([ref[low], ref[high]], axis=0))
-            ref[low] = values[:W]
-            ref[high] = values[W:]
-
-        get = lambda c: raw[c, plane, :, :]
-        properties(
-            get, 0 if is_columns else plane, is_columns, put, tabs, arrays, halo, centre, slice(0, 8)
-        )
-
-    cells(total, True)
-
-    @pl.loop(0, total, unroll=2)
-    def _(plane):
-        cells(plane)
-
-    def links(plane, is_columns=False):
-        out = slice(0, 8)
-        own = (halo, out, edge_halo_results) if is_columns else (arrays, out, edge_results)
-        res = link_cells(plane, is_columns, 2, 2, *own)
-        if not is_columns:
-            for c in range(3):
-                edge_store[c, plane] = res[c]
-
-    links(0, True)
-
-    @pl.loop(1, total - 1)
-    def _(plane):
-        links(plane)
+        for slot in (0, 2 * W - 1):
+            raw[c, slot] = jnp.zeros((2 * W, depth), f32)
+
+    def cells(slot, plane, is_columns=False):
+        done = among_own(planes, (2 * W, depth)) if is_columns else None
+        get, span = lambda c: raw[c, slot], slice(0, 2 * W)
+        properties(get, plane, is_columns, put_ring, tabs, arrays, halo, centre, span, done)
+
+    cells(2 * W, 0, True)
+
+    @pl.loop(0, W)
+    def _(n):
+        cells(n, n)
+        cells(W + n, W + planes + n)
+
+    ring_links(0, True, halo, edge_halo_results, None)
+
+    @pl.loop(0, W)
+    def _(n):
+        ring_links(1 + n, False, arrays, edge_results, edge_store)
+        ring_links(W + planes - 1 + n, False, arrays, edge_results, edge_store)
 
     tiles = rows // 8
 
@@ -732,7 +775,7 @@
         functools.partial(join_x, ax, ay),
         "join_x",
         8,
-        out_shape=(c_shape, c_shape) + (like(CHANNELS * planes, W, depth),) * count_y,
+        out_shape=(c_shape, c_shape) + (like(CHANNELS * planes + groups, W, depth),) * count_y,
     )(za, zb, local)
     c_send, y_send = sent[:2], sent[2:]
     ca, cb = fill(c_shape, swaps(ax, *c_send))
@@ -782,25 +825,42 @@
     solutions = [
         (3, count, height, depth) for height in (rows + 16, 16) for count in (total, 1) for _ in range(2)
     ]
-    before = 3 + 2 * count_y + 7
+    edge_shapes = result_shapes(total, 2 * W, depth)
+    shapes = edges + edge_shapes[:3] + [(3, total, 2 * W, depth)]
+    found = call(
+        functools.partial(finish_local, ay, count_y, planes),
+        "finish_local",
+        16,
+        out_shape=[like(*shape) for shape in shapes],
+        in_specs=[VMEM] * (1 + count_y + 10),
+        out_specs=[VMEM] * len(shapes),
+        scratch_shapes=vmem(
+            [
+                (CHANNELS, planes, 2 * W, depth),
+                (groups, 2 * W, depth),
+                (SHIFTED + UP, 2 * W, depth),
+            ]
+        ),
+        input_output_aliases={1 + count_y + i: i for i in range(10)},
+    )(tabs, *ys, *halves[7:])
+    before = 3 + count_y + 7
     residual, update, *_ = call(
         functools.partial(finish, ay, count_y),
         "finish",
-        24,
-        out_shape=[cells, like(planes, rows, depth)] + [like(*shape) for shape in edges],
-        in_specs=[VMEM] * (before + len(edges)),
-        out_specs=[VMEM] * (2 + len(edges)),
+        16,
+        out_shape=[cells, like(planes, rows, depth)] + [like(*shape) for shape in shapes],
+        in_specs=[VMEM] * (before + len(shapes)),
+        out_specs=[VMEM] * (2 + len(shapes)),
         scratch_shapes=vmem(
             [
-                (3, total, 8, depth),
-                (CHANNELS, total + 1, 2 * W, depth),
+                (CHANNELS, 2 * W + 1, 2 * W, depth),
                 (SHIFTED + UP, 2 * W, depth),
-                *result_shapes(total, 8, depth),
+                *edge_shapes[3:],
                 *solutions,
             ]
         ),
-        input_output_aliases={before + i: 2 + i for i in range(len(edges))},
-    )(local, tabs, accum, *ys, *more_ys, *halves)
+        input_output_aliases={before + i: 2 + i for i in range(len(shapes))},
+    )(local, tabs, accum, *more_ys, *halves[:7], *found)
     return residual, update
 
 

time: 43 us -> 40.9 us (0.951)
  waiting for transfers between devices: 6.2 us -> 3.64 us
    ppermute x8, waiting for transfers between devices: 6.2 us -> 3.64 us  [swaps(): got.append(lax.ppermute(message, axis, pairs + [(b, a) for a, b in pairs]))]
    pallas_call x1 -> x2, Pallas kernels: 9.4 us -> 9.79 us  [the longest x1 7.24 us: body(): call(functools.partial(finish, ay, count_y), 'finish', 16, out_shape=[cel...]
  transfers between devices with their start and end apart: 8 -> 8, of which waited for: 2 -> 2; matrix products, arithmetic and copies ran while one was open for 0% -> 0% of each run, Pallas kernels for 25% -> 33%
where the time goes in v8:
time: 40.9 us; the launch traced here: 40.3 us
  Pallas kernels  23.4 us (57%)
  starting transfers between devices  12.5 us (31%)
  waiting for transfers between devices  3.64 us (9%)
  between operations  0.76 us (2%)
    ppermute x8, starting transfers between devices, swaps(): got.append(lax.ppermute(message, axis, pairs + [(b, a) for a, b in pairs]))  12.5 us
    pallas_call x1, Pallas kernels, body(): call(functools.partial(finish, ay, count_y), 'finish', 16, out_shape=[cel...  7.24 us
    pallas_call x1, Pallas kernels, body(): call(functools.partial(inner, ax, planes), 'inner', 16, out_shape=[like(*...  6.03 us
    pallas_call x1, Pallas kernels, body(): call(inner_local, 'inner_local', 16, out_shape=[like(*shape) for shape in...  4.58 us
    ppermute x8, waiting for transfers between devices, swaps(): got.append(lax.ppermute(message, axis, pairs + [(b, a) for a, b in pairs]))  3.64 us
    pallas_call x1, Pallas kernels, body(): call(functools.partial(finish_local, ay, count_y, planes), 'finish_local'...  2.55 us
    pallas_call x1, Pallas kernels, body(): call(functools.partial(pack_z, az), 'pack_z', 8, out_shape=(like(CHANNELS...  2.33 us
  transfers between devices with their start and end apart: 8, of which 2 were waited for; matrix products, arithmetic and copies ran while one was open for 0% of the time, Pallas kernels for 33%

profile of v8, /device:TPU:17, one launch (start us, length us, event | category | flops | bytes accessed | tf_op | source)
XLA Modules:
  0.0 40.3 jit_solution(18164161404409314171)
XLA Ops:
  0.6 2.3 %pack_z.1 = (f32[20,8,16,128]{3,2,1,0:T(8,128)S(1)}, f32[3,8,16,128]{3,2,1,0:T(8,128)S(1)}, f32[9,8,128]{2,1,0:T(8,128)S(1)}, f32[10,16,128]{2,1,0:T(8,128)S(1)}, f32[10,16,128]{2,1,0:T(8,128)S(1)}) custom-call(f32[3,8,16,128]{3,2,1,0:T(8,128)} %refs_0_.1, f32[3,8,16,128]{3,2,1,0:T(8,128)} %refs_1_.1, f32[8,16,128]{2,1,0:T(8,128)} %refs_2_.1, ...), custom_call_target="tpu_custom_call" | custom-call | tf_op jit(solution)/shard_map/pack_z/pallas_call | solution.py:750
  3.0 0.1 pack_x.1
  3.1 1.4 %collective-permute-start.2 = (f32[74,16,128]{2,1,0:T(8,128)S(1)}, f32[74,16,128]{2,1,0:T(8,128)S(1)}, u32[]{:S(2)}, u32[]{:S(2)}) collective-permute-start(f32[74,16,128]{2,1,0:T(8,128)S(1)} %get-tuple-element.63), channel_id=1, source_target_pairs={{0,8},{16,24},{8,0},{24,16},{1,9},{17,25},{9,1},{25,17},{2,10},{18... | collective-permute-start | bytes 1818632 | tf_op jit(solution)/shard_map/ppermute | solution.py:63
  4.4 1.9 %collective-permute-start.3 = (f32[74,16,128]{2,1,0:T(8,128)S(1)}, f32[74,16,128]{2,1,0:T(8,128)S(1)}, u32[]{:S(2)}, u32[]{:S(2)}) collective-permute-start(f32[74,16,128]{2,1,0:T(8,128)S(1)} %get-tuple-element.64), channel_id=1, source_target_pairs={{8,16},{16,8},{9,17},{17,9},{10,18},{18,10},{11,19},{19,11},{12,20... | collective-permute-start | bytes 1818632 | tf_op jit(solution)/shard_map/ppermute | solution.py:63
  6.4 1.0 %collective-permute-start = (f32[10,16,128]{2,1,0:T(8,128)S(1)}, f32[10,16,128]{2,1,0:T(8,128)S(1)}, u32[]{:S(2)}, u32[]{:S(2)}) collective-permute-start(f32[10,16,128]{2,1,0:T(8,128)S(1)} %get-tuple-element.61), channel_id=1, source_target_pairs={{0,1},{2,3},{1,0},{3,2},{4,5},{6,7},{5,4},{7,6},{8,9},{10,11},{9,8... | collective-permute-start | bytes 245768 | tf_op jit(solution)/shard_map/ppermute | solution.py:63
  7.4 3.0 %collective-permute-start.1 = (f32[10,16,128]{2,1,0:T(8,128)S(1)}, f32[10,16,128]{2,1,0:T(8,128)S(1)}, u32[]{:S(2)}, u32[]{:S(2)}) collective-permute-start(f32[10,16,128]{2,1,0:T(8,128)S(1)} %get-tuple-element.62), channel_id=1, source_target_pairs={{1,2},{2,1},{5,6},{6,5},{9,10},{10,9},{13,14},{14,13},{17,18},{18,... | collective-permute-start | bytes 245768 | tf_op jit(solution)/shard_map/ppermute | solution.py:63
  10.4 0.0 collective-permute-done.za
  10.4 3.0 %collective-permute-done.1.zb = f32[10,16,128]{2,1,0:T(8,128)S(1)} collective-permute-done((f32[10,16,128]{2,1,0:T(8,128)S(1)}, f32[10,16,128]{2,1,0:T(8,128)S(1)}, u32[]{:S(2)}, u32[]{:S(2)}) %collective-permute-start.1) | collective-permute-done | bytes 81952 | tf_op jit(solution)/shard_map/ppermute | solution.py:63
  13.4 0.1 join_x.1
  13.5 1.3 %collective-permute-start.6 = (f32[170,4,128]{2,1,0:T(4,128)S(1)}, f32[170,4,128]{2,1,0:T(4,128)S(1)}, u32[]{:S(2)}, u32[]{:S(2)}) collective-permute-start(f32[170,4,128]{2,1,0:T(4,128)S(1)} %get-tuple-element.67), channel_id=1, source_target_pairs={{0,4},{4,0},{1,5},{5,1},{2,6},{6,2},{3,7},{7,3},{8,12},{12,8},{9,1... | collective-permute-start | bytes 1044488 | tf_op jit(solution)/shard_map/ppermute | solution.py:63
  14.9 0.0 collective-permute-start.4
  14.9 3.6 %collective-permute-start.5 = (f32[5,16,128]{2,1,0:T(8,128)S(1)}, f32[5,16,128]{2,1,0:T(8,128)S(1)}, u32[]{:S(2)}, u32[]{:S(2)}) collective-permute-start(f32[5,16,128]{2,1,0:T(8,128)S(1)} %get-tuple-element.66), channel_id=1, source_target_pairs={{8,16},{16,8},{9,17},{17,9},{10,18},{18,10},{11,19},{19,11},{12,20... | collective-permute-start | bytes 122888 | tf_op jit(solution)/shard_map/ppermute | solution.py:63
  18.5 4.6 %inner_local.1 = (f32[8,3,16,32,128]{4,3,2,1,0:T(8,128)S(1)}, f32[13,16,32,128]{3,2,1,0:T(8,128)S(1)}, f32[13,16,32,128]{3,2,1,0:T(8,128)S(1)}, f32[3,16,32,128]...) custom-call(f32[20,8,16,128]{3,2,1,0:T(8,128)S(1)} %get-tuple-elemen, ...), custom_call_target="tpu_custom_call" | custom-call | tf_op jit(solution)/shard_map/inner_local/pallas_call | solution.py:790
  23.1 0.0 collective-permute-done.4.ca
  23.1 0.0 collective-permute-done.5.cb
  23.1 0.0 collective-permute-done.6.refs_0_
  23.1 0.0 collective-permute-done.2.xa
  23.1 0.0 collective-permute-done.3.xb
  23.1 0.4 %join_y.1 = (f32[20,16,128]{2,1,0:T(8,128)S(1)}, f32[168,4,128]{2,1,0:T(4,128)S(1)}) custom-call(f32[10,16,128]{2,1,0:T(8,128)S(1)} %collective-permute-done.za, f32[10,16,128]{2,1,0:T(8,128)S(1)} %collective-permute-done.1.zb, f32[74,16,128]{2,1,0:T(8,128)S(1)} %collective-permute-done.2.xa, f32[74,16,128]{2,1,0:T(8,128)S(1)} %collective-permute-done.3.xb, ...), custom_call_target="tpu_custom_call" | custom-call | tf_op jit(solution)/shard_map/join_y/pallas_call | solution.py:801
  23.6 0.3 collective-permute-start.7
  23.9 6.0 %inner.1 = (f32[26,16,16,128]{3,2,1,0:T(8,128)S(1)}, f32[16,16,128]{2,1,0:T(8,128)S(1)}, f32[16,16,128]{2,1,0:T(8,128)S(1)}, f32[26,1,16,128]{3,2,1,0:T(8,128)S(...) custom-call(f32[20,16,128]{2,1,0:T(8,128)S(1)} %get-tuple-element.70, ...), custom_call_target="tpu_custom_call", output_to_operand_aliasing={{0}: (6, {}), {1}: (7, {}), {2}: (8, {}), {6}: (9, {}), {17... | custom-call | tf_op jit(solution)/shard_map/inner/pallas_call | solution.py:814
  29.9 2.6 %finish_local.1 = (f32[8,3,16,16,128]{4,3,2,1,0:T(8,128)S(1)}, f32[13,16,16,128]{3,2,1,0:T(8,128)S(1)}, f32[13,16,16,128]{3,2,1,0:T(8,128)S(1)}, f32[3,16,16,128...) custom-call(f32[9,8,128]{2,1,0:T(8,128)S(1)} %get-tuple-element.59.t, ...), custom_call_target="tpu_custom_call", output_to_operand_aliasing={{0}: (2, {}), {1}: (3, {}), {2}: (4, {}), {3}: (5, {}), {4}... | custom-call | tf_op jit(solution)/shard_map/finish_local/pallas_call | solution.py:830
  32.5 0.6 %collective-permute-done.7.refs_2_ = f32[168,4,128]{2,1,0:T(4,128)S(1)} collective-permute-done((f32[168,4,128]{2,1,0:T(4,128)S(1)}, f32[168,4,128]{2,1,0:T(4,128)S(1)}, u32[]{:S(2)}, u32[]{:S(2)}) %collective-permute-start.7) | collective-permute-done | bytes 344096 | tf_op jit(solution)/shard_map/ppermute | solution.py:63
  33.1 7.2 %finish.1 = (f32[3,8,16,128]{3,2,1,0:T(8,128)}, f32[8,16,128]{2,1,0:T(8,128)}, f32[8,3,16,16,128]{4,3,2,1,0:T(8,128)S(1)}, f32[13,16,16,128]{3,2,1,0:T(8,128)S(1...) custom-call(f32[20,8,16,128]{3,2,1,0:T(8,128)S(1)} %get-tuple-elemen, ...), custom_call_target="tpu_custom_call", output_to_operand_aliasing={{2}: (11, {}), {3}: (12, {}), {4}: (13, {}), {5}: (14, {}),... | custom-call | tf_op jit(solution)/shard_map/finish/pallas_call | solution.py:847
Async XLA Ops:
  3.1 20.0 %collective-permute-start.2 = (f32[74,16,128]{2,1,0:T(8,128)S(1)}, f32[74,16,128]{2,1,0:T(8,128)S(1)}, u32[]{:S(2)}, u32[]{:S(2)}) collective-permute-start(f32[74,16,128]{2,1,0:T(8,128)S(1)} %get-tuple-element.63), channel_id=1, source_target_pairs={{0,8},{16,24},{8,0},{24,16},{1,9},{17,25},{9,1},{25,17},{2,10},{18... | collective-permute-start | bytes 1818632 | tf_op jit(solution)/shard_map/ppermute | solution.py:63
  4.4 18.7 %collective-permute-start.3 = (f32[74,16,128]{2,1,0:T(8,128)S(1)}, f32[74,16,128]{2,1,0:T(8,128)S(1)}, u32[]{:S(2)}, u32[]{:S(2)}) collective-permute-start(f32[74,16,128]{2,1,0:T(8,128)S(1)} %get-tuple-element.64), channel_id=1, source_target_pairs={{8,16},{16,8},{9,17},{17,9},{10,18},{18,10},{11,19},{19,11},{12,20... | collective-permute-start | bytes 1818632 | tf_op jit(solution)/shard_map/ppermute | solution.py:63
  6.4 4.0 %collective-permute-start = (f32[10,16,128]{2,1,0:T(8,128)S(1)}, f32[10,16,128]{2,1,0:T(8,128)S(1)}, u32[]{:S(2)}, u32[]{:S(2)}) collective-permute-start(f32[10,16,128]{2,1,0:T(8,128)S(1)} %get-tuple-element.61), channel_id=1, source_target_pairs={{0,1},{2,3},{1,0},{3,2},{4,5},{6,7},{5,4},{7,6},{8,9},{10,11},{9,8... | collective-permute-start | bytes 245768 | tf_op jit(solution)/shard_map/ppermute | solution.py:63
  7.4 6.0 %collective-permute-start.1 = (f32[10,16,128]{2,1,0:T(8,128)S(1)}, f32[10,16,128]{2,1,0:T(8,128)S(1)}, u32[]{:S(2)}, u32[]{:S(2)}) collective-permute-start(f32[10,16,128]{2,1,0:T(8,128)S(1)} %get-tuple-element.62), channel_id=1, source_target_pairs={{1,2},{2,1},{5,6},{6,5},{9,10},{10,9},{13,14},{14,13},{17,18},{18,... | collective-permute-start | bytes 245768 | tf_op jit(solution)/shard_map/ppermute | solution.py:63
  13.5 9.6 %collective-permute-start.6 = (f32[170,4,128]{2,1,0:T(4,128)S(1)}, f32[170,4,128]{2,1,0:T(4,128)S(1)}, u32[]{:S(2)}, u32[]{:S(2)}) collective-permute-start(f32[170,4,128]{2,1,0:T(4,128)S(1)} %get-tuple-element.67), channel_id=1, source_target_pairs={{0,4},{4,0},{1,5},{5,1},{2,6},{6,2},{3,7},{7,3},{8,12},{12,8},{9,1... | collective-permute-start | bytes 1044488 | tf_op jit(solution)/shard_map/ppermute | solution.py:63
  14.9 8.2 %collective-permute-start.4 = (f32[5,16,128]{2,1,0:T(8,128)S(1)}, f32[5,16,128]{2,1,0:T(8,128)S(1)}, u32[]{:S(2)}, u32[]{:S(2)}) collective-permute-start(f32[5,16,128]{2,1,0:T(8,128)S(1)} %get-tuple-element.65), channel_id=1, source_target_pairs={{0,8},{16,24},{8,0},{24,16},{1,9},{17,25},{9,1},{25,17},{2,10},{18... | collective-permute-start | bytes 122888 | tf_op jit(solution)/shard_map/ppermute | solution.py:63
  14.9 8.2 %collective-permute-start.5 = (f32[5,16,128]{2,1,0:T(8,128)S(1)}, f32[5,16,128]{2,1,0:T(8,128)S(1)}, u32[]{:S(2)}, u32[]{:S(2)}) collective-permute-start(f32[5,16,128]{2,1,0:T(8,128)S(1)} %get-tuple-element.66), channel_id=1, source_target_pairs={{8,16},{16,8},{9,17},{17,9},{10,18},{18,10},{11,19},{19,11},{12,20... | collective-permute-start | bytes 122888 | tf_op jit(solution)/shard_map/ppermute | solution.py:63
  23.6 9.5 %collective-permute-start.7 = (f32[168,4,128]{2,1,0:T(4,128)S(1)}, f32[168,4,128]{2,1,0:T(4,128)S(1)}, u32[]{:S(2)}, u32[]{:S(2)}) collective-permute-start(f32[168,4,128]{2,1,0:T(4,128)S(1)} %get-tuple-element.69), channel_id=1, source_target_pairs={{0,4},{4,0},{1,5},{5,1},{2,6},{6,2},{3,7},{7,3},{8,12},{12,8},{9,1... | collective-permute-start | bytes 1032200 | tf_op jit(solution)/shard_map/ppermute | solution.py:63

commit v9 on v8

--- a/solution.py
+++ b/solution.py
@@ -139,7 +139,7 @@
     even = parity_of(axis)
     lane = lanes_of((8, depth))
 
-    @pl.loop(0, rows // 8)
+    @pl.loop(0, rows // 8, unroll=True)
     def _(tile):
         span = pl.ds(pl.multiple_of(8 * tile, 8), 8)
         for group in range(groups):
@@ -220,7 +220,7 @@
         columns[c] = values
         put_rows(outs, 2 * XMAIN + c, values, even)
 
-    @pl.loop(0, XMAIN // 2)
+    @pl.loop(0, XMAIN // 2, unroll=True)
     def _(i):
         for j in range(2):
             n = 2 * i + j
@@ -401,11 +401,11 @@
 
     cells(columns, 0, True)
 
-    @pl.loop(0, planes)
+    @pl.loop(0, planes, unroll=True)
     def _(x):
         cells(lambda c, span: local[c, x, span, :], W + x)
 
-    @pl.loop(W + 1, W + planes - 1)
+    @pl.loop(W + 1, W + planes - 1, unroll=True)
     def _(plane):
         row_links(tiles, plane, False, arrays, results, store)
 
@@ -438,7 +438,7 @@
 
         return get
 
-    @pl.loop(0, NEAR)
+    @pl.loop(0, NEAR, unroll=True)
     def _(q):
         near = lambda c: c * NEAR + q
         cells(from_x(near, True), 1 + q)
@@ -458,13 +458,13 @@
 
     hand_on(halo, edges[5:], 0)
 
-    @pl.loop(0, total)
+    @pl.loop(0, total, unroll=True)
     def _(plane):
         hand_on(arrays, edges[:5], plane)
 
     row_links(tiles, 0, True, halo, halo_results)
 
-    @pl.loop(0, W)
+    @pl.loop(0, W, unroll=True)
     def _(n):
         row_links(tiles, 1 + n, False, arrays, results, store)
         row_links(tiles, W + planes - 1 + n, False, arrays, results, store)
@@ -510,7 +510,7 @@
     for group in range(groups):
         halo_rows(even_y, ys, CHANNELS * planes + group, packed, (group,))
 
-    @pl.loop(0, CHANNELS)
+    @pl.loop(0, CHANNELS, unroll=True)
     def _(c):
         for x in range(planes):
             halo_rows(even_y, ys, c * planes + x, raw, (c, x))
@@ -527,11 +527,11 @@
 
     cells(columns, 0, True)
 
-    @pl.loop(0, planes, unroll=2)
+    @pl.loop(0, planes, unroll=True)
     def _(x):
         cells(lambda c: raw[c, x], W + x)
 
-    @pl.loop(W + 1, W + planes - 1)
+    @pl.loop(W + 1, W + planes - 1, unroll=True)
     def _(plane):
         ring_links(plane, False, arrays, results, store)
 
@@ -548,14 +548,14 @@
     total = planes + 2 * W
     even_y = parity_of(axis)
 
-    @pl.loop(0, CHANNELS)
+    @pl.loop(0, CHANNELS, unroll=True)
     def _(c):
         for q in range(NEAR):
             halo_rows(even_y, more_ys, c * NEAR + q, raw, (c, 1 + q))
             halo_rows(even_y, more_ys, XMAIN + c * NEAR + q, raw, (c, W + q))
         halo_rows(even_y, more_ys, 2 * XMAIN + c, raw, (c, 2 * W))
 
-    @pl.loop(0, FAR)
+    @pl.loop(0, FAR, unroll=True)
     def _(c):
         halo_rows(even_y, more_ys, CHANNELS * NEAR + c, raw, (c, 0))
         halo_rows(even_y, more_ys, XMAIN + CHANNELS * NEAR + c, raw, (c, 2 * W - 1))
@@ -571,14 +571,14 @@
 
     cells(2 * W, 0, True)
 
-    @pl.loop(0, W)
+    @pl.loop(0, W, unroll=True)
     def _(n):
         cells(n, n)
         cells(W + n, W + planes + n)
 
     ring_links(0, True, halo, edge_halo_results, None)
 
-    @pl.loop(0, W)
+    @pl.loop(0, W, unroll=True)
     def _(n):
         ring_links(1 + n, False, arrays, edge_results, edge_store)
         ring_links(W + planes - 1 + n, False, arrays, edge_results, edge_store)
@@ -660,7 +660,7 @@
 
     first_sweep(0, True)
 
-    @pl.loop(1, total - 1, unroll=2)
+    @pl.loop(1, total - 1, unroll=True)
     def _(plane):
         first_sweep(plane)
 
@@ -672,11 +672,11 @@
         slot = sweep % 2
         sweep_of(slot, 0, True)
 
-        @pl.loop(sweep, total - sweep, unroll=2)
+        @pl.loop(sweep, total - sweep, unroll=True)
         def _(plane):
             sweep_of(slot, plane)
 
-    @pl.loop(0, planes, unroll=2)
+    @pl.loop(0, planes, unroll=True)
     def _(x):
         slot, plane = SWEEPS % 2, W + x
         edge = relaxed(slot, plane, None)

time: 40.9 us -> 36.9 us (0.902)
  the two profiles are of different devices: /device:TPU:17 before, /device:TPU:8 now
where the time goes in v9:
time: 36.9 us; the launch traced here: 36.7 us
  Pallas kernels  17.4 us (47%)
  starting transfers between devices  10.9 us (30%)
  waiting for transfers between devices  7.63 us (21%)
  between operations  0.73 us (2%)
    ppermute x8, starting transfers between devices, swaps(): got.append(lax.ppermute(message, axis, pairs + [(b, a) for a, b in pairs]))  10.9 us
    ppermute x8, waiting for transfers between devices, swaps(): got.append(lax.ppermute(message, axis, pairs + [(b, a) for a, b in pairs]))  7.63 us
    pallas_call x1, Pallas kernels, body(): call(functools.partial(finish, ay, count_y), 'finish', 16, out_shape=[cel...  4.85 us
    pallas_call x1, Pallas kernels, body(): call(functools.partial(inner, ax, planes), 'inner', 16, out_shape=[like(*...  4.81 us
    pallas_call x1, Pallas kernels, body(): call(inner_local, 'inner_local', 16, out_shape=[like(*shape) for shape in...  3.3 us
    pallas_call x1, Pallas kernels, body(): call(functools.partial(pack_z, az), 'pack_z', 8, out_shape=(like(CHANNELS...  2.25 us
    pallas_call x1, Pallas kernels, body(): call(functools.partial(finish_local, ay, count_y, planes), 'finish_local'...  1.83 us
  transfers between devices with their start and end apart: 8, of which 4 were waited for; matrix products, arithmetic and copies ran while one was open for 0% of the time, Pallas kernels for 27%

profile of v9, /device:TPU:8, one launch (start us, length us, event | category | flops | bytes accessed | tf_op | source)
XLA Modules:
  0.0 36.7 jit_solution(17267935023079930468)
XLA Ops:
  0.6 2.3 %pack_z.1 = (f32[20,8,16,128]{3,2,1,0:T(8,128)S(1)}, f32[3,8,16,128]{3,2,1,0:T(8,128)S(1)}, f32[9,8,128]{2,1,0:T(8,128)S(1)}, f32[10,16,128]{2,1,0:T(8,128)S(1)}, f32[10,16,128]{2,1,0:T(8,128)S(1)}) custom-call(f32[3,8,16,128]{3,2,1,0:T(8,128)} %refs_0_.1, f32[3,8,16,128]{3,2,1,0:T(8,128)} %refs_1_.1, f32[8,16,128]{2,1,0:T(8,128)} %refs_2_.1, ...), custom_call_target="tpu_custom_call" | custom-call | tf_op jit(solution)/shard_map/pack_z/pallas_call | solution.py:750
  2.9 0.1 pack_x.1
  3.0 0.1 collective-permute-start.2
  3.1 5.0 %collective-permute-start.3 = (f32[74,16,128]{2,1,0:T(8,128)S(1)}, f32[74,16,128]{2,1,0:T(8,128)S(1)}, u32[]{:S(2)}, u32[]{:S(2)}) collective-permute-start(f32[74,16,128]{2,1,0:T(8,128)S(1)} %get-tuple-element.64), channel_id=1, source_target_pairs={{8,16},{16,8},{9,17},{17,9},{10,18},{18,10},{11,19},{19,11},{12,20... | collective-permute-start | bytes 1818632 | tf_op jit(solution)/shard_map/ppermute | solution.py:63
  8.1 0.1 collective-permute-start
  8.2 0.7 %collective-permute-start.1 = (f32[10,16,128]{2,1,0:T(8,128)S(1)}, f32[10,16,128]{2,1,0:T(8,128)S(1)}, u32[]{:S(2)}, u32[]{:S(2)}) collective-permute-start(f32[10,16,128]{2,1,0:T(8,128)S(1)} %get-tuple-element.62), channel_id=1, source_target_pairs={{1,2},{2,1},{5,6},{6,5},{9,10},{10,9},{13,14},{14,13},{17,18},{18,... | collective-permute-start | bytes 245768 | tf_op jit(solution)/shard_map/ppermute | solution.py:63
  8.9 0.6 %collective-permute-done.za = f32[10,16,128]{2,1,0:T(8,128)S(1)} collective-permute-done((f32[10,16,128]{2,1,0:T(8,128)S(1)}, f32[10,16,128]{2,1,0:T(8,128)S(1)}, u32[]{:S(2)}, u32[]{:S(2)}) %collective-permute-start) | collective-permute-done | bytes 81952 | tf_op jit(solution)/shard_map/ppermute | solution.py:63
  9.5 0.0 collective-permute-done.1.zb
  9.5 0.1 join_x.1
  9.6 1.6 %collective-permute-start.6 = (f32[170,4,128]{2,1,0:T(4,128)S(1)}, f32[170,4,128]{2,1,0:T(4,128)S(1)}, u32[]{:S(2)}, u32[]{:S(2)}) collective-permute-start(f32[170,4,128]{2,1,0:T(4,128)S(1)} %get-tuple-element.67), channel_id=1, source_target_pairs={{0,4},{4,0},{1,5},{5,1},{2,6},{6,2},{3,7},{7,3},{8,12},{12,8},{9,1... | collective-permute-start | bytes 1044488 | tf_op jit(solution)/shard_map/ppermute | solution.py:63
  11.2 0.0 collective-permute-start.4
  11.2 1.9 %collective-permute-start.5 = (f32[5,16,128]{2,1,0:T(8,128)S(1)}, f32[5,16,128]{2,1,0:T(8,128)S(1)}, u32[]{:S(2)}, u32[]{:S(2)}) collective-permute-start(f32[5,16,128]{2,1,0:T(8,128)S(1)} %get-tuple-element.66), channel_id=1, source_target_pairs={{8,16},{16,8},{9,17},{17,9},{10,18},{18,10},{11,19},{19,11},{12,20... | collective-permute-start | bytes 122888 | tf_op jit(solution)/shard_map/ppermute | solution.py:63
  13.1 3.3 %inner_local.1 = (f32[8,3,16,32,128]{4,3,2,1,0:T(8,128)S(1)}, f32[13,16,32,128]{3,2,1,0:T(8,128)S(1)}, f32[13,16,32,128]{3,2,1,0:T(8,128)S(1)}, f32[3,16,32,128]...) custom-call(f32[20,8,16,128]{3,2,1,0:T(8,128)S(1)} %get-tuple-elemen, ...), custom_call_target="tpu_custom_call" | custom-call | tf_op jit(solution)/shard_map/inner_local/pallas_call | solution.py:790
  16.4 2.7 %collective-permute-done.4.ca = f32[5,16,128]{2,1,0:T(8,128)S(1)} collective-permute-done((f32[5,16,128]{2,1,0:T(8,128)S(1)}, f32[5,16,128]{2,1,0:T(8,128)S(1)}, u32[]{:S(2)}, u32[]{:S(2)}) %collective-permute-start.4) | collective-permute-done | bytes 40992 | tf_op jit(solution)/shard_map/ppermute | solution.py:63
  19.1 3.3 %collective-permute-done.5.cb = f32[5,16,128]{2,1,0:T(8,128)S(1)} collective-permute-done((f32[5,16,128]{2,1,0:T(8,128)S(1)}, f32[5,16,128]{2,1,0:T(8,128)S(1)}, u32[]{:S(2)}, u32[]{:S(2)}) %collective-permute-start.5) | collective-permute-done | bytes 40992 | tf_op jit(solution)/shard_map/ppermute | solution.py:63
  22.4 0.0 collective-permute-done.6.refs_0_
  22.4 0.0 collective-permute-done.2.xa
  22.4 0.0 collective-permute-done.3.xb
  22.4 0.2 join_y.1
  22.6 1.6 %collective-permute-start.7 = (f32[168,4,128]{2,1,0:T(4,128)S(1)}, f32[168,4,128]{2,1,0:T(4,128)S(1)}, u32[]{:S(2)}, u32[]{:S(2)}) collective-permute-start(f32[168,4,128]{2,1,0:T(4,128)S(1)} %get-tuple-element.69), channel_id=1, source_target_pairs={{0,4},{4,0},{1,5},{5,1},{2,6},{6,2},{3,7},{7,3},{8,12},{12,8},{9,1... | collective-permute-start | bytes 1032200 | tf_op jit(solution)/shard_map/ppermute | solution.py:63
  24.2 4.8 %inner.1 = (f32[26,16,16,128]{3,2,1,0:T(8,128)S(1)}, f32[16,16,128]{2,1,0:T(8,128)S(1)}, f32[16,16,128]{2,1,0:T(8,128)S(1)}, f32[26,1,16,128]{3,2,1,0:T(8,128)S(...) custom-call(f32[20,16,128]{2,1,0:T(8,128)S(1)} %get-tuple-element.70, ...), custom_call_target="tpu_custom_call", output_to_operand_aliasing={{0}: (6, {}), {1}: (7, {}), {2}: (8, {}), {6}: (9, {}), {17... | custom-call | tf_op jit(solution)/shard_map/inner/pallas_call | solution.py:814
  29.0 1.8 %finish_local.1 = (f32[8,3,16,16,128]{4,3,2,1,0:T(8,128)S(1)}, f32[13,16,16,128]{3,2,1,0:T(8,128)S(1)}, f32[13,16,16,128]{3,2,1,0:T(8,128)S(1)}, f32[3,16,16,128...) custom-call(f32[9,8,128]{2,1,0:T(8,128)S(1)} %get-tuple-element.59.t, ...), custom_call_target="tpu_custom_call", output_to_operand_aliasing={{0}: (2, {}), {1}: (3, {}), {2}: (4, {}), {3}: (5, {}), {4}... | custom-call | tf_op jit(solution)/shard_map/finish_local/pallas_call | solution.py:830
  30.8 1.1 %collective-permute-done.7.refs_2_ = f32[168,4,128]{2,1,0:T(4,128)S(1)} collective-permute-done((f32[168,4,128]{2,1,0:T(4,128)S(1)}, f32[168,4,128]{2,1,0:T(4,128)S(1)}, u32[]{:S(2)}, u32[]{:S(2)}) %collective-permute-start.7) | collective-permute-done | bytes 344096 | tf_op jit(solution)/shard_map/ppermute | solution.py:63
  31.9 4.8 %finish.1 = (f32[3,8,16,128]{3,2,1,0:T(8,128)}, f32[8,16,128]{2,1,0:T(8,128)}, f32[8,3,16,16,128]{4,3,2,1,0:T(8,128)S(1)}, f32[13,16,16,128]{3,2,1,0:T(8,128)S(1...) custom-call(f32[20,8,16,128]{3,2,1,0:T(8,128)S(1)} %get-tuple-elemen, ...), custom_call_target="tpu_custom_call", output_to_operand_aliasing={{2}: (11, {}), {3}: (12, {}), {4}: (13, {}), {5}: (14, {}),... | custom-call | tf_op jit(solution)/shard_map/finish/pallas_call | solution.py:847
Async XLA Ops:
  3.0 19.4 %collective-permute-start.2 = (f32[74,16,128]{2,1,0:T(8,128)S(1)}, f32[74,16,128]{2,1,0:T(8,128)S(1)}, u32[]{:S(2)}, u32[]{:S(2)}) collective-permute-start(f32[74,16,128]{2,1,0:T(8,128)S(1)} %get-tuple-element.63), channel_id=1, source_target_pairs={{0,8},{16,24},{8,0},{24,16},{1,9},{17,25},{9,1},{25,17},{2,10},{18... | collective-permute-start | bytes 1818632 | tf_op jit(solution)/shard_map/ppermute | solution.py:63
  3.1 19.3 %collective-permute-start.3 = (f32[74,16,128]{2,1,0:T(8,128)S(1)}, f32[74,16,128]{2,1,0:T(8,128)S(1)}, u32[]{:S(2)}, u32[]{:S(2)}) collective-permute-start(f32[74,16,128]{2,1,0:T(8,128)S(1)} %get-tuple-element.64), channel_id=1, source_target_pairs={{8,16},{16,8},{9,17},{17,9},{10,18},{18,10},{11,19},{19,11},{12,20... | collective-permute-start | bytes 1818632 | tf_op jit(solution)/shard_map/ppermute | solution.py:63
  8.1 1.3 %collective-permute-start = (f32[10,16,128]{2,1,0:T(8,128)S(1)}, f32[10,16,128]{2,1,0:T(8,128)S(1)}, u32[]{:S(2)}, u32[]{:S(2)}) collective-permute-start(f32[10,16,128]{2,1,0:T(8,128)S(1)} %get-tuple-element.61), channel_id=1, source_target_pairs={{0,1},{2,3},{1,0},{3,2},{4,5},{6,7},{5,4},{7,6},{8,9},{10,11},{9,8... | collective-permute-start | bytes 245768 | tf_op jit(solution)/shard_map/ppermute | solution.py:63
  8.2 1.3 %collective-permute-start.1 = (f32[10,16,128]{2,1,0:T(8,128)S(1)}, f32[10,16,128]{2,1,0:T(8,128)S(1)}, u32[]{:S(2)}, u32[]{:S(2)}) collective-permute-start(f32[10,16,128]{2,1,0:T(8,128)S(1)} %get-tuple-element.62), channel_id=1, source_target_pairs={{1,2},{2,1},{5,6},{6,5},{9,10},{10,9},{13,14},{14,13},{17,18},{18,... | collective-permute-start | bytes 245768 | tf_op jit(solution)/shard_map/ppermute | solution.py:63
  9.6 12.8 %collective-permute-start.6 = (f32[170,4,128]{2,1,0:T(4,128)S(1)}, f32[170,4,128]{2,1,0:T(4,128)S(1)}, u32[]{:S(2)}, u32[]{:S(2)}) collective-permute-start(f32[170,4,128]{2,1,0:T(4,128)S(1)} %get-tuple-element.67), channel_id=1, source_target_pairs={{0,4},{4,0},{1,5},{5,1},{2,6},{6,2},{3,7},{7,3},{8,12},{12,8},{9,1... | collective-permute-start | bytes 1044488 | tf_op jit(solution)/shard_map/ppermute | solution.py:63
  11.2 7.9 %collective-permute-start.4 = (f32[5,16,128]{2,1,0:T(8,128)S(1)}, f32[5,16,128]{2,1,0:T(8,128)S(1)}, u32[]{:S(2)}, u32[]{:S(2)}) collective-permute-start(f32[5,16,128]{2,1,0:T(8,128)S(1)} %get-tuple-element.65), channel_id=1, source_target_pairs={{0,8},{16,24},{8,0},{24,16},{1,9},{17,25},{9,1},{25,17},{2,10},{18... | collective-permute-start | bytes 122888 | tf_op jit(solution)/shard_map/ppermute | solution.py:63
  11.2 11.2 %collective-permute-start.5 = (f32[5,16,128]{2,1,0:T(8,128)S(1)}, f32[5,16,128]{2,1,0:T(8,128)S(1)}, u32[]{:S(2)}, u32[]{:S(2)}) collective-permute-start(f32[5,16,128]{2,1,0:T(8,128)S(1)} %get-tuple-element.66), channel_id=1, source_target_pairs={{8,16},{16,8},{9,17},{17,9},{10,18},{18,10},{11,19},{19,11},{12,20... | collective-permute-start | bytes 122888 | tf_op jit(solution)/shard_map/ppermute | solution.py:63
  22.6 9.3 %collective-permute-start.7 = (f32[168,4,128]{2,1,0:T(4,128)S(1)}, f32[168,4,128]{2,1,0:T(4,128)S(1)}, u32[]{:S(2)}, u32[]{:S(2)}) collective-permute-start(f32[168,4,128]{2,1,0:T(4,128)S(1)} %get-tuple-element.69), channel_id=1, source_target_pairs={{0,4},{4,0},{1,5},{5,1},{2,6},{6,2},{3,7},{7,3},{8,12},{12,8},{9,1... | collective-permute-start | bytes 1032200 | tf_op jit(solution)/shard_map/ppermute | solution.py:63

commit v10 on v9

--- a/solution.py
+++ b/solution.py
@@ -208,8 +208,12 @@
     rows, depth = xa.shape[1:]
     even = parity_of(axis)
     even_x = parity_of(x_axis)
-    per_x, _ = groups_of(W, depth)
+    per_x, groups_x = groups_of(W, depth)
     lane = lanes_of((rows, depth))
+    for group in range(groups_x):
+        a, b = ca[group], cb[group]
+        put_rows(outs, 2 * XMAIN + group, pick(even_x, b, a), even)
+        put_rows(outs, 2 * XMAIN + groups_x + group, pick(even_x, a, b), even)
     for c in range(CHANNELS):
         own = own_columns(c, za, zb, planes, slice(0, rows))
         group, base = c // per_x, (c % per_x) * span_of(W)
@@ -218,7 +222,6 @@
         above = pltpu.roll(pick(even_x, a, b), (2 * W * (planes + W) - base) % depth, 1)
         values = jnp.where(lane < 2 * W * W, below, jnp.where(lane < 2 * W * (W + planes), own, above))
         columns[c] = values
-        put_rows(outs, 2 * XMAIN + c, values, even)
 
     @pl.loop(0, XMAIN // 2, unroll=True)
     def _(i):
@@ -537,13 +540,14 @@
 
 
 def finish(axis, count_y, local, *refs):
-    tabs, accum, more_ys, refs = refs[0], refs[1], refs[2 : 2 + count_y], refs[2 + count_y :]
+    tabs, accum, ys, more_ys = refs[0], refs[1], refs[2 : 2 + count_y], refs[2 + count_y : 2 + 2 * count_y]
+    refs = refs[2 + 2 * count_y :]
     results, halo_results, store = refs[:3], refs[3:6], refs[6]
     residual, update = refs[21:23]
     arrays, halo = refs[23:28], refs[28:33]
     edge_results, edge_store = refs[33:36], refs[36]
-    raw, centre, edge_halo_results = refs[37], refs[38], refs[39:42]
-    sols, halo_sols, edge_sols, edge_halo_sols = (refs[42 + 2 * i : 44 + 2 * i] for i in range(4))
+    raw, packed, centre, edge_halo_results = refs[37], refs[38], refs[39], refs[40:43]
+    sols, halo_sols, edge_sols, edge_halo_sols = (refs[43 + 2 * i : 45 + 2 * i] for i in range(4))
     planes, rows, depth = local.shape[1:]
     total = planes + 2 * W
     even_y = parity_of(axis)
@@ -553,7 +557,6 @@
         for q in range(NEAR):
             halo_rows(even_y, more_ys, c * NEAR + q, raw, (c, 1 + q))
             halo_rows(even_y, more_ys, XMAIN + c * NEAR + q, raw, (c, W + q))
-        halo_rows(even_y, more_ys, 2 * XMAIN + c, raw, (c, 2 * W))
 
     @pl.loop(0, FAR, unroll=True)
     def _(c):
@@ -568,6 +571,22 @@
         done = among_own(planes, (2 * W, depth)) if is_columns else None
         get, span = lambda c: raw[c, slot], slice(0, 2 * W)
         properties(get, plane, is_columns, put_ring, tabs, arrays, halo, centre, span, done)
+
+    per, groups = groups_of(planes, depth)
+    per_x, groups_x = groups_of(W, depth)
+    for group in range(groups):
+        halo_rows(even_y, ys, CHANNELS * planes + group, packed, (group,))
+    for group in range(2 * groups_x):
+        halo_rows(even_y, more_ys, 2 * XMAIN + group, packed, (groups + group,))
+    lane = lanes_of((2 * W, depth))
+    for c in range(CHANNELS):
+        base, base_x = (c % per) * span_of(planes), (c % per_x) * span_of(W)
+        own = pltpu.roll(packed[c // per], (2 * W * W - base) % depth, 1)
+        below = pltpu.roll(packed[groups + c // per_x], (depth - base_x) % depth, 1)
+        above = packed[groups + groups_x + c // per_x]
+        above = pltpu.roll(above, (2 * W * (planes + W) - base_x) % depth, 1)
+        own = jnp.where(lane < 2 * W * (W + planes), own, above)
+        raw[c, 2 * W] = jnp.where(lane < 2 * W * W, below, own)
 
     cells(2 * W, 0, True)
 
@@ -803,7 +822,7 @@
         "join_y",
         8,
         out_shape=(like(CHANNELS, rows, depth),)
-        + (like(2 * XMAIN + CHANNELS, W, depth),) * count_y,
+        + (like(2 * XMAIN + 2 * groups_of(W, depth)[1], W, depth),) * count_y,
         in_specs=[VMEM] * 6 + [ANY] * (count_y + 1),
     )(za, zb, xa, xb, ca, cb, *ys, parts[1])
     if count_y:
@@ -826,6 +845,7 @@
         (3, count, height, depth) for height in (rows + 16, 16) for count in (total, 1) for _ in range(2)
     ]
     edge_shapes = result_shapes(total, 2 * W, depth)
+    groups_x = groups_of(W, depth)[1]
     shapes = edges + edge_shapes[:3] + [(3, total, 2 * W, depth)]
     found = call(
         functools.partial(finish_local, ay, count_y, planes),
@@ -843,7 +863,7 @@
         ),
         input_output_aliases={1 + count_y + i: i for i in range(10)},
     )(tabs, *ys, *halves[7:])
-    before = 3 + count_y + 7
+    before = 3 + 2 * count_y + 7
     residual, update, *_ = call(
         functools.partial(finish, ay, count_y),
         "finish",
@@ -854,13 +874,14 @@
         scratch_shapes=vmem(
             [
                 (CHANNELS, 2 * W + 1, 2 * W, depth),
+                (groups + 2 * groups_x, 2 * W, depth),
                 (SHIFTED + UP, 2 * W, depth),
                 *edge_shapes[3:],
                 *solutions,
             ]
         ),
         input_output_aliases={before + i: 2 + i for i in range(len(shapes))},
-    )(local, tabs, accum, *more_ys, *halves[:7], *found)
+    )(local, tabs, accum, *ys, *more_ys, *halves[:7], *found)
     return residual, update
 
 

time: 36.9 us -> 36.6 us (level)
  waiting for transfers between devices: 7.63 us -> 7.18 us
    ppermute x8, waiting for transfers between devices: 7.63 us -> 7.18 us  [swaps(): got.append(lax.ppermute(message, axis, pairs + [(b, a) for a, b in pairs]))]
  transfers between devices with their start and end apart: 8 -> 8, of which waited for: 4 -> 4; matrix products, arithmetic and copies ran while one was open for 0% -> 0% of each run, Pallas kernels for 27% -> 28%
where the time goes in v10:
time: 36.6 us; the launch traced here: 36.4 us
  Pallas kernels  17.6 us (48%)
  starting transfers between devices  10.9 us (30%)
  waiting for transfers between devices  7.18 us (20%)
  between operations  0.73 us (2%)
    ppermute x8, starting transfers between devices, swaps(): got.append(lax.ppermute(message, axis, pairs + [(b, a) for a, b in pairs]))  10.9 us
    ppermute x8, waiting for transfers between devices, swaps(): got.append(lax.ppermute(message, axis, pairs + [(b, a) for a, b in pairs]))  7.18 us
    pallas_call x1, Pallas kernels, body(): call(functools.partial(finish, ay, count_y), 'finish', 16, out_shape=[cel...  4.93 us
    pallas_call x1, Pallas kernels, body(): call(functools.partial(inner, ax, planes), 'inner', 16, out_shape=[like(*...  4.81 us
    pallas_call x1, Pallas kernels, body(): call(inner_local, 'inner_local', 16, out_shape=[like(*shape) for shape in...  3.3 us
    pallas_call x1, Pallas kernels, body(): call(functools.partial(pack_z, az), 'pack_z', 8, out_shape=(like(CHANNELS...  2.25 us
    pallas_call x1, Pallas kernels, body(): call(functools.partial(finish_local, ay, count_y, planes), 'finish_local'...  1.83 us
  transfers between devices with their start and end apart: 8, of which 4 were waited for; matrix products, arithmetic and copies ran while one was open for 0% of the time, Pallas kernels for 28%

profile of v10, /device:TPU:8, one launch (start us, length us, event | category | flops | bytes accessed | tf_op | source)
XLA Modules:
  0.0 36.4 jit_solution(2841031524941628773)
XLA Ops:
  0.6 2.3 %pack_z.1 = (f32[20,8,16,128]{3,2,1,0:T(8,128)S(1)}, f32[3,8,16,128]{3,2,1,0:T(8,128)S(1)}, f32[9,8,128]{2,1,0:T(8,128)S(1)}, f32[10,16,128]{2,1,0:T(8,128)S(1)}, f32[10,16,128]{2,1,0:T(8,128)S(1)}) custom-call(f32[3,8,16,128]{3,2,1,0:T(8,128)} %refs_0_.1, f32[3,8,16,128]{3,2,1,0:T(8,128)} %refs_1_.1, f32[8,16,128]{2,1,0:T(8,128)} %refs_2_.1, ...), custom_call_target="tpu_custom_call" | custom-call | tf_op jit(solution)/shard_map/pack_z/pallas_call | solution.py:769
  2.9 0.1 pack_x.1
  3.0 0.1 collective-permute-start.3
  3.1 5.0 %collective-permute-start.4 = (f32[74,16,128]{2,1,0:T(8,128)S(1)}, f32[74,16,128]{2,1,0:T(8,128)S(1)}, u32[]{:S(2)}, u32[]{:S(2)}) collective-permute-start(f32[74,16,128]{2,1,0:T(8,128)S(1)} %get-tuple-element.65), channel_id=1, source_target_pairs={{8,16},{16,8},{9,17},{17,9},{10,18},{18,10},{11,19},{19,11},{12,20... | collective-permute-start | bytes 1818632 | tf_op jit(solution)/shard_map/ppermute | solution.py:63
  8.1 0.1 collective-permute-start
  8.2 0.7 %collective-permute-start.1 = (f32[10,16,128]{2,1,0:T(8,128)S(1)}, f32[10,16,128]{2,1,0:T(8,128)S(1)}, u32[]{:S(2)}, u32[]{:S(2)}) collective-permute-start(f32[10,16,128]{2,1,0:T(8,128)S(1)} %get-tuple-element.62), channel_id=1, source_target_pairs={{1,2},{2,1},{5,6},{6,5},{9,10},{10,9},{13,14},{14,13},{17,18},{18,... | collective-permute-start | bytes 245768 | tf_op jit(solution)/shard_map/ppermute | solution.py:63
  8.9 0.6 %collective-permute-done.za = f32[10,16,128]{2,1,0:T(8,128)S(1)} collective-permute-done((f32[10,16,128]{2,1,0:T(8,128)S(1)}, f32[10,16,128]{2,1,0:T(8,128)S(1)}, u32[]{:S(2)}, u32[]{:S(2)}) %collective-permute-start) | collective-permute-done | bytes 81952 | tf_op jit(solution)/shard_map/ppermute | solution.py:63
  9.5 0.0 collective-permute-done.1.zb
  9.5 0.1 join_x.1
  9.6 1.6 %collective-permute-start.2 = (f32[170,4,128]{2,1,0:T(4,128)S(1)}, f32[170,4,128]{2,1,0:T(4,128)S(1)}, u32[]{:S(2)}, u32[]{:S(2)}) collective-permute-start(f32[170,4,128]{2,1,0:T(4,128)S(1)} %get-tuple-element.63), channel_id=1, source_target_pairs={{0,4},{4,0},{1,5},{5,1},{2,6},{6,2},{3,7},{7,3},{8,12},{12,8},{9,1... | collective-permute-start | bytes 1044488 | tf_op jit(solution)/shard_map/ppermute | solution.py:63
  11.2 0.0 collective-permute-start.5
  11.2 1.9 %collective-permute-start.6 = (f32[5,16,128]{2,1,0:T(8,128)S(1)}, f32[5,16,128]{2,1,0:T(8,128)S(1)}, u32[]{:S(2)}, u32[]{:S(2)}) collective-permute-start(f32[5,16,128]{2,1,0:T(8,128)S(1)} %get-tuple-element.67), channel_id=1, source_target_pairs={{8,16},{16,8},{9,17},{17,9},{10,18},{18,10},{11,19},{19,11},{12,20... | collective-permute-start | bytes 122888 | tf_op jit(solution)/shard_map/ppermute | solution.py:63
  13.1 3.3 %inner_local.1 = (f32[8,3,16,32,128]{4,3,2,1,0:T(8,128)S(1)}, f32[13,16,32,128]{3,2,1,0:T(8,128)S(1)}, f32[13,16,32,128]{3,2,1,0:T(8,128)S(1)}, f32[3,16,32,128]...) custom-call(f32[20,8,16,128]{3,2,1,0:T(8,128)S(1)} %get-tuple-elemen, ...), custom_call_target="tpu_custom_call" | custom-call | tf_op jit(solution)/shard_map/inner_local/pallas_call | solution.py:809
  16.4 2.7 %collective-permute-done.5.ca = f32[5,16,128]{2,1,0:T(8,128)S(1)} collective-permute-done((f32[5,16,128]{2,1,0:T(8,128)S(1)}, f32[5,16,128]{2,1,0:T(8,128)S(1)}, u32[]{:S(2)}, u32[]{:S(2)}) %collective-permute-start.5) | collective-permute-done | bytes 40992 | tf_op jit(solution)/shard_map/ppermute | solution.py:63
  19.1 3.3 %collective-permute-done.6.cb = f32[5,16,128]{2,1,0:T(8,128)S(1)} collective-permute-done((f32[5,16,128]{2,1,0:T(8,128)S(1)}, f32[5,16,128]{2,1,0:T(8,128)S(1)}, u32[]{:S(2)}, u32[]{:S(2)}) %collective-permute-start.6) | collective-permute-done | bytes 40992 | tf_op jit(solution)/shard_map/ppermute | solution.py:63
  22.4 0.0 collective-permute-done.2.refs_0_.refs_2_
  22.4 0.0 collective-permute-done.3.xa
  22.4 0.0 collective-permute-done.4.xb
  22.4 0.3 join_y.1
  22.7 1.6 %collective-permute-start.7 = (f32[158,4,128]{2,1,0:T(4,128)S(1)}, f32[158,4,128]{2,1,0:T(4,128)S(1)}, u32[]{:S(2)}, u32[]{:S(2)}) collective-permute-start(f32[158,4,128]{2,1,0:T(4,128)S(1)} %get-tuple-element.69), channel_id=1, source_target_pairs={{0,4},{4,0},{1,5},{5,1},{2,6},{6,2},{3,7},{7,3},{8,12},{12,8},{9,1... | collective-permute-start | bytes 970760 | tf_op jit(solution)/shard_map/ppermute | solution.py:63
  24.2 4.8 %inner.1 = (f32[26,16,16,128]{3,2,1,0:T(8,128)S(1)}, f32[16,16,128]{2,1,0:T(8,128)S(1)}, f32[16,16,128]{2,1,0:T(8,128)S(1)}, f32[26,1,16,128]{3,2,1,0:T(8,128)S(...) custom-call(f32[20,16,128]{2,1,0:T(8,128)S(1)} %get-tuple-element.70, ...), custom_call_target="tpu_custom_call", output_to_operand_aliasing={{0}: (6, {}), {1}: (7, {}), {2}: (8, {}), {6}: (9, {}), {17... | custom-call | tf_op jit(solution)/shard_map/inner/pallas_call | solution.py:833
  29.1 1.8 %finish_local.1 = (f32[8,3,16,16,128]{4,3,2,1,0:T(8,128)S(1)}, f32[13,16,16,128]{3,2,1,0:T(8,128)S(1)}, f32[13,16,16,128]{3,2,1,0:T(8,128)S(1)}, f32[3,16,16,128...) custom-call(f32[9,8,128]{2,1,0:T(8,128)S(1)} %get-tuple-element.59.t, ...), custom_call_target="tpu_custom_call", output_to_operand_aliasing={{0}: (2, {}), {1}: (3, {}), {2}: (4, {}), {3}: (5, {}), {4}... | custom-call | tf_op jit(solution)/shard_map/finish_local/pallas_call | solution.py:850
  30.9 0.6 %collective-permute-done.7.refs_3_ = f32[158,4,128]{2,1,0:T(4,128)S(1)} collective-permute-done((f32[158,4,128]{2,1,0:T(4,128)S(1)}, f32[158,4,128]{2,1,0:T(4,128)S(1)}, u32[]{:S(2)}, u32[]{:S(2)}) %collective-permute-start.7) | collective-permute-done | bytes 323616 | tf_op jit(solution)/shard_map/ppermute | solution.py:63
  31.5 4.9 %finish.1 = (f32[3,8,16,128]{3,2,1,0:T(8,128)}, f32[8,16,128]{2,1,0:T(8,128)}, f32[8,3,16,16,128]{4,3,2,1,0:T(8,128)S(1)}, f32[13,16,16,128]{3,2,1,0:T(8,128)S(1...) custom-call(f32[20,8,16,128]{3,2,1,0:T(8,128)S(1)} %get-tuple-elemen, ...), custom_call_target="tpu_custom_call", output_to_operand_aliasing={{2}: (12, {}), {3}: (13, {}), {4}: (14, {}), {5}: (15, {}),... | custom-call | tf_op jit(solution)/shard_map/finish/pallas_call | solution.py:867
Async XLA Ops:
  3.0 19.4 %collective-permute-start.3 = (f32[74,16,128]{2,1,0:T(8,128)S(1)}, f32[74,16,128]{2,1,0:T(8,128)S(1)}, u32[]{:S(2)}, u32[]{:S(2)}) collective-permute-start(f32[74,16,128]{2,1,0:T(8,128)S(1)} %get-tuple-element.64), channel_id=1, source_target_pairs={{0,8},{16,24},{8,0},{24,16},{1,9},{17,25},{9,1},{25,17},{2,10},{18... | collective-permute-start | bytes 1818632 | tf_op jit(solution)/shard_map/ppermute | solution.py:63
  3.1 19.3 %collective-permute-start.4 = (f32[74,16,128]{2,1,0:T(8,128)S(1)}, f32[74,16,128]{2,1,0:T(8,128)S(1)}, u32[]{:S(2)}, u32[]{:S(2)}) collective-permute-start(f32[74,16,128]{2,1,0:T(8,128)S(1)} %get-tuple-element.65), channel_id=1, source_target_pairs={{8,16},{16,8},{9,17},{17,9},{10,18},{18,10},{11,19},{19,11},{12,20... | collective-permute-start | bytes 1818632 | tf_op jit(solution)/shard_map/ppermute | solution.py:63
  8.1 1.3 %collective-permute-start = (f32[10,16,128]{2,1,0:T(8,128)S(1)}, f32[10,16,128]{2,1,0:T(8,128)S(1)}, u32[]{:S(2)}, u32[]{:S(2)}) collective-permute-start(f32[10,16,128]{2,1,0:T(8,128)S(1)} %get-tuple-element.61), channel_id=1, source_target_pairs={{0,1},{2,3},{1,0},{3,2},{4,5},{6,7},{5,4},{7,6},{8,9},{10,11},{9,8... | collective-permute-start | bytes 245768 | tf_op jit(solution)/shard_map/ppermute | solution.py:63
  8.2 1.3 %collective-permute-start.1 = (f32[10,16,128]{2,1,0:T(8,128)S(1)}, f32[10,16,128]{2,1,0:T(8,128)S(1)}, u32[]{:S(2)}, u32[]{:S(2)}) collective-permute-start(f32[10,16,128]{2,1,0:T(8,128)S(1)} %get-tuple-element.62), channel_id=1, source_target_pairs={{1,2},{2,1},{5,6},{6,5},{9,10},{10,9},{13,14},{14,13},{17,18},{18,... | collective-permute-start | bytes 245768 | tf_op jit(solution)/shard_map/ppermute | solution.py:63
  9.6 12.8 %collective-permute-start.2 = (f32[170,4,128]{2,1,0:T(4,128)S(1)}, f32[170,4,128]{2,1,0:T(4,128)S(1)}, u32[]{:S(2)}, u32[]{:S(2)}) collective-permute-start(f32[170,4,128]{2,1,0:T(4,128)S(1)} %get-tuple-element.63), channel_id=1, source_target_pairs={{0,4},{4,0},{1,5},{5,1},{2,6},{6,2},{3,7},{7,3},{8,12},{12,8},{9,1... | collective-permute-start | bytes 1044488 | tf_op jit(solution)/shard_map/ppermute | solution.py:63
  11.2 7.9 %collective-permute-start.5 = (f32[5,16,128]{2,1,0:T(8,128)S(1)}, f32[5,16,128]{2,1,0:T(8,128)S(1)}, u32[]{:S(2)}, u32[]{:S(2)}) collective-permute-start(f32[5,16,128]{2,1,0:T(8,128)S(1)} %get-tuple-element.66), channel_id=1, source_target_pairs={{0,8},{16,24},{8,0},{24,16},{1,9},{17,25},{9,1},{25,17},{2,10},{18... | collective-permute-start | bytes 122888 | tf_op jit(solution)/shard_map/ppermute | solution.py:63
  11.2 11.2 %collective-permute-start.6 = (f32[5,16,128]{2,1,0:T(8,128)S(1)}, f32[5,16,128]{2,1,0:T(8,128)S(1)}, u32[]{:S(2)}, u32[]{:S(2)}) collective-permute-start(f32[5,16,128]{2,1,0:T(8,128)S(1)} %get-tuple-element.67), channel_id=1, source_target_pairs={{8,16},{16,8},{9,17},{17,9},{10,18},{18,10},{11,19},{19,11},{12,20... | collective-permute-start | bytes 122888 | tf_op jit(solution)/shard_map/ppermute | solution.py:63
  22.7 8.9 %collective-permute-start.7 = (f32[158,4,128]{2,1,0:T(4,128)S(1)}, f32[158,4,128]{2,1,0:T(4,128)S(1)}, u32[]{:S(2)}, u32[]{:S(2)}) collective-permute-start(f32[158,4,128]{2,1,0:T(4,128)S(1)} %get-tuple-element.69), channel_id=1, source_target_pairs={{0,4},{4,0},{1,5},{5,1},{2,6},{6,2},{3,7},{7,3},{8,12},{12,8},{9,1... | collective-permute-start | bytes 970760 | tf_op jit(solution)/shard_map/ppermute | solution.py:63
